TPU v7x, 32 devices: a whole 2x2x4 slice. The times are simulated.
32 devices in a mesh: tok: 8 (over z, x), tp: 4 (over y, core).
Axes of the slice: x: 2, y: 2, z: 4, core: 2. Of those that a mesh axis runs over, the one named last changes fastest.
Arguments:
- resid: bfloat16 [1024, 8192], P('tok', 'tp'), may hold values from -7 to 7
- norm_gain: float32 [8192], P('tp'), may hold values from 0.5 to 1.5
- head_in: bfloat16 [8192, 2048], P('tp'), may hold values from -0.088388348 to 0.088388348
- head_bias: float32 [2048], replicated, may hold values from -3 to 3
- head_out: float32 [16, 128], replicated, may hold values from -0.26516504 to 0.26516504
- targets: float32 [1024, 16], P('tok'), may hold values from -12 to 12
- label_mask: int32 [1024, 16], P('tok'), may hold values 0 or 1
- obj_weight: int32 [16], replicated, may hold values from 1 to 16
Outputs:
- resid_grad: bfloat16 [1024, 8192], P('tok', 'tp')
- gain_grad: float32 [8192], P('tp')
- head_in_grad: float32 [8192, 2048], P('tp', 'tok')
- head_bias_grad: float32 [2048], replicated
All inputs are finite; a program needn't handle non-finite values. No bound on the sum of `label_mask` on one device may be relied on, other than what follows from the above.
Results may differ from a plain program's by a relative error of at most 0.0078.
Values may be sent and summed in bfloat16 or wider, within the bound.
No kernel may reach another device: no remote copies, remote signals or barrier semaphores. Data moves between devices by JAX's collectives and lax.ppermute only.
A program may use at most 128 MiB of HBM per device.

v0:
```python
import functools

import jax
import jax.numpy as jnp
from jax import lax
from jax.experimental import pallas as pl
from jax.experimental.pallas import tpu as pltpu
from jax.sharding import PartitionSpec as P


norm_eps = 1e-05
grad_eps = 1e-06
denominator = 8.0
LANES = 128
BF = jnp.bfloat16
F32 = jnp.float32
MIB = 1 << 20
BIG = 57


def exchange(value, axis, flip):
    count = lax.axis_size(axis)
    return lax.ppermute(value, axis, [(i, i ^ flip) for i in range(count)])


def params(mib):
    return pltpu.CompilerParams(vmem_limit_bytes=mib * MIB)


def cost(flops, nbytes):
    return pl.CostEstimate(flops=int(flops), bytes_accessed=int(nbytes), transcendentals=0)


def vmem():
    return pl.BlockSpec(memory_space=pltpu.VMEM)


def fetch_columns(source, target, sems):
    width = target.shape[1] // sems.shape[0]

    def copy(i):
        part = pl.ds(pl.multiple_of(i * width, width), width)
        return pltpu.make_async_copy(source.at[:, part], target.at[:, part], sems.at[i])

    for i in range(sems.shape[0]):
        copy(i).start()
    return copy, width


def fetch_rows(source, target, sems):
    depth = target.shape[0] // sems.shape[0]

    def copy(i):
        part = pl.ds(pl.multiple_of(i * depth, depth), depth)
        return pltpu.make_async_copy(source.at[part, :], target.at[part, :], sems.at[i])

    for i in range(sems.shape[0]):
        copy(i).start()
    return copy, depth


def smem():
    return pl.BlockSpec(memory_space=pltpu.SMEM)


def hbm():
    return pl.BlockSpec(memory_space=pl.ANY)


def forward_kernel(core_ref, resid_ref, gain_ref, weight_hbm, keep_ref, send_ref, weight_ref, scaled_ref, sems):
    halves, rows, total = keep_ref.shape
    columns = total - LANES
    core = core_ref[0]
    copy, width = fetch_columns(weight_hbm, weight_ref, sems)

    def put(value, cols):
        for quarter in range(2 * halves):
            piece = value[quarter * rows : (quarter + 1) * rows]
            half = quarter // 2

            @pl.when(core == quarter % 2)
            def _():
                keep_ref[half, :, cols] = piece

            @pl.when(core != quarter % 2)
            def _():
                send_ref[half, :, cols] = piece

    floated = resid_ref[...].astype(F32)
    scaled_ref[...] = (floated * gain_ref[...]).astype(BF)
    sums = jnp.sum(floated * floated, axis=1, keepdims=True)
    put(jnp.broadcast_to(sums, (sums.shape[0], LANES)), pl.ds(columns, LANES))

    @pl.loop(0, sems.shape[0])
    def _(i):
        copy(i).wait()
        cols = pl.ds(pl.multiple_of(i * width, width), width)
        put(jnp.dot(scaled_ref[...], weight_ref[:, cols], preferred_element_type=F32), cols)


def forward(core, resid, gain, weight):
    tokens, features = resid.shape
    columns = weight.shape[1]
    out = jax.ShapeDtypeStruct((2, tokens // 4, columns + LANES), F32)
    return pl.pallas_call(
        forward_kernel,
        out_shape=(out, out),
        in_specs=[smem(), vmem(), vmem(), hbm()],
        out_specs=(vmem(), vmem()),
        scratch_shapes=[
            pltpu.VMEM(weight.shape, BF),
            pltpu.VMEM((tokens, features), BF),
            pltpu.SemaphoreType.DMA((4,)),
        ],
        compiler_params=params(BIG),
        cost_estimate=cost(2 * tokens * features * columns, 2 * features * columns),
        name="forward",
    )(core, resid, gain, weight)


def merge_kernel(side_ref, keep_ref, recv_ref, mine_ref, send_ref):
    side = side_ref[0]
    mine_ref[...] = keep_ref[side] + recv_ref[side]
    other = keep_ref[1 - side] + recv_ref[1 - side]
    columns = other.shape[1] - LANES
    send_ref[:, :columns] = other[:, :columns].astype(BF)
    tail = other[:, columns:]
    lane = lax.broadcasted_iota(jnp.int32, tail.shape, 1)
    high = tail.astype(BF).astype(F32)
    rest = tail - high
    middle = rest.astype(BF).astype(F32)
    send_ref[:, columns:] = jnp.where(lane == 0, high, jnp.where(lane == 1, middle, rest - middle)).astype(BF)


def merge(side, keep, recv):
    shape = keep.shape[1:]
    return pl.pallas_call(
        merge_kernel,
        out_shape=(jax.ShapeDtypeStruct(shape, F32), jax.ShapeDtypeStruct(shape, BF)),
        in_specs=[pl.BlockSpec(memory_space=pltpu.SMEM), vmem(), vmem()],
        out_specs=(vmem(), vmem()),
        compiler_params=params(8),
        cost_estimate=cost(keep.size, 3 * keep.size),
        name="merge",
    )(side, keep, recv)


def heads_kernel(
    features, me_ref, mine_ref, recv_ref, bias_ref, out_ref, targets_ref, mask_ref, msg_ref, turned_ref
):
    rows = mine_ref.shape[0]
    columns = mine_ref.shape[1] - LANES
    objectives = targets_ref.shape[0]
    hidden = columns // objectives
    start = pl.multiple_of(me_ref[0] * rows, rows)
    turned_ref[0] = targets_ref[...].T
    turned_ref[1] = mask_ref[...].astype(F32).T
    target = turned_ref[0, pl.ds(start, rows), :]
    mask = turned_ref[1, pl.ds(start, rows), :]
    tail = recv_ref[:, columns:].astype(F32)
    sums = mine_ref[:, columns : columns + 1] + ((tail[:, 0:1] + tail[:, 1:2]) + tail[:, 2:3])
    inverse = lax.rsqrt(sums / features + norm_eps)
    lane = lax.broadcasted_iota(jnp.int32, (rows, LANES), 1)
    extra = jnp.zeros((rows, LANES), F32)
    for which in range(objectives):
        cols = slice(which * hidden, (which + 1) * hidden)
        product = (mine_ref[:, cols] + recv_ref[:, cols].astype(F32)) * inverse
        value = product + bias_ref[:, cols]
        squash = jax.nn.sigmoid(value)
        weight = out_ref[:, cols]
        score = jnp.sum(value * squash * weight, axis=1, keepdims=True)
        error = mask[:, which : which + 1] * (score - target[:, which : which + 1])
        grad = (error * weight * (squash * (1.0 + value * (1.0 - squash)))).astype(BF)
        msg_ref[:, cols] = grad
        along = jnp.sum(grad.astype(F32) * product, axis=1, keepdims=True)
        high = along.astype(BF).astype(F32)
        extra = jnp.where(lane == which, high, extra)
        extra = jnp.where(lane == objectives + which, along - high, extra)
    high = inverse.astype(BF).astype(F32)
    rest = inverse - high
    middle = rest.astype(BF).astype(F32)
    extra = jnp.where(lane == 2 * objectives, high, extra)
    extra = jnp.where(lane == 2 * objectives + 1, middle, extra)
    extra = jnp.where(lane == 2 * objectives + 2, rest - middle, extra)
    msg_ref[:, columns:] = extra.astype(BF)


def heads(features, me, mine, recv, bias, head_out, targets, mask):
    tokens = targets.shape[1]
    return pl.pallas_call(
        functools.partial(heads_kernel, features),
        out_shape=jax.ShapeDtypeStruct(mine.shape, BF),
        in_specs=[pl.BlockSpec(memory_space=pltpu.SMEM)] + [vmem()] * 6,
        out_specs=vmem(),
        scratch_shapes=[pltpu.VMEM((2, tokens, targets.shape[0]), F32)],
        compiler_params=params(8),
        cost_estimate=cost(30 * mine.size, 8 * mine.size),
        name="heads",
    )(me, mine, recv, bias, head_out, targets, mask)


def scales(extra, objectives):
    extra = extra.astype(F32)
    at = 2 * objectives
    inverse = (extra[:, at : at + 1] + extra[:, at + 1 : at + 2]) + extra[:, at + 2 : at + 3]
    along = extra[:, :objectives] + extra[:, objectives:at]
    return inverse, along


def gram_kernel(weight_hbm, gram_ref, weight_ref, sems):
    objectives, hidden, _ = gram_ref.shape
    copy, width = fetch_columns(weight_hbm, weight_ref, sems)
    for which in range(objectives):
        if which * hidden % width == 0:
            copy(which * hidden // width).wait()
        block = weight_ref[:, which * hidden : (which + 1) * hidden]
        gram_ref[which] = lax.dot_general(block, block, (((0,), (0,)), ((), ())), preferred_element_type=F32)


def gram_of(weight, objectives, hidden):
    features, columns = weight.shape
    return pl.pallas_call(
        gram_kernel,
        out_shape=jax.ShapeDtypeStruct((objectives, hidden, hidden), F32),
        in_specs=[hbm()],
        out_specs=vmem(),
        scratch_shapes=[pltpu.VMEM(weight.shape, BF), pltpu.SemaphoreType.DMA((4,))],
        compiler_params=params(BIG),
        cost_estimate=cost(2 * features * columns * hidden, 2 * features * columns),
        name="gram",
    )(weight)


def spread_kernel(spot_ref, part0_ref, part1_ref, part2_ref, part3_ref, gram_ref, grad_ref, msg_ref, sums_ref):
    objectives, hidden, _ = gram_ref.shape
    peers, rows, width = msg_ref.shape
    tokens = grad_ref.shape[0]
    columns = objectives * hidden
    share = tokens // 4
    for flip, part_ref in enumerate((part0_ref, part1_ref, part2_ref, part3_ref)):
        start = pl.multiple_of((spot_ref[0] ^ flip) * share, share)
        grad_ref[pl.ds(start, share), :] = part_ref[...]
    inverse, _ = scales(grad_ref[:, columns:], objectives)
    lane = lax.broadcasted_iota(jnp.int32, (1, width), 1)
    squares = jnp.zeros((1, width), F32)
    for which in range(objectives):
        block = grad_ref[:, which * hidden : (which + 1) * hidden]
        pair = lax.dot_general(block, block, (((0,), (0,)), ((), ())), preferred_element_type=F32)
        total = jnp.sum(jnp.sum(pair * gram_ref[which], axis=0, keepdims=True), axis=1, keepdims=True)
        squares = jnp.where(lane == which, total, squares)
    for peer in range(peers):
        piece = grad_ref[:, peer * width : (peer + 1) * width].astype(F32)
        sums_ref[:, peer * width : (peer + 1) * width] = jnp.sum(piece, axis=0, keepdims=True)
        msg_ref[peer, :tokens, :] = (piece * inverse).astype(BF)
    high = squares.astype(BF).astype(F32)
    rest = squares - high
    middle = rest.astype(BF).astype(F32)
    row = lax.broadcasted_iota(jnp.int32, (rows - tokens, width), 0)
    tail = jnp.where(row == 0, high, jnp.where(row == 1, middle, jnp.where(row == 2, rest - middle, 0.0)))
    for peer in range(peers):
        msg_ref[peer, tokens:, :] = tail.astype(BF)


def spread(me, parts, gram, peers):
    share, total = parts[0].shape
    tokens = 4 * share
    columns = gram.shape[0] * gram.shape[1]
    return pl.pallas_call(
        spread_kernel,
        out_shape=(
            jax.ShapeDtypeStruct((tokens, total), BF),
            jax.ShapeDtypeStruct((peers, tokens + 16, columns // peers), BF),
            jax.ShapeDtypeStruct((1, columns), F32),
        ),
        in_specs=[pl.BlockSpec(memory_space=pltpu.SMEM)] + [vmem()] * 5,
        out_specs=(vmem(), vmem(), vmem()),
        compiler_params=params(16),
        cost_estimate=cost(2 * tokens * columns * gram.shape[1], 8 * tokens * total),
        name="spread",
    )(me, *parts, gram)


def products_kernel(resid_ref, weight_hbm, grad_ref, along_ref, weight_ref, scal_ref, sems):
    objectives = along_ref.shape[0]
    columns = weight_hbm.shape[1]
    hidden = columns // objectives
    copy, depth = fetch_rows(weight_hbm, weight_ref, sems)
    inverse, _ = scales(grad_ref[:, columns:], objectives)
    scal_ref[...] = jnp.broadcast_to(inverse, scal_ref.shape)

    @pl.loop(0, sems.shape[0])
    def _(i):
        copy(i).wait()
        rows = pl.ds(pl.multiple_of(i * depth, depth), depth)
        unit = resid_ref[:, rows].astype(F32) * scal_ref[:, 0:1]
        for which in range(objectives):
            cols = slice(which * hidden, (which + 1) * hidden)
            value = lax.dot_general(
                grad_ref[:, cols], weight_ref[rows, cols], (((1,), (1,)), ((), ())), preferred_element_type=F32
            )
            along_ref[which : which + 1, rows] = jnp.sum(value * unit, axis=0, keepdims=True)


def products(resid, weight, grad, objectives):
    tokens, features = resid.shape
    return pl.pallas_call(
        products_kernel,
        out_shape=jax.ShapeDtypeStruct((objectives, features), F32),
        in_specs=[vmem(), hbm(), vmem()],
        out_specs=vmem(),
        scratch_shapes=[
            pltpu.VMEM(weight.shape, BF),
            pltpu.VMEM((tokens, LANES), F32),
            pltpu.SemaphoreType.DMA((4,)),
        ],
        compiler_params=params(BIG),
        cost_estimate=cost(2 * weight.size * tokens, 2 * weight.size),
        name="products",
    )(resid, weight, grad)


def backward_kernel(
    total, bal_ref, share_ref, resid_ref, gain_ref, weight_hbm, grad_ref, out_ref, weight_ref, pre_ref, scal_ref, sems
):
    columns = weight_hbm.shape[1]
    copy, depth = fetch_rows(weight_hbm, weight_ref, sems)
    pre_ref[...] = (grad_ref[:, :columns].astype(F32) * bal_ref[...]).astype(BF)
    inverse, along = scales(grad_ref[:, columns:], share_ref.shape[1])
    scal_ref[0] = jnp.broadcast_to(inverse, scal_ref.shape[1:])
    projection = jnp.sum(along * share_ref[...], axis=1, keepdims=True) / total
    scal_ref[1] = jnp.broadcast_to(projection, scal_ref.shape[1:])

    @pl.loop(0, sems.shape[0])
    def _(i):
        copy(i).wait()
        rows = pl.ds(pl.multiple_of(i * depth, depth), depth)
        grad = lax.dot_general(
            pre_ref[...], weight_ref[rows, :], (((1,), (1,)), ((), ())), preferred_element_type=F32
        )
        inverse = scal_ref[0, :, 0:1]
        unit = resid_ref[:, rows].astype(F32) * inverse
        out_ref[:, rows] = (inverse * (gain_ref[:, rows] * grad - unit * scal_ref[1, :, 0:1])).astype(BF)


def backward(total, resid, gain, weight, grad, bal_cols, balance):
    tokens, _ = resid.shape
    return pl.pallas_call(
        functools.partial(backward_kernel, total),
        out_shape=jax.ShapeDtypeStruct(resid.shape, BF),
        in_specs=[vmem(), vmem(), vmem(), vmem(), hbm(), vmem()],
        out_specs=vmem(),
        scratch_shapes=[
            pltpu.VMEM(weight.shape, BF),
            pltpu.VMEM((tokens, weight.shape[1]), BF),
            pltpu.VMEM((2, tokens, LANES), F32),
            pltpu.SemaphoreType.DMA((4,)),
        ],
        compiler_params=params(BIG),
        cost_estimate=cost(2 * weight.size * tokens, 2 * weight.size),
        name="backward",
    )(bal_cols, balance, resid, gain, weight, grad)


def weight_kernel(plan, depth, order_ref, gain_ref, scale_ref, grad_ref, *rest):
    count = len(plan)
    block_refs = rest[:-6]
    out_hbm, turned_ref, blocks_ref, result_ref, sems, out_sems = rest[-6:]
    tokens, features = block_refs[0].shape
    steps = features // depth
    inner = order_ref[count]

    def load(k, source):
        place = pl.ds(k * tokens, tokens)
        return pltpu.make_async_copy(block_refs[source], blocks_ref.at[place, :], sems.at[k])

    for k, choice in enumerate(plan):
        if len(choice) == 1:
            load(k, choice[0]).start()
        else:

            @pl.when(inner == 1)
            def _():
                load(k, choice[0]).start()

            @pl.when(inner == 0)
            def _():
                load(k, choice[1]).start()

    for k in range(count):
        turned_ref[:, k * tokens : (k + 1) * tokens] = grad_ref[order_ref[k], :tokens, :].T
    for k, choice in enumerate(plan):
        load(k, choice[0]).wait()

    def store(i):
        rows = pl.ds(pl.multiple_of(i * depth, depth), depth)
        return pltpu.make_async_copy(result_ref.at[rows, :], out_hbm.at[rows, :], out_sems.at[i])

    @pl.loop(0, steps)
    def _(i):
        part = pl.ds(pl.multiple_of(i * depth, depth), depth)
        value = jnp.dot(turned_ref[...], blocks_ref[:, part], preferred_element_type=F32)
        result_ref[part, :] = (value * gain_ref[:, part]).T * scale_ref[...]
        store(i).start()

    @pl.loop(0, steps)
    def _(i):
        store(i).wait()


def weight_grad(order, gain, col_scale, grads, blocks, plan):
    tokens, features = blocks[0].shape
    columns = grads.shape[2]
    depth = 512
    count = len(plan)
    return pl.pallas_call(
        functools.partial(weight_kernel, plan, depth),
        out_shape=jax.ShapeDtypeStruct((features, columns), F32),
        in_specs=[smem(), vmem(), vmem(), vmem()] + [hbm()] * len(blocks),
        out_specs=hbm(),
        scratch_shapes=[
            pltpu.VMEM((columns, tokens * count), BF),
            pltpu.VMEM((tokens * count, features), BF),
            pltpu.VMEM((features, columns), F32),
            pltpu.SemaphoreType.DMA((count,)),
            pltpu.SemaphoreType.DMA((features // depth,)),
        ],
        compiler_params=params(BIG),
        cost_estimate=cost(2 * tokens * count * features * columns, 8 * features * columns),
        name="weights",
    )(order, gain, col_scale, grads, *blocks)


def gather_blocks(resid):
    count = lax.axis_size("tok")
    place = lax.axis_index("tok")
    if count == 8:
        line, side = place // 2, place % 2

        def pairs(moves):
            return [(2 * a + s, 2 * b + s) for a, b in moves for s in range(2)]

        def cross(lines):
            return [(2 * a + s, 2 * a + 1 - s) for a in lines for s in range(2)]

        swap, out = pairs([(1, 2), (2, 1)]), pairs([(1, 0), (2, 3)])
        x0 = lax.ppermute(resid, "tok", cross(range(4)))
        z1 = lax.ppermute(resid, "tok", pairs([(0, 1), (1, 0), (2, 3), (3, 2)]))
        m1 = lax.ppermute(resid, "tok", swap)
        m2 = lax.ppermute(z1, "tok", swap)
        x1 = lax.ppermute(z1, "tok", cross(range(4)))
        f1 = lax.ppermute(m1, "tok", out)
        f2 = lax.ppermute(m2, "tok", out)
        x2m = lax.ppermute(m1, "tok", cross((1, 2)))
        x2e = lax.ppermute(f1, "tok", cross((0, 3)))
        x3m = lax.ppermute(m2, "tok", cross((1, 2)))
        x3e = lax.ppermute(f2, "tok", cross((0, 3)))
        low = line < 2
        inner = (line == 1) | (line == 2)
        lines = [line, line ^ 1, jnp.where(low, 2, 1), jnp.where(low, 3, 0)]
        order = [2 * a + (side ^ s) for a in lines for s in range(2)] + [inner.astype(jnp.int32)]
        blocks = [resid, x0, z1, x1, m1, f1, x2m, x2e, m2, f2, x3m, x3e]
        plan = ((0,), (1,), (2,), (3,), (4, 5), (6, 7), (8, 9), (10, 11))
        return blocks, jnp.stack(order), plan
    found = {0: resid}
    for flip in range(2, count, 2):
        found[flip] = exchange(resid, "tok", flip)
    for flip in range(0, count, 2):
        found[flip + 1] = exchange(found[flip], "tok", 1)
    order = jnp.append(place ^ jnp.arange(count), 0)
    return [found[flip] for flip in range(count)], order, tuple((flip,) for flip in range(count))


def total_over_tok(value):
    count = lax.axis_size("tok")
    flips = [1 << bit for bit in range(1, count.bit_length() - 1)] + [1] * (count > 1)
    for flip in flips:
        got = lax.ppermute(value, "tok", [(i, i ^ flip) for i in range(count)])
        value = value + got
    return value


def fast_device(resid, norm_gain, head_in, head_bias, head_out, targets, label_mask, obj_weight):
    tokens, features = resid.shape
    objectives, hidden = head_out.shape
    columns = objectives * hidden
    peers = lax.axis_size("tok")
    total_features = features * lax.axis_size("tp")
    total_tokens = tokens * peers
    me = lax.axis_index("tp")
    place = lax.axis_index("tok")
    gain = norm_gain[None, :]
    partner = [(i, i ^ 1) for i in range(4)]
    across = [(i, i ^ 2) for i in range(4)]

    blocks, order, plan = gather_blocks(resid)
    keep, send = forward((me % 2)[None], resid, gain, head_in)
    recv = lax.ppermute(send, "tp", partner)
    mine, send = merge((me // 2)[None], keep, recv)
    recv = lax.ppermute(send, "tp", across)
    gram = gram_of(head_in, objectives, hidden)
    part = heads(
        total_features,
        me[None],
        mine,
        recv,
        head_bias[None, :],
        head_out.reshape(1, columns),
        targets.T,
        label_mask.T,
    )
    part1 = lax.ppermute(part, "tp", partner)
    part2 = lax.ppermute(part, "tp", across)
    part3 = lax.ppermute(part2, "tp", partner)
    grad, message, col_sums = spread(me[None], (part, part1, part2, part3), gram, peers)
    grads = lax.all_to_all(message, "tok", 0, 0)
    along = products(resid, head_in, grad, objectives)
    squares = jnp.sum(grads[:, tokens : tokens + 3, :objectives].astype(F32), axis=(0, 1))
    squares = lax.psum(squares, "tp")
    obj_rms = jnp.sqrt(squares / (total_tokens * total_features) + grad_eps)
    balance = obj_weight.astype(F32) / denominator / obj_rms
    bal_cols = jnp.repeat(balance, hidden)
    gain_part = jnp.sum(balance[:, None] * along, axis=0, keepdims=True)
    sums = jnp.concatenate([gain_part, col_sums], axis=0)
    sums = total_over_tok(sums)
    resid_grad = backward(total_features, resid, gain, head_in, grad, bal_cols[None, :], balance[None, :])
    gain_grad = sums[0] / total_tokens
    head_bias_grad = sums[1] * bal_cols / total_tokens
    width = columns // peers
    col_scale = lax.dynamic_slice_in_dim(bal_cols, place * width, width, 0) / total_tokens
    head_in_grad = weight_grad(order, gain, col_scale[None, :], grads, blocks, plan)
    return (resid_grad, gain_grad, head_in_grad, head_bias_grad)


def head_gradient(preact, head_out, targets, label_mask):
    count = preact.shape[0]
    objectives, hidden = head_out.shape
    cube = preact.reshape(count, objectives, hidden)
    squash = jax.nn.sigmoid(cube)
    scores = jnp.sum(cube * squash * head_out[None], axis=2)
    errors = label_mask.astype(jnp.float32) * (scores - targets)
    slopes = squash * (1.0 + cube * (1.0 - squash))
    row_grad = (errors[:, :, None] * head_out[None] * slopes).astype(jnp.bfloat16)
    return row_grad.reshape(count, objectives * hidden)


def general_device(resid, norm_gain, head_in, head_bias, head_out, targets, label_mask, obj_weight):
    tok_rows = resid.shape[0]
    total_features = resid.shape[1] * lax.axis_size("tp")
    objectives, hidden = head_out.shape
    total_tokens = tok_rows * lax.axis_size("tok")
    floated = resid.astype(jnp.float32)
    row_sums = lax.psum(jnp.sum(floated * floated, axis=1), "tp")
    inverse = lax.rsqrt(row_sums[:, None] / total_features + norm_eps)
    unit = floated * inverse
    normed = (unit * norm_gain[None, :]).astype(jnp.bfloat16)
    partial_value = jnp.dot(normed, head_in, preferred_element_type=jnp.float32)
    quarter = lax.psum_scatter(partial_value, "tp", scatter_dimension=0, tiled=True)
    share = quarter.shape[0]
    offset = lax.axis_index("tp") * share
    part_targets = lax.dynamic_slice_in_dim(targets, offset, share, 0)
    part_mask = lax.dynamic_slice_in_dim(label_mask, offset, share, 0)
    part_grad = head_gradient(quarter + head_bias[None, :], head_out, part_targets, part_mask)
    row_grad = lax.all_gather(part_grad, "tp", axis=0, tiled=True)
    grad_float = row_grad.astype(jnp.float32)

    def objective_square(which):
        grad_slice = lax.dynamic_slice_in_dim(row_grad, which * hidden, hidden, 1)
        weight_slice = lax.dynamic_slice_in_dim(head_in, which * hidden, hidden, 1)
        feature_grad = lax.dot_general(
            grad_slice, weight_slice, (((1,), (1,)), ((), ())), preferred_element_type=jnp.float32
        )
        return jnp.sum(feature_grad * feature_grad)

    local_squares = lax.map(objective_square, jnp.arange(objectives))
    squares = lax.psum(local_squares, ("tok", "tp"))
    obj_rms = jnp.sqrt(squares / (total_tokens * total_features) + grad_eps)
    balance = obj_weight.astype(jnp.float32) / denominator / obj_rms
    balance_cols = jnp.repeat(balance, hidden)
    pre_grad = (grad_float * balance_cols[None, :]).astype(jnp.bfloat16)
    norm_grad = lax.dot_general(
        pre_grad, head_in, (((1,), (1,)), ((), ())), preferred_element_type=jnp.float32
    )
    gain_sum, bias_sum = lax.psum(
        (jnp.sum(norm_grad * unit, axis=0), jnp.sum(grad_float, axis=0)), "tok"
    )
    gain_grad = gain_sum / total_tokens
    head_bias_grad = bias_sum * balance_cols / total_tokens
    projection = lax.psum(jnp.sum(unit * norm_gain[None, :] * norm_grad, axis=1), "tp")
    resid_grad = (
        inverse * (norm_gain[None, :] * norm_grad - unit * (projection[:, None] / total_features))
    ).astype(jnp.bfloat16)
    weight_term = lax.dot_general(
        normed, row_grad, (((0,), (0,)), ((), ())), preferred_element_type=jnp.float32
    )
    summed_block = lax.psum_scatter(weight_term, "tok", scatter_dimension=1, tiled=True)
    columns = summed_block.shape[1]
    col_scale = lax.dynamic_slice_in_dim(balance_cols, lax.axis_index("tok") * columns, columns, 0)
    head_in_grad = summed_block * col_scale[None, :] / total_tokens
    return (resid_grad, gain_grad, head_in_grad, head_bias_grad)


def fits_fast(mesh, resid, head_in, head_out):
    peers, shards = mesh.shape["tok"], mesh.shape["tp"]
    columns = head_in.shape[1]
    tokens, features = resid.shape[0] // peers, resid.shape[1] // shards
    width = columns // peers
    fits = shards == 4 and peers & (peers - 1) == 0 and columns % peers == 0
    fits = fits and width % LANES == 0 and head_out.shape[1] == LANES and head_out.shape[0] <= 32
    return fits and tokens % 128 == 0 and features % 512 == 0 and columns % 1024 == 0


def solution(mesh):
    def mapped(body):
        return jax.shard_map(
            body,
            mesh=mesh,
            in_specs=(
                P("tok", "tp"),
                P("tp"),
                P("tp", None),
                P(),
                P(),
                P("tok", None),
                P("tok", None),
                P(),
            ),
            out_specs=(P("tok", "tp"), P("tp"), P("tp", "tok"), P()),
            check_vma=False,
        )


    def step(*args):
        if fits_fast(mesh, args[0], args[2], args[4]):
            return mapped(fast_device)(*args)
        return mapped(general_device)(*args)

    return step
```

profile of v0, /device:TPU:0, one launch (start us, length us, event | category | flops | bytes accessed | tf_op | source)
XLA Modules:
  0.0 139.7 jit_solution(2241471372014600472)
XLA Ops:
  0.7 6.1 %forward.1 = (f32[2,32,2176]{2,1,0:T(8,128)}, f32[2,32,2176]{2,1,0:T(8,128)}) custom-call(s32[1]{0:T(128)} %bitcast.2.core_ref, bf16[128,2048]{1,0:T(8,128)(2,1)} %rest_0_.1, f32[1,2048]{1,0:T(1,128)} %bitcast.33, bf16[2048,2048]{1,0:T(8,128)(2,1)} %weight_hbm.7), custom_call_target="tpu_custom_call" | custom-call | flops 1073741824 | bytes 8388608 | tf_op jit(solution)/shard_map/forward/pallas_call | solution.py:105
  7.4 1.8 %collective-permute-done.recv_ref = f32[2,32,2176]{2,1,0:T(8,128)S(1)} collective-permute-done((f32[2,32,2176]{2,1,0:T(8,128)}, f32[2,32,2176]{2,1,0:T(8,128)S(1)}, u32[]{:S(2)}, u32[]{:S(2)}) %collective-permute-start) | collective-permute-done | bytes 557088 | tf_op jit(solution)/shard_map/ppermute | solution.py:497
  10.3 2.9 %collective-permute-start.1 = (bf16[32,2176]{1,0:T(8,128)(2,1)S(1)}, bf16[32,2176]{1,0:T(8,128)(2,1)S(1)}, u32[]{:S(2)}, u32[]{:S(2)}) collective-permute-start(bf16[32,2176]{1,0:T(8,128)(2,1)S(1)} %get-tuple-element.14), channel_id=1, source_target_pairs={{0,2},{1,3},{2,0},{3,1},{4,6},{5,7},{6,4},{7,5},{8,10},{9,11},{10,... | collective-permute-start | bytes 417800 | tf_op jit(solution)/shard_map/ppermute | solution.py:499
  13.2 4.0 %collective-permute-done.1.recv_ref = bf16[32,2176]{1,0:T(8,128)(2,1)S(1)} collective-permute-done((bf16[32,2176]{1,0:T(8,128)(2,1)S(1)}, bf16[32,2176]{1,0:T(8,128)(2,1)S(1)}, u32[]{:S(2)}, u32[]{:S(2)}) %collective-permute-start.1) | collective-permute-done | bytes 139296 | tf_op jit(solution)/shard_map/ppermute | solution.py:499
  17.2 2.0 %heads.1.part0_ref = bf16[32,2176]{1,0:T(8,128)(2,1)S(1)} custom-call(s32[1]{0:T(128)} %bitcast.me_ref.spot_ref, f32[32,2176]{1,0:T(8,128)S(1)} %get-tuple-element.13.mine_ref, bf16[32,2176]{1,0:T(8,128)(2,1)S(1)} %collective-permute-done.1.recv_ref, f32[1,2048]{1,0:T(1,128)S(1)} %bitcast.26, f32[1,2048]{1,0:T(1,128)S(1)} %bitcast.27, ...), custom_call_target="tpu_custom_call" | custom-call | flops 2088960 | bytes 557056 | tf_op jit(solution)/shard_map/heads/pallas_call | solution.py:190
  19.2 1.8 %collective-permute-start.3 = (bf16[32,2176]{1,0:T(8,128)(2,1)S(1)}, bf16[32,2176]{1,0:T(8,128)(2,1)S(1)}, u32[]{:S(2)}, u32[]{:S(2)}) collective-permute-start(bf16[32,2176]{1,0:T(8,128)(2,1)S(1)} %heads.1.part0_ref), channel_id=1, source_target_pairs={{0,2},{1,3},{2,0},{3,1},{4,6},{5,7},{6,4},{7,5},{8,10},{9,11},{10,... | collective-permute-start | bytes 417800 | tf_op jit(solution)/shard_map/ppermute | solution.py:512
  21.0 3.4 %collective-permute-done.3.part2_ref = bf16[32,2176]{1,0:T(8,128)(2,1)S(1)} collective-permute-done((bf16[32,2176]{1,0:T(8,128)(2,1)S(1)}, bf16[32,2176]{1,0:T(8,128)(2,1)S(1)}, u32[]{:S(2)}, u32[]{:S(2)}) %collective-permute-start.3) | collective-permute-done | bytes 139296 | tf_op jit(solution)/shard_map/ppermute | solution.py:512
  24.4 1.7 %collective-permute-start.9 = (bf16[128,2048]{1,0:T(8,128)(2,1)S(1)}, bf16[128,2048]{1,0:T(8,128)(2,1)S(1)}, u32[]{:S(2)}, u32[]{:S(2)}) collective-permute-start(bf16[128,2048]{1,0:T(8,128)(2,1)S(1)} %copy-done.7), channel_id=1, source_target_pairs={{0,8},{4,12},{8,0},{12,4},{16,24},{20,28},{24,16},{28,20},{1,9},{5... | collective-permute-start | bytes 1572872 | tf_op jit(solution)/shard_map/ppermute | solution.py:447
  26.2 5.8 %gram.1.gram_ref = f32[16,128,128]{2,1,0:T(8,128)} custom-call(bf16[2048,2048]{1,0:T(8,128)(2,1)} %weight_hbm.7), custom_call_target="tpu_custom_call" | custom-call | flops 1073741824 | bytes 8388608 | tf_op jit(solution)/shard_map/gram/pallas_call | solution.py:222
  35.4 4.8 %all-to-all-start = ((bf16[8,144,256]{2,1,0:T(8,128)(2,1)}), bf16[8,144,256]{2,1,0:T(8,128)(2,1)S(1)}, u32[]{:S(2)}, u32[]{:S(2)}) async-start(bf16[8,144,256]{2,1,0:T(8,128)(2,1)} %get-tuple-element.15), calls=%async_computation | async-start | bytes 1179648 | tf_op jit(solution)/shard_map/all_to_all | solution.py:515
  41.6 2.1 %collective-permute-start.8 = (bf16[128,2048]{1,0:T(8,128)(2,1)S(1)}, bf16[128,2048]{1,0:T(8,128)(2,1)S(1)}, u32[]{:S(2)}, u32[]{:S(2)}) collective-permute-start(bf16[128,2048]{1,0:T(8,128)(2,1)S(1)} %copy-done.7), channel_id=1, source_target_pairs={{0,4},{4,0},{8,12},{12,8},{16,20},{20,16},{24,28},{28,24},{1,5},{5... | collective-permute-start | bytes 1572872 | tf_op jit(solution)/shard_map/ppermute | solution.py:446
  45.7 6.5 %products.1 = f32[16,2048]{1,0:T(8,128)} custom-call(bf16[128,2048]{1,0:T(8,128)(2,1)} %rest_0_.1, bf16[2048,2048]{1,0:T(8,128)(2,1)} %weight_hbm.7, bf16[128,2176]{1,0:T(8,128)(2,1)} %copy-done.1), custom_call_target="tpu_custom_call" | custom-call | flops 1073741824 | bytes 8388608 | tf_op jit(solution)/shard_map/products/pallas_call | solution.py:306
  53.5 3.9 %all-to-all-done.grad_ref = bf16[8,144,256]{2,1,0:T(8,128)(2,1)S(1)} async-done(((bf16[8,144,256]{2,1,0:T(8,128)(2,1)}), bf16[8,144,256]{2,1,0:T(8,128)(2,1)S(1)}, u32[]{:S(2)}, u32[]{:S(2)}) %all-to-all-start) | async-done | bytes 589856 | tf_op jit(solution)/shard_map/all_to_all | solution.py:515
  57.5 6.0 %psum.7 = f32[16]{0:T(128)S(1)} all-reduce(f32[16]{0:T(128)S(1)} %convert_reduce_fusion), channel_id=1, replica_groups=mesh['tok'=8,'tp'=4] {'tp'}, use_global_device_ids=true, to_apply=%region_1.2 | all-reduce | flops 16 | bytes 128 | tf_op jit(solution)/shard_map/psum | solution.py:518
  64.5 24.0 %collective-permute-start.5 = (f32[2,2048]{1,0:T(2,128)S(1)}, f32[2,2048]{1,0:T(2,128)S(1)}, u32[]{:S(2)}, u32[]{:S(2)}) collective-permute-start(f32[2,2048]{1,0:T(2,128)S(1)} %pad_maximum_fusion), channel_id=1, source_target_pairs={{0,8},{4,12},{8,0},{12,4},{16,24},{20,28},{24,16},{28,20},{1,9},{5... | collective-permute-start | bytes 49160 | tf_op jit(solution)/shard_map/ppermute | solution.py:477
  88.6 3.7 %collective-permute-done.5 = f32[2,2048]{1,0:T(2,128)S(1)} collective-permute-done((f32[2,2048]{1,0:T(2,128)S(1)}, f32[2,2048]{1,0:T(2,128)S(1)}, u32[]{:S(2)}, u32[]{:S(2)}) %collective-permute-start.5) | collective-permute-done | bytes 16416 | tf_op jit(solution)/shard_map/ppermute | solution.py:477
  93.8 3.3 %collective-permute-done.6 = f32[2,2048]{1,0:T(2,128)S(1)} collective-permute-done((f32[2,2048]{1,0:T(2,128)S(1)}, f32[2,2048]{1,0:T(2,128)S(1)}, u32[]{:S(2)}, u32[]{:S(2)}) %collective-permute-start.6) | collective-permute-done | bytes 16416 | tf_op jit(solution)/shard_map/ppermute | solution.py:477
  97.1 1.6 %collective-permute-start.7 = (f32[2,2048]{1,0:T(2,128)S(1)}, f32[2,2048]{1,0:T(2,128)S(1)}, u32[]{:S(2)}, u32[]{:S(2)}) collective-permute-start(f32[2,2048]{1,0:T(2,128)S(1)} %fusion.2), channel_id=1, source_target_pairs={{0,4},{4,0},{8,12},{12,8},{16,20},{20,16},{24,28},{28,24},{1,5},{5... | collective-permute-start | bytes 49160 | tf_op jit(solution)/shard_map/ppermute | solution.py:477
  99.4 7.0 %backward.1 = bf16[128,2048]{1,0:T(8,128)(2,1)} custom-call(f32[1,2048]{1,0:T(1,128)} %bitcast.36, f32[1,16]{1,0:T(1,128)} %bitcast.38, bf16[128,2048]{1,0:T(8,128)(2,1)} %rest_0_.1, f32[1,2048]{1,0:T(1,128)} %bitcast.34, bf16[2048,2048]{1,0:T(8,128)(2,1)} %weight_hbm.7, bf16[128,2176]{1,0:T(8,128)(2,1)} %copy-done.1), custom_call_target="tpu_custom_call" | custom-call | flops 1073741824 | bytes 8388608 | tf_op jit(solution)/shard_map/backward/pallas_call | solution.py:347
  107.9 2.4 %collective-permute-start.14 = (bf16[128,2048]{1,0:T(8,128)(2,1)}, bf16[128,2048]{1,0:T(8,128)(2,1)S(1)}, u32[]{:S(2)}, u32[]{:S(2)}) collective-permute-start(bf16[128,2048]{1,0:T(8,128)(2,1)} %collective-permute-done.12.rest_5_), channel_id=1, source_target_pairs={{0,4},{4,0},{24,28},{28,24},{1,5},{5,1},{25,29},{29,25},{2,6},{6,2... | collective-permute-start | bytes 1572872 | tf_op jit(solution)/shard_map/ppermute | solution.py:454
  110.3 3.4 %collective-permute-start.18 = (bf16[128,2048]{1,0:T(8,128)(2,1)}, bf16[128,2048]{1,0:T(8,128)(2,1)S(1)}, u32[]{:S(2)}, u32[]{:S(2)}) collective-permute-start(bf16[128,2048]{1,0:T(8,128)(2,1)} %collective-permute-done.16.rest_9_), channel_id=1, source_target_pairs={{0,4},{4,0},{24,28},{28,24},{1,5},{5,1},{25,29},{29,25},{2,6},{6,2... | collective-permute-start | bytes 1572872 | tf_op jit(solution)/shard_map/ppermute | solution.py:456
  115.7 9.1 %collective-permute-done.14.rest_7_ = bf16[128,2048]{1,0:T(8,128)(2,1)S(1)} collective-permute-done((bf16[128,2048]{1,0:T(8,128)(2,1)}, bf16[128,2048]{1,0:T(8,128)(2,1)S(1)}, u32[]{:S(2)}, u32[]{:S(2)}) %collective-permute-start.14) | collective-permute-done | bytes 524320 | tf_op jit(solution)/shard_map/ppermute | solution.py:454
  124.8 7.6 %collective-permute-done.18.rest_11_ = bf16[128,2048]{1,0:T(8,128)(2,1)S(1)} collective-permute-done((bf16[128,2048]{1,0:T(8,128)(2,1)}, bf16[128,2048]{1,0:T(8,128)(2,1)S(1)}, u32[]{:S(2)}, u32[]{:S(2)}) %collective-permute-start.18) | collective-permute-done | bytes 524320 | tf_op jit(solution)/shard_map/ppermute | solution.py:456
  133.2 6.5 %weights.1 = f32[2048,256]{1,0:T(8,128)} custom-call(s32[9]{0:T(128)} %stack.43.order_ref, f32[1,2048]{1,0:T(1,128)} %bitcast.35, f32[1,256]{1,0:T(1,128)} %bitcast.40, bf16[8,144,256]{2,1,0:T(8,128)(2,1)} %copy-done.8, bf16[128,2048]{1,0:T(8,128)(2,1)} %rest_0_.1, bf16[128,2048]{1,0:T(8,128)(2,1)} %copy-done.12, bf16[128,2048]{1,0:T(8,128)(2,1)} %copy-done.9, ...), custom_call_target="tpu_custom_call" | custom-call | flops 1073741824 | bytes 4194304 | tf_op jit(solution)/shard_map/weights/pallas_call | solution.py:415
  (76 shorter events, 17.2 us)
Async XLA Ops:
  6.8 2.4 %collective-permute-start = (f32[2,32,2176]{2,1,0:T(8,128)}, f32[2,32,2176]{2,1,0:T(8,128)S(1)}, u32[]{:S(2)}, u32[]{:S(2)}) collective-permute-start(f32[2,32,2176]{2,1,0:T(8,128)} %get-tuple-element.12), channel_id=1, source_target_pairs={{0,1},{1,0},{2,3},{3,2},{4,5},{5,4},{6,7},{7,6},{8,9},{9,8},{10,11... | collective-permute-start | bytes 1671176 | tf_op jit(solution)/shard_map/ppermute | solution.py:497
  10.3 6.9 %collective-permute-start.1 = (bf16[32,2176]{1,0:T(8,128)(2,1)S(1)}, bf16[32,2176]{1,0:T(8,128)(2,1)S(1)}, u32[]{:S(2)}, u32[]{:S(2)}) collective-permute-start(bf16[32,2176]{1,0:T(8,128)(2,1)S(1)} %get-tuple-element.14), channel_id=1, source_target_pairs={{0,2},{1,3},{2,0},{3,1},{4,6},{5,7},{6,4},{7,5},{8,10},{9,11},{10,... | collective-permute-start | bytes 417800 | tf_op jit(solution)/shard_map/ppermute | solution.py:499
  19.2 5.2 %collective-permute-start.3 = (bf16[32,2176]{1,0:T(8,128)(2,1)S(1)}, bf16[32,2176]{1,0:T(8,128)(2,1)S(1)}, u32[]{:S(2)}, u32[]{:S(2)}) collective-permute-start(bf16[32,2176]{1,0:T(8,128)(2,1)S(1)} %heads.1.part0_ref), channel_id=1, source_target_pairs={{0,2},{1,3},{2,0},{3,1},{4,6},{5,7},{6,4},{7,5},{8,10},{9,11},{10,... | collective-permute-start | bytes 417800 | tf_op jit(solution)/shard_map/ppermute | solution.py:512
  21.0 10.9 %collective-permute-start.2 = (bf16[32,2176]{1,0:T(8,128)(2,1)S(1)}, bf16[32,2176]{1,0:T(8,128)(2,1)S(1)}, u32[]{:S(2)}, u32[]{:S(2)}) collective-permute-start(bf16[32,2176]{1,0:T(8,128)(2,1)S(1)} %heads.1.part0_ref), channel_id=1, source_target_pairs={{0,1},{1,0},{2,3},{3,2},{4,5},{5,4},{6,7},{7,6},{8,9},{9,8},{10,11... | collective-permute-start | bytes 417800 | tf_op jit(solution)/shard_map/ppermute | solution.py:511
  24.4 7.5 %collective-permute-start.4 = (bf16[32,2176]{1,0:T(8,128)(2,1)S(1)}, bf16[32,2176]{1,0:T(8,128)(2,1)S(1)}, u32[]{:S(2)}, u32[]{:S(2)}) collective-permute-start(bf16[32,2176]{1,0:T(8,128)(2,1)S(1)} %collective-permute-done.3.part2_ref), channel_id=1, source_target_pairs={{0,1},{1,0},{2,3},{3,2},{4,5},{5,4},{6,7},{7,6},{8,9},{9,8},{10,11... | collective-permute-start | bytes 417800 | tf_op jit(solution)/shard_map/ppermute | solution.py:513
  24.4 16.4 %collective-permute-start.9 = (bf16[128,2048]{1,0:T(8,128)(2,1)S(1)}, bf16[128,2048]{1,0:T(8,128)(2,1)S(1)}, u32[]{:S(2)}, u32[]{:S(2)}) collective-permute-start(bf16[128,2048]{1,0:T(8,128)(2,1)S(1)} %copy-done.7), channel_id=1, source_target_pairs={{0,8},{4,12},{8,0},{12,4},{16,24},{20,28},{24,16},{28,20},{1,9},{5... | collective-permute-start | bytes 1572872 | tf_op jit(solution)/shard_map/ppermute | solution.py:447
  35.4 22.1 %all-to-all-start = ((bf16[8,144,256]{2,1,0:T(8,128)(2,1)}), bf16[8,144,256]{2,1,0:T(8,128)(2,1)S(1)}, u32[]{:S(2)}, u32[]{:S(2)}) async-start(bf16[8,144,256]{2,1,0:T(8,128)(2,1)} %get-tuple-element.15), calls=%async_computation | async-start | bytes 1179648 | tf_op jit(solution)/shard_map/all_to_all | solution.py:515
  40.2 4.2 %collective-permute-start.11 = (bf16[128,2048]{1,0:T(8,128)(2,1)S(1)}, bf16[128,2048]{1,0:T(8,128)(2,1)S(1)}, u32[]{:S(2)}, u32[]{:S(2)}) collective-permute-start(bf16[128,2048]{1,0:T(8,128)(2,1)S(1)} %copy-done.7), channel_id=1, source_target_pairs={{8,16},{12,20},{16,8},{20,12},{9,17},{13,21},{17,9},{21,13},{10,18... | collective-permute-start | bytes 1572872 | tf_op jit(solution)/shard_map/ppermute | solution.py:448
  40.9 65.5 %copy-start.9 = (bf16[128,2048]{1,0:T(8,128)(2,1)}, bf16[128,2048]{1,0:T(8,128)(2,1)S(1)}, u32[]{:S(2)}) copy-start(bf16[128,2048]{1,0:T(8,128)(2,1)S(1)} %collective-permute-done.9.rest_2_) | copy-start | bytes 1572868
  40.9 11.3 %collective-permute-start.15 = (bf16[128,2048]{1,0:T(8,128)(2,1)S(1)}, bf16[128,2048]{1,0:T(8,128)(2,1)S(1)}, u32[]{:S(2)}, u32[]{:S(2)}) collective-permute-start(bf16[128,2048]{1,0:T(8,128)(2,1)S(1)} %collective-permute-done.9.rest_2_), channel_id=1, source_target_pairs={{8,16},{12,20},{16,8},{20,12},{9,17},{13,21},{17,9},{21,13},{10,18... | collective-permute-start | bytes 1572872 | tf_op jit(solution)/shard_map/ppermute | solution.py:449
  41.6 65.6 %collective-permute-start.8 = (bf16[128,2048]{1,0:T(8,128)(2,1)S(1)}, bf16[128,2048]{1,0:T(8,128)(2,1)S(1)}, u32[]{:S(2)}, u32[]{:S(2)}) collective-permute-start(bf16[128,2048]{1,0:T(8,128)(2,1)S(1)} %copy-done.7), channel_id=1, source_target_pairs={{0,4},{4,0},{8,12},{12,8},{16,20},{20,16},{24,28},{28,24},{1,5},{5... | collective-permute-start | bytes 1572872 | tf_op jit(solution)/shard_map/ppermute | solution.py:446
  44.4 71.3 %collective-permute-start.10 = (bf16[128,2048]{1,0:T(8,128)(2,1)S(1)}, bf16[128,2048]{1,0:T(8,128)(2,1)}, u32[]{:S(2)}, u32[]{:S(2)}) collective-permute-start(bf16[128,2048]{1,0:T(8,128)(2,1)S(1)} %collective-permute-done.9.rest_2_), channel_id=1, source_target_pairs={{0,4},{4,0},{8,12},{12,8},{16,20},{20,16},{24,28},{28,24},{1,5},{5... | collective-permute-start | bytes 1572872 | tf_op jit(solution)/shard_map/ppermute | solution.py:450
  44.4 62.0 %copy-start.10 = (bf16[128,2048]{1,0:T(8,128)(2,1)}, bf16[128,2048]{1,0:T(8,128)(2,1)S(1)}, u32[]{:S(2)}) copy-start(bf16[128,2048]{1,0:T(8,128)(2,1)S(1)} %collective-permute-done.11.rest_4_) | copy-start | bytes 1572868
  44.4 63.5 %collective-permute-start.12 = (bf16[128,2048]{1,0:T(8,128)(2,1)S(1)}, bf16[128,2048]{1,0:T(8,128)(2,1)}, u32[]{:S(2)}, u32[]{:S(2)}) collective-permute-start(bf16[128,2048]{1,0:T(8,128)(2,1)S(1)} %collective-permute-done.11.rest_4_), channel_id=1, source_target_pairs={{8,0},{12,4},{16,24},{20,28},{9,1},{13,5},{17,25},{21,29},{10,2},{... | collective-permute-start | bytes 1572872 | tf_op jit(solution)/shard_map/ppermute | solution.py:451
  52.2 80.1 %copy-start.11 = (bf16[128,2048]{1,0:T(8,128)(2,1)}, bf16[128,2048]{1,0:T(8,128)(2,1)S(1)}, u32[]{:S(2)}) copy-start(bf16[128,2048]{1,0:T(8,128)(2,1)S(1)} %collective-permute-done.15.rest_8_) | copy-start | bytes 1572868
  52.2 58.1 %collective-permute-start.16 = (bf16[128,2048]{1,0:T(8,128)(2,1)S(1)}, bf16[128,2048]{1,0:T(8,128)(2,1)}, u32[]{:S(2)}, u32[]{:S(2)}) collective-permute-start(bf16[128,2048]{1,0:T(8,128)(2,1)S(1)} %collective-permute-done.15.rest_8_), channel_id=1, source_target_pairs={{8,0},{12,4},{16,24},{20,28},{9,1},{13,5},{17,25},{21,29},{10,2},{... | collective-permute-start | bytes 1572872 | tf_op jit(solution)/shard_map/ppermute | solution.py:452
  57.5 74.9 %copy-start.8 = (bf16[8,144,256]{2,1,0:T(8,128)(2,1)}, bf16[8,144,256]{2,1,0:T(8,128)(2,1)S(1)}, u32[]{:S(2)}) copy-start(bf16[8,144,256]{2,1,0:T(8,128)(2,1)S(1)} %all-to-all-done.grad_ref) | copy-start | bytes 1769476
  64.5 27.9 %collective-permute-start.5 = (f32[2,2048]{1,0:T(2,128)S(1)}, f32[2,2048]{1,0:T(2,128)S(1)}, u32[]{:S(2)}, u32[]{:S(2)}) collective-permute-start(f32[2,2048]{1,0:T(2,128)S(1)} %pad_maximum_fusion), channel_id=1, source_target_pairs={{0,8},{4,12},{8,0},{12,4},{16,24},{20,28},{24,16},{28,20},{1,9},{5... | collective-permute-start | bytes 49160 | tf_op jit(solution)/shard_map/ppermute | solution.py:477
  92.4 4.7 %collective-permute-start.6 = (f32[2,2048]{1,0:T(2,128)S(1)}, f32[2,2048]{1,0:T(2,128)S(1)}, u32[]{:S(2)}, u32[]{:S(2)}) collective-permute-start(f32[2,2048]{1,0:T(2,128)S(1)} %fusion), channel_id=1, source_target_pairs={{0,16},{4,20},{8,24},{12,28},{16,0},{20,4},{24,8},{28,12},{1,17},{... | collective-permute-start | bytes 49160 | tf_op jit(solution)/shard_map/ppermute | solution.py:477
  97.1 9.3 %collective-permute-start.7 = (f32[2,2048]{1,0:T(2,128)S(1)}, f32[2,2048]{1,0:T(2,128)S(1)}, u32[]{:S(2)}, u32[]{:S(2)}) collective-permute-start(f32[2,2048]{1,0:T(2,128)S(1)} %fusion.2), channel_id=1, source_target_pairs={{0,4},{4,0},{8,12},{12,8},{16,20},{20,16},{24,28},{28,24},{1,5},{5... | collective-permute-start | bytes 49160 | tf_op jit(solution)/shard_map/ppermute | solution.py:477
  106.4 9.3 %collective-permute-start.13 = (bf16[128,2048]{1,0:T(8,128)(2,1)S(1)}, bf16[128,2048]{1,0:T(8,128)(2,1)S(1)}, u32[]{:S(2)}, u32[]{:S(2)}) collective-permute-start(bf16[128,2048]{1,0:T(8,128)(2,1)S(1)} %collective-permute-done.11.rest_4_), channel_id=1, source_target_pairs={{8,12},{12,8},{16,20},{20,16},{9,13},{13,9},{17,21},{21,17},{10,14... | collective-permute-start | bytes 1572872 | tf_op jit(solution)/shard_map/ppermute | solution.py:453
  107.2 17.6 %collective-permute-start.17 = (bf16[128,2048]{1,0:T(8,128)(2,1)S(1)}, bf16[128,2048]{1,0:T(8,128)(2,1)S(1)}, u32[]{:S(2)}, u32[]{:S(2)}) collective-permute-start(bf16[128,2048]{1,0:T(8,128)(2,1)S(1)} %collective-permute-done.15.rest_8_), channel_id=1, source_target_pairs={{8,12},{12,8},{16,20},{20,16},{9,13},{13,9},{17,21},{21,17},{10,14... | collective-permute-start | bytes 1572872 | tf_op jit(solution)/shard_map/ppermute | solution.py:455
  107.9 16.9 %collective-permute-start.14 = (bf16[128,2048]{1,0:T(8,128)(2,1)}, bf16[128,2048]{1,0:T(8,128)(2,1)S(1)}, u32[]{:S(2)}, u32[]{:S(2)}) collective-permute-start(bf16[128,2048]{1,0:T(8,128)(2,1)} %collective-permute-done.12.rest_5_), channel_id=1, source_target_pairs={{0,4},{4,0},{24,28},{28,24},{1,5},{5,1},{25,29},{29,25},{2,6},{6,2... | collective-permute-start | bytes 1572872 | tf_op jit(solution)/shard_map/ppermute | solution.py:454
  110.3 22.0 %collective-permute-start.18 = (bf16[128,2048]{1,0:T(8,128)(2,1)}, bf16[128,2048]{1,0:T(8,128)(2,1)S(1)}, u32[]{:S(2)}, u32[]{:S(2)}) collective-permute-start(bf16[128,2048]{1,0:T(8,128)(2,1)} %collective-permute-done.16.rest_9_), channel_id=1, source_target_pairs={{0,4},{4,0},{24,28},{28,24},{1,5},{5,1},{25,29},{29,25},{2,6},{6,2... | collective-permute-start | bytes 1572872 | tf_op jit(solution)/shard_map/ppermute | solution.py:456
  (15 other events, 224.4 us)
where the time goes:
time: 140 us
  starting transfers between devices  51.5 us (37%)
  waiting for transfers between devices  36.8 us (26%)
  Pallas kernels  35.4 us (25%)
  blocking collectives  5.95 us (4%)
  local copies, waits for them, and re-layouts  5.35 us (4%)
  other arithmetic  3.7 us (3%)
    ppermute x3, starting transfers between devices, total_over_tok(): got = lax.ppermute(value, 'tok', [(i, i ^ flip) for i in range(count)])  26.4 us
    ppermute x1, waiting for transfers between devices, gather_blocks(): x2e = lax.ppermute(f1, 'tok', cross((0, 3)))  9.08 us
    ppermute x1, waiting for transfers between devices, gather_blocks(): x3e = lax.ppermute(f2, 'tok', cross((0, 3)))  7.58 us
    ppermute x3, waiting for transfers between devices, total_over_tok(): got = lax.ppermute(value, 'tok', [(i, i ^ flip) for i in range(count)])  7.04 us
    pallas_call x1, Pallas kernels, backward(): pl.pallas_call(functools.partial(backward_kernel, total), out_shape=jax.S...  7.03 us
    pallas_call x1, Pallas kernels, products(): pl.pallas_call(products_kernel, out_shape=jax.ShapeDtypeStruct((objective...  6.52 us
    pallas_call x1, Pallas kernels, weight_grad(): pl.pallas_call(functools.partial(weight_kernel, plan, depth), out_shape=j...  6.5 us
    pallas_call x1, Pallas kernels, forward(): pl.pallas_call(forward_kernel, out_shape=(out, out), in_specs=[smem(), vm...  6.12 us
  transfers between devices with their start and end apart: 20, of which 8 were waited for; matrix products, arithmetic and copies ran while one was open for 4% of the time, Pallas kernels for 15%

commit v1 on v0

--- a/solution.py
+++ b/solution.py
@@ -15,7 +15,7 @@
 BF = jnp.bfloat16
 F32 = jnp.float32
 MIB = 1 << 20
-BIG = 57
+BIG = 50
 
 
 def exchange(value, axis, flip):
@@ -64,7 +64,7 @@
 
 
 def hbm():
-    return pl.BlockSpec(memory_space=pl.ANY)
+    return pl.BlockSpec(memory_space=pltpu.HBM)
 
 
 def forward_kernel(core_ref, resid_ref, gain_ref, weight_hbm, keep_ref, send_ref, weight_ref, scaled_ref, sems):
@@ -280,13 +280,17 @@
     )(me, *parts, gram)
 
 
-def products_kernel(resid_ref, weight_hbm, grad_ref, along_ref, weight_ref, scal_ref, sems):
+def products_kernel(resid_ref, weight_hbm, grad_ref, prod_hbm, along_ref, weight_ref, prod_ref, scal_ref, sems, out_sems):
     objectives = along_ref.shape[0]
     columns = weight_hbm.shape[1]
     hidden = columns // objectives
     copy, depth = fetch_rows(weight_hbm, weight_ref, sems)
     inverse, _ = scales(grad_ref[:, columns:], objectives)
     scal_ref[...] = jnp.broadcast_to(inverse, scal_ref.shape)
+
+    def store(i):
+        rows = pl.ds(pl.multiple_of(i * depth, depth), depth)
+        return pltpu.make_async_copy(prod_ref.at[:, :, rows], prod_hbm.at[:, :, rows], out_sems.at[i])
 
     @pl.loop(0, sems.shape[0])
     def _(i):
@@ -299,142 +303,214 @@
                 grad_ref[:, cols], weight_ref[rows, cols], (((1,), (1,)), ((), ())), preferred_element_type=F32
             )
             along_ref[which : which + 1, rows] = jnp.sum(value * unit, axis=0, keepdims=True)
+            prod_ref[which, :, rows] = value.astype(BF)
+        store(i).start()
+
+    @pl.loop(0, sems.shape[0])
+    def _(i):
+        store(i).wait()
 
 
 def products(resid, weight, grad, objectives):
     tokens, features = resid.shape
+    shape = (objectives, tokens, features)
     return pl.pallas_call(
         products_kernel,
-        out_shape=jax.ShapeDtypeStruct((objectives, features), F32),
+        out_shape=(jax.ShapeDtypeStruct(shape, BF), jax.ShapeDtypeStruct((objectives, features), F32)),
         in_specs=[vmem(), hbm(), vmem()],
-        out_specs=vmem(),
+        out_specs=(hbm(), vmem()),
         scratch_shapes=[
             pltpu.VMEM(weight.shape, BF),
+            pltpu.VMEM(shape, BF),
             pltpu.VMEM((tokens, LANES), F32),
+            pltpu.SemaphoreType.DMA((4,)),
             pltpu.SemaphoreType.DMA((4,)),
         ],
         compiler_params=params(BIG),
-        cost_estimate=cost(2 * weight.size * tokens, 2 * weight.size),
+        cost_estimate=cost(2 * weight.size * tokens, 4 * weight.size),
         name="products",
     )(resid, weight, grad)
 
 
-def backward_kernel(
-    total, bal_ref, share_ref, resid_ref, gain_ref, weight_hbm, grad_ref, out_ref, weight_ref, pre_ref, scal_ref, sems
-):
-    columns = weight_hbm.shape[1]
-    copy, depth = fetch_rows(weight_hbm, weight_ref, sems)
-    pre_ref[...] = (grad_ref[:, :columns].astype(F32) * bal_ref[...]).astype(BF)
-    inverse, along = scales(grad_ref[:, columns:], share_ref.shape[1])
+def balance_kernel(entries, squares_ref, level_ref, along_ref, cols_ref, sums_ref, share_ref, wide_ref):
+    objectives = along_ref.shape[0]
+    hidden = wide_ref.shape[1] // objectives
+    rms = jnp.sqrt(squares_ref[...] / entries + grad_eps)
+    share = level_ref[...].astype(F32) / denominator / rms
+    share_ref[...] = share
+    row = lax.broadcasted_iota(jnp.int32, (objectives, objectives), 0)
+    lane = lax.broadcasted_iota(jnp.int32, (objectives, objectives), 1)
+    down = jnp.sum(jnp.where(row == lane, share, 0.0), axis=1, keepdims=True)
+    sums_ref[0:1, :] = jnp.sum(along_ref[...] * down, axis=0, keepdims=True)
+    sums_ref[1:2, :] = cols_ref[...]
+    for which in range(objectives):
+        wide_ref[:, which * hidden : (which + 1) * hidden] = jnp.broadcast_to(share[:, which : which + 1], (1, hidden))
+
+
+def balance_of(entries, squares, level, along, col_sums):
+    objectives, features = along.shape
+    columns = col_sums.shape[1]
+    return pl.pallas_call(
+        functools.partial(balance_kernel, entries),
+        out_shape=(
+            jax.ShapeDtypeStruct((2, features), F32),
+            jax.ShapeDtypeStruct((1, objectives), F32),
+            jax.ShapeDtypeStruct((1, columns), F32),
+        ),
+        in_specs=[vmem()] * 4,
+        out_specs=(vmem(), vmem(), vmem()),
+        compiler_params=params(4),
+        cost_estimate=cost(4 * along.size, 8 * along.size),
+        name="balance",
+    )(squares, level, along, col_sums)
+
+
+def backward_kernel(total, share_ref, row_ref, resid_ref, gain_ref, prod_hbm, extra_ref, out_ref, prod_ref, scal_ref, sems):
+    objectives, _, features = prod_hbm.shape
+    chunks = sems.shape[0]
+    depth = features // chunks
+
+    def copy(i):
+        part = pl.ds(pl.multiple_of(i * depth, depth), depth)
+        return pltpu.make_async_copy(prod_hbm.at[:, :, part], prod_ref.at[:, :, part], sems.at[i])
+
+    for i in range(chunks):
+        copy(i).start()
+    inverse, along = scales(extra_ref[...], objectives)
+    projection = jnp.sum(along * row_ref[...], axis=1, keepdims=True) / total
     scal_ref[0] = jnp.broadcast_to(inverse, scal_ref.shape[1:])
-    projection = jnp.sum(along * share_ref[...], axis=1, keepdims=True) / total
     scal_ref[1] = jnp.broadcast_to(projection, scal_ref.shape[1:])
 
-    @pl.loop(0, sems.shape[0])
+    @pl.loop(0, chunks)
     def _(i):
         copy(i).wait()
-        rows = pl.ds(pl.multiple_of(i * depth, depth), depth)
-        grad = lax.dot_general(
-            pre_ref[...], weight_ref[rows, :], (((1,), (1,)), ((), ())), preferred_element_type=F32
-        )
-        inverse = scal_ref[0, :, 0:1]
-        unit = resid_ref[:, rows].astype(F32) * inverse
-        out_ref[:, rows] = (inverse * (gain_ref[:, rows] * grad - unit * scal_ref[1, :, 0:1])).astype(BF)
-
-
-def backward(total, resid, gain, weight, grad, bal_cols, balance):
+
+        @pl.loop(0, depth // LANES)
+        def _(k):
+            part = pl.ds(pl.multiple_of(i * depth + k * LANES, LANES), LANES)
+            grad = prod_ref[0, :, part].astype(F32) * share_ref[0, 0]
+            for which in range(1, objectives):
+                grad += prod_ref[which, :, part].astype(F32) * share_ref[0, which]
+            inverse = scal_ref[0]
+            unit = resid_ref[:, part].astype(F32) * inverse
+            out_ref[:, part] = (inverse * (gain_ref[:, part] * grad - unit * scal_ref[1])).astype(BF)
+
+
+def backward(total, resid, gain, prods, grad, share):
     tokens, _ = resid.shape
+    tail = grad.shape[1] // LANES - 1
+    whole = lambda array: pl.BlockSpec(array.shape, lambda i: (0,) * array.ndim)
     return pl.pallas_call(
         functools.partial(backward_kernel, total),
         out_shape=jax.ShapeDtypeStruct(resid.shape, BF),
-        in_specs=[vmem(), vmem(), vmem(), vmem(), hbm(), vmem()],
-        out_specs=vmem(),
+        grid=(1,),
+        in_specs=[
+            smem(),
+            whole(share),
+            whole(resid),
+            whole(gain),
+            hbm(),
+            pl.BlockSpec((tokens, LANES), lambda i: (0, tail)),
+        ],
+        out_specs=whole(resid),
         scratch_shapes=[
-            pltpu.VMEM(weight.shape, BF),
-            pltpu.VMEM((tokens, weight.shape[1]), BF),
+            pltpu.VMEM(prods.shape, BF),
             pltpu.VMEM((2, tokens, LANES), F32),
             pltpu.SemaphoreType.DMA((4,)),
         ],
         compiler_params=params(BIG),
-        cost_estimate=cost(2 * weight.size * tokens, 2 * weight.size),
+        cost_estimate=cost(2 * prods.size, 2 * prods.size),
         name="backward",
-    )(bal_cols, balance, resid, gain, weight, grad)
-
-
-def weight_kernel(plan, depth, order_ref, gain_ref, scale_ref, grad_ref, *rest):
+    )(share, share, resid, gain, prods, grad)
+
+
+def weight_kernel(plan, order_of, depth, place_ref, gain_ref, wide_ref, sum_ref, got_ref, grad_ref, *rest):
     count = len(plan)
-    block_refs = rest[:-6]
-    out_hbm, turned_ref, blocks_ref, result_ref, sems, out_sems = rest[-6:]
+    block_refs = rest[:-8]
+    out_hbm, gain_out_ref, bias_out_ref, turned_ref, blocks_ref, result_ref, sems, out_sems = rest[-8:]
     tokens, features = block_refs[0].shape
-    steps = features // depth
-    inner = order_ref[count]
-
-    def load(k, source):
-        place = pl.ds(k * tokens, tokens)
-        return pltpu.make_async_copy(block_refs[source], blocks_ref.at[place, :], sems.at[k])
-
-    for k, choice in enumerate(plan):
-        if len(choice) == 1:
-            load(k, choice[0]).start()
-        else:
-
-            @pl.when(inner == 1)
-            def _():
-                load(k, choice[0]).start()
-
-            @pl.when(inner == 0)
-            def _():
-                load(k, choice[1]).start()
+    columns = grad_ref.shape[2]
+    total_tokens = tokens * count
+    order, inner = order_of(place_ref[0])
+    chunks = sems.shape[1]
+    width = features // chunks
+
+    def load(k, source, i):
+        place = (pl.ds(k * tokens, tokens), pl.ds(i * width, width))
+        return pltpu.make_async_copy(block_refs[source].at[:, place[1]], blocks_ref.at[place], sems.at[k, i])
+
+    for i in range(chunks):
+        for k, choice in enumerate(plan):
+            if len(choice) == 1:
+                load(k, choice[0], i).start()
+            else:
+
+                @pl.when(inner == 1)
+                def _():
+                    load(k, choice[0], i).start()
+
+                @pl.when(inner == 0)
+                def _():
+                    load(k, choice[1], i).start()
 
     for k in range(count):
-        turned_ref[:, k * tokens : (k + 1) * tokens] = grad_ref[order_ref[k], :tokens, :].T
-    for k, choice in enumerate(plan):
-        load(k, choice[0]).wait()
+        turned_ref[:, k * tokens : (k + 1) * tokens] = grad_ref[order[k], :tokens, :].T
+    sums = (sum_ref[...] + got_ref[...]) / total_tokens
+    gain_out_ref[...] = sums[0:1]
+    bias_out_ref[...] = sums[1:2] * wide_ref[...]
+    start = pl.multiple_of(place_ref[0] * columns, columns)
+    scale = wide_ref[:, pl.ds(start, columns)] / total_tokens
 
     def store(i):
         rows = pl.ds(pl.multiple_of(i * depth, depth), depth)
         return pltpu.make_async_copy(result_ref.at[rows, :], out_hbm.at[rows, :], out_sems.at[i])
 
-    @pl.loop(0, steps)
-    def _(i):
-        part = pl.ds(pl.multiple_of(i * depth, depth), depth)
-        value = jnp.dot(turned_ref[...], blocks_ref[:, part], preferred_element_type=F32)
-        result_ref[part, :] = (value * gain_ref[:, part]).T * scale_ref[...]
-        store(i).start()
-
-    @pl.loop(0, steps)
-    def _(i):
-        store(i).wait()
-
-
-def weight_grad(order, gain, col_scale, grads, blocks, plan):
+    for i in range(chunks):
+        for k, choice in enumerate(plan):
+            load(k, choice[0], i).wait()
+
+        @pl.loop(i * width // depth, (i + 1) * width // depth)
+        def _(step):
+            part = pl.ds(pl.multiple_of(step * depth, depth), depth)
+            value = jnp.dot(turned_ref[...], blocks_ref[:, part], preferred_element_type=F32)
+            result_ref[part, :] = (value * gain_ref[:, part]).T * scale
+            store(step).start()
+
+    @pl.loop(0, features // depth)
+    def _(step):
+        store(step).wait()
+
+
+def weight_grad(place, gain, wide, sums, got, grads, blocks, plan, order_of):
     tokens, features = blocks[0].shape
     columns = grads.shape[2]
     depth = 512
     count = len(plan)
     return pl.pallas_call(
-        functools.partial(weight_kernel, plan, depth),
-        out_shape=jax.ShapeDtypeStruct((features, columns), F32),
-        in_specs=[smem(), vmem(), vmem(), vmem()] + [hbm()] * len(blocks),
-        out_specs=hbm(),
+        functools.partial(weight_kernel, plan, order_of, depth),
+        out_shape=(
+            jax.ShapeDtypeStruct((features, columns), F32),
+            jax.ShapeDtypeStruct((1, features), F32),
+            jax.ShapeDtypeStruct(wide.shape, F32),
+        ),
+        in_specs=[smem()] + [vmem()] * 5 + [hbm()] * len(blocks),
+        out_specs=(hbm(), vmem(), vmem()),
         scratch_shapes=[
             pltpu.VMEM((columns, tokens * count), BF),
             pltpu.VMEM((tokens * count, features), BF),
             pltpu.VMEM((features, columns), F32),
-            pltpu.SemaphoreType.DMA((count,)),
+            pltpu.SemaphoreType.DMA((count, 2)),
             pltpu.SemaphoreType.DMA((features // depth,)),
         ],
         compiler_params=params(BIG),
         cost_estimate=cost(2 * tokens * count * features * columns, 8 * features * columns),
         name="weights",
-    )(order, gain, col_scale, grads, *blocks)
+    )(place, gain, wide, sums, got, grads, *blocks)
 
 
 def gather_blocks(resid):
     count = lax.axis_size("tok")
-    place = lax.axis_index("tok")
     if count == 8:
-        line, side = place // 2, place % 2
 
         def pairs(moves):
             return [(2 * a + s, 2 * b + s) for a, b in moves for s in range(2)]
@@ -454,29 +530,35 @@
         x2e = lax.ppermute(f1, "tok", cross((0, 3)))
         x3m = lax.ppermute(m2, "tok", cross((1, 2)))
         x3e = lax.ppermute(f2, "tok", cross((0, 3)))
-        low = line < 2
-        inner = (line == 1) | (line == 2)
-        lines = [line, line ^ 1, jnp.where(low, 2, 1), jnp.where(low, 3, 0)]
-        order = [2 * a + (side ^ s) for a in lines for s in range(2)] + [inner.astype(jnp.int32)]
+
+        def order_of(place):
+            line, side = place // 2, place % 2
+            low = line < 2
+            inner = jnp.where((line == 1) | (line == 2), 1, 0)
+            lines = [line, jnp.where(line % 2 == 0, line + 1, line - 1), jnp.where(low, 2, 1), jnp.where(low, 3, 0)]
+            return [2 * a + s for a in lines for s in (side, 1 - side)], inner
+
         blocks = [resid, x0, z1, x1, m1, f1, x2m, x2e, m2, f2, x3m, x3e]
         plan = ((0,), (1,), (2,), (3,), (4, 5), (6, 7), (8, 9), (10, 11))
-        return blocks, jnp.stack(order), plan
+        return blocks, plan, order_of
     found = {0: resid}
     for flip in range(2, count, 2):
         found[flip] = exchange(resid, "tok", flip)
     for flip in range(0, count, 2):
         found[flip + 1] = exchange(found[flip], "tok", 1)
-    order = jnp.append(place ^ jnp.arange(count), 0)
-    return [found[flip] for flip in range(count)], order, tuple((flip,) for flip in range(count))
+    plan = tuple((flip,) for flip in range(count))
+    return [found[flip] for flip in range(count)], plan, lambda place: ([place ^ flip for flip in range(count)], 0)
 
 
 def total_over_tok(value):
     count = lax.axis_size("tok")
-    flips = [1 << bit for bit in range(1, count.bit_length() - 1)] + [1] * (count > 1)
-    for flip in flips:
+    flips = [1 << bit for bit in range(1, count.bit_length() - 1)] + [1]
+    got = None
+    for step, flip in enumerate(flips):
+        if step:
+            value = value + got
         got = lax.ppermute(value, "tok", [(i, i ^ flip) for i in range(count)])
-        value = value + got
-    return value
+    return value, got
 
 
 def fast_device(resid, norm_gain, head_in, head_bias, head_out, targets, label_mask, obj_weight):
@@ -492,7 +574,7 @@
     partner = [(i, i ^ 1) for i in range(4)]
     across = [(i, i ^ 2) for i in range(4)]
 
-    blocks, order, plan = gather_blocks(resid)
+    blocks, plan, order_of = gather_blocks(resid)
     keep, send = forward((me % 2)[None], resid, gain, head_in)
     recv = lax.ppermute(send, "tp", partner)
     mine, send = merge((me // 2)[None], keep, recv)
@@ -513,22 +595,17 @@
     part3 = lax.ppermute(part2, "tp", partner)
     grad, message, col_sums = spread(me[None], (part, part1, part2, part3), gram, peers)
     grads = lax.all_to_all(message, "tok", 0, 0)
-    along = products(resid, head_in, grad, objectives)
+    prods, along = products(resid, head_in, grad, objectives)
     squares = jnp.sum(grads[:, tokens : tokens + 3, :objectives].astype(F32), axis=(0, 1))
-    squares = lax.psum(squares, "tp")
-    obj_rms = jnp.sqrt(squares / (total_tokens * total_features) + grad_eps)
-    balance = obj_weight.astype(F32) / denominator / obj_rms
-    bal_cols = jnp.repeat(balance, hidden)
-    gain_part = jnp.sum(balance[:, None] * along, axis=0, keepdims=True)
-    sums = jnp.concatenate([gain_part, col_sums], axis=0)
-    sums = total_over_tok(sums)
-    resid_grad = backward(total_features, resid, gain, head_in, grad, bal_cols[None, :], balance[None, :])
-    gain_grad = sums[0] / total_tokens
-    head_bias_grad = sums[1] * bal_cols / total_tokens
-    width = columns // peers
-    col_scale = lax.dynamic_slice_in_dim(bal_cols, place * width, width, 0) / total_tokens
-    head_in_grad = weight_grad(order, gain, col_scale[None, :], grads, blocks, plan)
-    return (resid_grad, gain_grad, head_in_grad, head_bias_grad)
+    squares = lax.psum(squares, "tp")[None, :]
+    entries = total_tokens * total_features
+    sums, share, wide = balance_of(entries, squares, obj_weight[None, :], along, col_sums)
+    sums, got = total_over_tok(sums)
+    resid_grad = backward(total_features, resid, gain, prods, grad, share)
+    head_in_grad, gain_grad, head_bias_grad = weight_grad(
+        place[None], gain, wide, sums, got, grads, blocks, plan, order_of
+    )
+    return (resid_grad, gain_grad[0], head_in_grad, head_bias_grad[0])
 
 
 def head_gradient(preact, head_out, targets, label_mask):
@@ -605,7 +682,7 @@
     tokens, features = resid.shape[0] // peers, resid.shape[1] // shards
     width = columns // peers
     fits = shards == 4 and peers & (peers - 1) == 0 and columns % peers == 0
-    fits = fits and width % LANES == 0 and head_out.shape[1] == LANES and head_out.shape[0] <= 32
+    fits = fits and peers > 1 and width % LANES == 0 and head_out.shape[1] == LANES and head_out.shape[0] <= 32
     return fits and tokens % 128 == 0 and features % 512 == 0 and columns % 1024 == 0
 
 

time: 140 us -> 133 us (0.950)
  starting transfers between devices: 51.5 us -> 65.2 us
  waiting for transfers between devices: 36.8 us -> 26.4 us
  Pallas kernels: 35.4 us -> 30.7 us
  other arithmetic: 3.7 us -> 0.77 us
  local copies, waits for them, and re-layouts: 5.35 us -> 2.56 us
    ppermute x3, starting transfers between devices: 26.4 us -> 35.5 us  [total_over_tok(): got = lax.ppermute(value, 'tok', [(i, i ^ flip) for i in range(count)])]
    ppermute x1, waiting for transfers between devices: 7.58 us -> 0.01 us  [gather_blocks(): x3e = lax.ppermute(f2, 'tok', cross((0, 3)))]
    ppermute x1, waiting for transfers between devices: 9.08 us -> 3.38 us  [gather_blocks(): x2e = lax.ppermute(f1, 'tok', cross((0, 3)))]
    ppermute x3, waiting for transfers between devices: 7.04 us -> 9.85 us  [total_over_tok(): got = lax.ppermute(value, 'tok', [(i, i ^ flip) for i in range(count)])]
    div x3 -> x0, other arithmetic: 1.98 us -> none  [the longest x1 1.32 us: fast_device(): head_bias_grad = sums[1] * bal_cols / total_tokens]
    pallas_call x1, Pallas kernels: 6.12 us -> 4.2 us  [forward(): pl.pallas_call(forward_kernel, out_shape=(out, out), in_specs=[smem(), vm...]
    ppermute x1, waiting for transfers between devices: 3.97 us -> 2.4 us  [fast_device(): recv = lax.ppermute(send, 'tp', across)]
    ppermute x1, waiting for transfers between devices: 0.01 us -> 1.57 us  [gather_blocks(): x1 = lax.ppermute(z1, 'tok', cross(range(4)))]
  transfers between devices with their start and end apart: 20 -> 20, of which waited for: 8 -> 8; matrix products, arithmetic and copies ran while one was open for 4% -> 1% of each run, Pallas kernels for 15% -> 15%
where the time goes in v1:
time: 133 us; the launch traced here: 132 us
  starting transfers between devices  65.2 us (49%)
  Pallas kernels  30.7 us (23%)
  waiting for transfers between devices  26.4 us (20%)
  blocking collectives  5.66 us (4%)
  local copies, waits for them, and re-layouts  2.56 us (2%)
    ppermute x3, starting transfers between devices, total_over_tok(): got = lax.ppermute(value, 'tok', [(i, i ^ flip) for i in range(count)])  35.5 us
    ppermute x3, waiting for transfers between devices, total_over_tok(): got = lax.ppermute(value, 'tok', [(i, i ^ flip) for i in range(count)])  9.85 us
    pallas_call x1, Pallas kernels, products(): pl.pallas_call(products_kernel, out_shape=(jax.ShapeDtypeStruct(shape, BF...  6.38 us
    pallas_call x1, Pallas kernels, weight_grad(): pl.pallas_call(functools.partial(weight_kernel, plan, order_of, depth), o...  6.17 us
    all_to_all x1, starting transfers between devices, fast_device(): grads = lax.all_to_all(message, 'tok', 0, 0)  5.95 us
    pallas_call x1, Pallas kernels, backward(): pl.pallas_call(functools.partial(backward_kernel, total), out_shape=jax.S...  5.68 us
    psum x1, blocking collectives, fast_device(): squares = lax.psum(squares, 'tp')[None, :]  5.66 us
    pallas_call x1, Pallas kernels, gram_of(): pl.pallas_call(gram_kernel, out_shape=jax.ShapeDtypeStruct((objectives, h...  4.74 us
  transfers between devices with their start and end apart: 20, of which 8 were waited for; matrix products, arithmetic and copies ran while one was open for 1% of the time, Pallas kernels for 15%

profile of v1, /device:TPU:0, one launch (start us, length us, event | category | flops | bytes accessed | tf_op | source)
XLA Modules:
  0.0 132.3 jit_solution(11145963739336021308)
XLA Ops:
  2.4 4.2 %forward.1 = (f32[2,32,2176]{2,1,0:T(8,128)S(1)}, f32[2,32,2176]{2,1,0:T(8,128)S(1)}) custom-call(s32[1]{0:T(128)} %bitcast.2.core_ref, bf16[128,2048]{1,0:T(8,128)(2,1)S(1)} %copy-done, f32[1,2048]{1,0:T(1,128)S(1)} %bitcast.13, bf16[2048,2048]{1,0:T(8,128)(2,1)} %weight_hbm.5), custom_call_target="tpu_custom_call" | custom-call | flops 1073741824 | bytes 8388608 | tf_op jit(solution)/shard_map/forward/pallas_call | solution.py:105
  7.2 1.6 %collective-permute-done.recv_ref = f32[2,32,2176]{2,1,0:T(8,128)S(1)} collective-permute-done((f32[2,32,2176]{2,1,0:T(8,128)S(1)}, f32[2,32,2176]{2,1,0:T(8,128)S(1)}, u32[]{:S(2)}, u32[]{:S(2)}) %collective-permute-start) | collective-permute-done | bytes 557088 | tf_op jit(solution)/shard_map/ppermute | solution.py:579
  8.8 2.9 %collective-permute-start.1 = (bf16[32,2176]{1,0:T(8,128)(2,1)S(1)}, bf16[32,2176]{1,0:T(8,128)(2,1)S(1)}, u32[]{:S(2)}, u32[]{:S(2)}) collective-permute-start(bf16[32,2176]{1,0:T(8,128)(2,1)S(1)} %get-tuple-element.22), channel_id=1, source_target_pairs={{0,2},{1,3},{2,0},{3,1},{4,6},{5,7},{6,4},{7,5},{8,10},{9,11},{10,... | collective-permute-start | bytes 417800 | tf_op jit(solution)/shard_map/ppermute | solution.py:581
  11.8 1.6 %collective-permute-start.9 = (bf16[128,2048]{1,0:T(8,128)(2,1)S(1)}, bf16[128,2048]{1,0:T(8,128)(2,1)S(1)}, u32[]{:S(2)}, u32[]{:S(2)}) collective-permute-start(bf16[128,2048]{1,0:T(8,128)(2,1)S(1)} %copy-done.1), channel_id=1, source_target_pairs={{0,8},{4,12},{8,0},{12,4},{16,24},{20,28},{24,16},{28,20},{1,9},{5... | collective-permute-start | bytes 1572872 | tf_op jit(solution)/shard_map/ppermute | solution.py:523
  13.4 2.4 %collective-permute-done.1.recv_ref = bf16[32,2176]{1,0:T(8,128)(2,1)S(1)} collective-permute-done((bf16[32,2176]{1,0:T(8,128)(2,1)S(1)}, bf16[32,2176]{1,0:T(8,128)(2,1)S(1)}, u32[]{:S(2)}, u32[]{:S(2)}) %collective-permute-start.1) | collective-permute-done | bytes 139296 | tf_op jit(solution)/shard_map/ppermute | solution.py:581
  15.8 2.0 %heads.1.part0_ref = bf16[32,2176]{1,0:T(8,128)(2,1)S(1)} custom-call(s32[1]{0:T(128)} %bitcast.me_ref.spot_ref, f32[32,2176]{1,0:T(8,128)S(1)} %get-tuple-element.21.mine_ref, bf16[32,2176]{1,0:T(8,128)(2,1)S(1)} %collective-permute-done.1.recv_ref, f32[1,2048]{1,0:T(1,128)S(1)} %bitcast.16, f32[1,2048]{1,0:T(1,128)S(1)} %bitcast.17, ...), custom_call_target="tpu_custom_call" | custom-call | flops 2088960 | bytes 557056 | tf_op jit(solution)/shard_map/heads/pallas_call | solution.py:190
  17.8 1.8 %collective-permute-start.3 = (bf16[32,2176]{1,0:T(8,128)(2,1)S(1)}, bf16[32,2176]{1,0:T(8,128)(2,1)S(1)}, u32[]{:S(2)}, u32[]{:S(2)}) collective-permute-start(bf16[32,2176]{1,0:T(8,128)(2,1)S(1)} %heads.1.part0_ref), channel_id=1, source_target_pairs={{0,2},{1,3},{2,0},{3,1},{4,6},{5,7},{6,4},{7,5},{8,10},{9,11},{10,... | collective-permute-start | bytes 417800 | tf_op jit(solution)/shard_map/ppermute | solution.py:594
  19.6 3.4 %collective-permute-done.3.part2_ref = bf16[32,2176]{1,0:T(8,128)(2,1)S(1)} collective-permute-done((bf16[32,2176]{1,0:T(8,128)(2,1)S(1)}, bf16[32,2176]{1,0:T(8,128)(2,1)S(1)}, u32[]{:S(2)}, u32[]{:S(2)}) %collective-permute-start.3) | collective-permute-done | bytes 139296 | tf_op jit(solution)/shard_map/ppermute | solution.py:594
  23.0 4.7 %gram.1.gram_ref = f32[16,128,128]{2,1,0:T(8,128)S(1)} custom-call(bf16[2048,2048]{1,0:T(8,128)(2,1)} %weight_hbm.5), custom_call_target="tpu_custom_call" | custom-call | flops 1073741824 | bytes 8388608 | tf_op jit(solution)/shard_map/gram/pallas_call | solution.py:222
  29.1 6.0 %all-to-all-start = ((bf16[8,144,256]{2,1,0:T(8,128)(2,1)}), bf16[8,144,256]{2,1,0:T(8,128)(2,1)}, u32[]{:S(2)}, u32[]{:S(2)}) async-start(bf16[8,144,256]{2,1,0:T(8,128)(2,1)} %get-tuple-element.23), calls=%async_computation | async-start | bytes 1179648 | tf_op jit(solution)/shard_map/all_to_all | solution.py:597
  37.3 2.0 %collective-permute-start.8 = (bf16[128,2048]{1,0:T(8,128)(2,1)S(1)}, bf16[128,2048]{1,0:T(8,128)(2,1)S(1)}, u32[]{:S(2)}, u32[]{:S(2)}) collective-permute-start(bf16[128,2048]{1,0:T(8,128)(2,1)S(1)} %copy-done.1), channel_id=1, source_target_pairs={{0,4},{4,0},{8,12},{12,8},{16,20},{20,16},{24,28},{28,24},{1,5},{5... | collective-permute-start | bytes 1572872 | tf_op jit(solution)/shard_map/ppermute | solution.py:522
  41.9 6.4 %products.1 = (bf16[16,128,2048]{2,1,0:T(8,128)(2,1)}, f32[16,2048]{1,0:T(8,128)S(1)}) custom-call(bf16[128,2048]{1,0:T(8,128)(2,1)S(1)} %copy-done.1, bf16[2048,2048]{1,0:T(8,128)(2,1)} %weight_hbm.5, bf16[128,2176]{1,0:T(8,128)(2,1)S(1)} %get-tuple-element.24.grad_ref.extra_ref), custom_call_target="tpu_custom_call" | custom-call | flops 1073741824 | bytes 16777216 | tf_op jit(solution)/shard_map/products/pallas_call | solution.py:317
  48.3 4.2 %all-to-all-done.grad_ref = bf16[8,144,256]{2,1,0:T(8,128)(2,1)} async-done(((bf16[8,144,256]{2,1,0:T(8,128)(2,1)}), bf16[8,144,256]{2,1,0:T(8,128)(2,1)}, u32[]{:S(2)}, u32[]{:S(2)}) %all-to-all-start) | async-done | bytes 589856 | tf_op jit(solution)/shard_map/all_to_all | solution.py:597
  53.2 5.7 %psum.7.squares_ref = f32[1,16]{1,0:T(1,128)S(1)} all-reduce(f32[1,16]{1,0:T(1,128)S(1)} %bitcast.21), channel_id=1, replica_groups=mesh['tok'=8,'tp'=4] {'tp'}, use_global_device_ids=true, to_apply=%region_1.2 | all-reduce | flops 16 | bytes 128 | tf_op jit(solution)/shard_map/psum | solution.py:600
  59.0 31.3 %collective-permute-start.5 = (f32[2,2048]{1,0:T(2,128)S(1)}, f32[2,2048]{1,0:T(2,128)S(1)}, u32[]{:S(2)}, u32[]{:S(2)}) collective-permute-start(f32[2,2048]{1,0:T(2,128)S(1)} %get-tuple-element.30), channel_id=1, source_target_pairs={{0,8},{4,12},{8,0},{12,4},{16,24},{20,28},{24,16},{28,20},{1,9},{5... | collective-permute-start | bytes 49160 | tf_op jit(solution)/shard_map/ppermute | solution.py:560
  92.1 2.7 %collective-permute-start.6 = (f32[2,2048]{1,0:T(2,128)S(1)}, f32[2,2048]{1,0:T(2,128)S(1)}, u32[]{:S(2)}, u32[]{:S(2)}) collective-permute-start(f32[2,2048]{1,0:T(2,128)S(1)} %add.14), channel_id=1, source_target_pairs={{0,16},{4,20},{8,24},{12,28},{16,0},{20,4},{24,8},{28,12},{1,17},{... | collective-permute-start | bytes 49160 | tf_op jit(solution)/shard_map/ppermute | solution.py:560
  94.8 1.5 %collective-permute-start.13 = (bf16[128,2048]{1,0:T(8,128)(2,1)S(1)}, bf16[128,2048]{1,0:T(8,128)(2,1)}, u32[]{:S(2)}, u32[]{:S(2)}) collective-permute-start(bf16[128,2048]{1,0:T(8,128)(2,1)S(1)} %collective-permute-done.11.rest_4_), channel_id=1, source_target_pairs={{8,12},{12,8},{16,20},{20,16},{9,13},{13,9},{17,21},{21,17},{10,14... | collective-permute-start | bytes 1572872 | tf_op jit(solution)/shard_map/ppermute | solution.py:529
  96.2 3.5 %collective-permute-start.14 = (bf16[128,2048]{1,0:T(8,128)(2,1)S(1)}, bf16[128,2048]{1,0:T(8,128)(2,1)}, u32[]{:S(2)}, u32[]{:S(2)}) collective-permute-start(bf16[128,2048]{1,0:T(8,128)(2,1)S(1)} %collective-permute-done.12.rest_5_), channel_id=1, source_target_pairs={{0,4},{4,0},{24,28},{28,24},{1,5},{5,1},{25,29},{29,25},{2,6},{6,2... | collective-permute-start | bytes 1572872 | tf_op jit(solution)/shard_map/ppermute | solution.py:530
  101.3 2.3 %collective-permute-start.18 = (bf16[128,2048]{1,0:T(8,128)(2,1)}, bf16[128,2048]{1,0:T(8,128)(2,1)}, u32[]{:S(2)}, u32[]{:S(2)}) collective-permute-start(bf16[128,2048]{1,0:T(8,128)(2,1)} %collective-permute-done.16.rest_9_), channel_id=1, source_target_pairs={{0,4},{4,0},{24,28},{28,24},{1,5},{5,1},{25,29},{29,25},{2,6},{6,2... | collective-permute-start | bytes 1572872 | tf_op jit(solution)/shard_map/ppermute | solution.py:532
  103.6 1.6 %collective-permute-done.10.rest_3_ = bf16[128,2048]{1,0:T(8,128)(2,1)S(1)} collective-permute-done((bf16[128,2048]{1,0:T(8,128)(2,1)S(1)}, bf16[128,2048]{1,0:T(8,128)(2,1)S(1)}, u32[]{:S(2)}, u32[]{:S(2)}) %collective-permute-start.10) | collective-permute-done | bytes 524320 | tf_op jit(solution)/shard_map/ppermute | solution.py:526
  107.4 5.7 %backward.1 = bf16[128,2048]{1,0:T(8,128)(2,1)} custom-call(f32[1,16]{1,0:T(1,128)S(1)} %get-tuple-element.27.share_ref.row_ref, f32[1,16]{1,0:T(1,128)S(1)} %get-tuple-element.27.share_ref.row_ref, bf16[128,2048]{1,0:T(8,128)(2,1)S(1)} %copy-done.1, f32[1,2048]{1,0:T(1,128)S(1)} %bitcast.14, bf16[16,128,2048]{2,1,0:T(8,128)(2,1)} %get-tuple-element.28.prod_hbm, ...), custom_call_target="tpu_custom_call" | custom-call | flops 8388608 | bytes 8388608 | tf_op jit(solution)/shard_map/backward/pallas_call | solution.py:403
  113.1 3.4 %collective-permute-done.14.rest_7_ = bf16[128,2048]{1,0:T(8,128)(2,1)} collective-permute-done((bf16[128,2048]{1,0:T(8,128)(2,1)S(1)}, bf16[128,2048]{1,0:T(8,128)(2,1)}, u32[]{:S(2)}, u32[]{:S(2)}) %collective-permute-start.14) | collective-permute-done | bytes 524320 | tf_op jit(solution)/shard_map/ppermute | solution.py:530
  116.5 9.6 %collective-permute-done.7.got_ref = f32[2,2048]{1,0:T(2,128)S(1)} collective-permute-done((f32[2,2048]{1,0:T(2,128)S(1)}, f32[2,2048]{1,0:T(2,128)S(1)}, u32[]{:S(2)}, u32[]{:S(2)}) %collective-permute-start.7) | collective-permute-done | bytes 16416 | tf_op jit(solution)/shard_map/ppermute | solution.py:560
  126.1 6.2 %weights.1 = (f32[2048,256]{1,0:T(8,128)}, f32[1,2048]{1,0:T(1,128)}, f32[1,2048]{1,0:T(1,128)}) custom-call(s32[1]{0:T(128)} %bitcast.10.place_ref, f32[1,2048]{1,0:T(1,128)S(1)} %bitcast.15, f32[1,2048]{1,0:T(1,128)S(1)} %get-tuple-element.29.wide_ref, f32[2,2048]{1,0:T(2,128)S(1)} %add.15.sum_ref, f32[2,2048]{1,0:T(2,128)S(1)} %collective-permute-done.7.got_ref, ...), custom_call_target="tpu_custom_call" | custom-call | flops 1073741824 | bytes 4194304 | tf_op jit(solution)/shard_map/weights/pallas_call | solution.py:489
  (51 shorter events, 14.8 us)
Async XLA Ops:
  0.6 15.1 %copy-start.6 = (f32[2048]{0:T(1024)S(1)}, f32[2048]{0:T(1024)}, u32[]{:S(2)}) copy-start(f32[2048]{0:T(1024)} %param.11) | copy-start | bytes 24580
  6.6 2.1 %collective-permute-start = (f32[2,32,2176]{2,1,0:T(8,128)S(1)}, f32[2,32,2176]{2,1,0:T(8,128)S(1)}, u32[]{:S(2)}, u32[]{:S(2)}) collective-permute-start(f32[2,32,2176]{2,1,0:T(8,128)S(1)} %get-tuple-element.20), channel_id=1, source_target_pairs={{0,1},{1,0},{2,3},{3,2},{4,5},{5,4},{6,7},{7,6},{8,9},{9,8},{10,11... | collective-permute-start | bytes 1671176 | tf_op jit(solution)/shard_map/ppermute | solution.py:579
  8.8 6.9 %collective-permute-start.1 = (bf16[32,2176]{1,0:T(8,128)(2,1)S(1)}, bf16[32,2176]{1,0:T(8,128)(2,1)S(1)}, u32[]{:S(2)}, u32[]{:S(2)}) collective-permute-start(bf16[32,2176]{1,0:T(8,128)(2,1)S(1)} %get-tuple-element.22), channel_id=1, source_target_pairs={{0,2},{1,3},{2,0},{3,1},{4,6},{5,7},{6,4},{7,5},{8,10},{9,11},{10,... | collective-permute-start | bytes 417800 | tf_op jit(solution)/shard_map/ppermute | solution.py:581
  11.8 24.0 %collective-permute-start.9 = (bf16[128,2048]{1,0:T(8,128)(2,1)S(1)}, bf16[128,2048]{1,0:T(8,128)(2,1)S(1)}, u32[]{:S(2)}, u32[]{:S(2)}) collective-permute-start(bf16[128,2048]{1,0:T(8,128)(2,1)S(1)} %copy-done.1), channel_id=1, source_target_pairs={{0,8},{4,12},{8,0},{12,4},{16,24},{20,28},{24,16},{28,20},{1,9},{5... | collective-permute-start | bytes 1572872 | tf_op jit(solution)/shard_map/ppermute | solution.py:523
  17.8 5.2 %collective-permute-start.3 = (bf16[32,2176]{1,0:T(8,128)(2,1)S(1)}, bf16[32,2176]{1,0:T(8,128)(2,1)S(1)}, u32[]{:S(2)}, u32[]{:S(2)}) collective-permute-start(bf16[32,2176]{1,0:T(8,128)(2,1)S(1)} %heads.1.part0_ref), channel_id=1, source_target_pairs={{0,2},{1,3},{2,0},{3,1},{4,6},{5,7},{6,4},{7,5},{8,10},{9,11},{10,... | collective-permute-start | bytes 417800 | tf_op jit(solution)/shard_map/ppermute | solution.py:594
  19.6 8.2 %collective-permute-start.2 = (bf16[32,2176]{1,0:T(8,128)(2,1)S(1)}, bf16[32,2176]{1,0:T(8,128)(2,1)S(1)}, u32[]{:S(2)}, u32[]{:S(2)}) collective-permute-start(bf16[32,2176]{1,0:T(8,128)(2,1)S(1)} %heads.1.part0_ref), channel_id=1, source_target_pairs={{0,1},{1,0},{2,3},{3,2},{4,5},{5,4},{6,7},{7,6},{8,9},{9,8},{10,11... | collective-permute-start | bytes 417800 | tf_op jit(solution)/shard_map/ppermute | solution.py:593
  23.0 4.8 %collective-permute-start.4 = (bf16[32,2176]{1,0:T(8,128)(2,1)S(1)}, bf16[32,2176]{1,0:T(8,128)(2,1)S(1)}, u32[]{:S(2)}, u32[]{:S(2)}) collective-permute-start(bf16[32,2176]{1,0:T(8,128)(2,1)S(1)} %collective-permute-done.3.part2_ref), channel_id=1, source_target_pairs={{0,1},{1,0},{2,3},{3,2},{4,5},{5,4},{6,7},{7,6},{8,9},{9,8},{10,11... | collective-permute-start | bytes 417800 | tf_op jit(solution)/shard_map/ppermute | solution.py:595
  27.7 31.2 %copy-start.10 = (s32[16]{0:T(128)S(1)}, s32[16]{0:T(128)}, u32[]{:S(2)}) copy-start(s32[16]{0:T(128)} %param.15) | copy-start | bytes 196
  27.7 79.7 %copy-start.5 = (f32[2048]{0:T(1024)S(1)}, f32[2048]{0:T(1024)}, u32[]{:S(2)}) copy-start(f32[2048]{0:T(1024)} %param.9) | copy-start | bytes 24580
  29.1 23.4 %all-to-all-start = ((bf16[8,144,256]{2,1,0:T(8,128)(2,1)}), bf16[8,144,256]{2,1,0:T(8,128)(2,1)}, u32[]{:S(2)}, u32[]{:S(2)}) async-start(bf16[8,144,256]{2,1,0:T(8,128)(2,1)} %get-tuple-element.23), calls=%async_computation | async-start | bytes 1179648 | tf_op jit(solution)/shard_map/all_to_all | solution.py:597
  35.1 4.2 %collective-permute-start.11 = (bf16[128,2048]{1,0:T(8,128)(2,1)S(1)}, bf16[128,2048]{1,0:T(8,128)(2,1)S(1)}, u32[]{:S(2)}, u32[]{:S(2)}) collective-permute-start(bf16[128,2048]{1,0:T(8,128)(2,1)S(1)} %copy-done.1), channel_id=1, source_target_pairs={{8,16},{12,20},{16,8},{20,12},{9,17},{13,21},{17,9},{21,13},{10,18... | collective-permute-start | bytes 1572872 | tf_op jit(solution)/shard_map/ppermute | solution.py:524
  35.8 4.8 %collective-permute-start.15 = (bf16[128,2048]{1,0:T(8,128)(2,1)S(1)}, bf16[128,2048]{1,0:T(8,128)(2,1)}, u32[]{:S(2)}, u32[]{:S(2)}) collective-permute-start(bf16[128,2048]{1,0:T(8,128)(2,1)S(1)} %collective-permute-done.9.rest_2_), channel_id=1, source_target_pairs={{8,16},{12,20},{16,8},{20,12},{9,17},{13,21},{17,9},{21,13},{10,18... | collective-permute-start | bytes 1572872 | tf_op jit(solution)/shard_map/ppermute | solution.py:525
  37.3 57.5 %collective-permute-start.8 = (bf16[128,2048]{1,0:T(8,128)(2,1)S(1)}, bf16[128,2048]{1,0:T(8,128)(2,1)S(1)}, u32[]{:S(2)}, u32[]{:S(2)}) collective-permute-start(bf16[128,2048]{1,0:T(8,128)(2,1)S(1)} %copy-done.1), channel_id=1, source_target_pairs={{0,4},{4,0},{8,12},{12,8},{16,20},{20,16},{24,28},{28,24},{1,5},{5... | collective-permute-start | bytes 1572872 | tf_op jit(solution)/shard_map/ppermute | solution.py:522
  39.3 57.0 %collective-permute-start.12 = (bf16[128,2048]{1,0:T(8,128)(2,1)S(1)}, bf16[128,2048]{1,0:T(8,128)(2,1)S(1)}, u32[]{:S(2)}, u32[]{:S(2)}) collective-permute-start(bf16[128,2048]{1,0:T(8,128)(2,1)S(1)} %collective-permute-done.11.rest_4_), channel_id=1, source_target_pairs={{8,0},{12,4},{16,24},{20,28},{9,1},{13,5},{17,25},{21,29},{10,2},{... | collective-permute-start | bytes 1572872 | tf_op jit(solution)/shard_map/ppermute | solution.py:527
  40.6 59.2 %collective-permute-start.16 = (bf16[128,2048]{1,0:T(8,128)(2,1)}, bf16[128,2048]{1,0:T(8,128)(2,1)}, u32[]{:S(2)}, u32[]{:S(2)}) collective-permute-start(bf16[128,2048]{1,0:T(8,128)(2,1)} %collective-permute-done.15.rest_8_), channel_id=1, source_target_pairs={{8,0},{12,4},{16,24},{20,28},{9,1},{13,5},{17,25},{21,29},{10,2},{... | collective-permute-start | bytes 1572872 | tf_op jit(solution)/shard_map/ppermute | solution.py:528
  59.0 33.0 %collective-permute-start.5 = (f32[2,2048]{1,0:T(2,128)S(1)}, f32[2,2048]{1,0:T(2,128)S(1)}, u32[]{:S(2)}, u32[]{:S(2)}) collective-permute-start(f32[2,2048]{1,0:T(2,128)S(1)} %get-tuple-element.30), channel_id=1, source_target_pairs={{0,8},{4,12},{8,0},{12,4},{16,24},{20,28},{24,16},{28,20},{1,9},{5... | collective-permute-start | bytes 49160 | tf_op jit(solution)/shard_map/ppermute | solution.py:560
  90.3 14.8 %collective-permute-start.10 = (bf16[128,2048]{1,0:T(8,128)(2,1)S(1)}, bf16[128,2048]{1,0:T(8,128)(2,1)S(1)}, u32[]{:S(2)}, u32[]{:S(2)}) collective-permute-start(bf16[128,2048]{1,0:T(8,128)(2,1)S(1)} %collective-permute-done.9.rest_2_), channel_id=1, source_target_pairs={{0,4},{4,0},{8,12},{12,8},{16,20},{20,16},{24,28},{28,24},{1,5},{5... | collective-permute-start | bytes 1572872 | tf_op jit(solution)/shard_map/ppermute | solution.py:526
  92.1 9.2 %collective-permute-start.6 = (f32[2,2048]{1,0:T(2,128)S(1)}, f32[2,2048]{1,0:T(2,128)S(1)}, u32[]{:S(2)}, u32[]{:S(2)}) collective-permute-start(f32[2,2048]{1,0:T(2,128)S(1)} %add.14), channel_id=1, source_target_pairs={{0,16},{4,20},{8,24},{12,28},{16,0},{20,4},{24,8},{28,12},{1,17},{... | collective-permute-start | bytes 49160 | tf_op jit(solution)/shard_map/ppermute | solution.py:560
  94.8 18.3 %collective-permute-start.13 = (bf16[128,2048]{1,0:T(8,128)(2,1)S(1)}, bf16[128,2048]{1,0:T(8,128)(2,1)}, u32[]{:S(2)}, u32[]{:S(2)}) collective-permute-start(bf16[128,2048]{1,0:T(8,128)(2,1)S(1)} %collective-permute-done.11.rest_4_), channel_id=1, source_target_pairs={{8,12},{12,8},{16,20},{20,16},{9,13},{13,9},{17,21},{21,17},{10,14... | collective-permute-start | bytes 1572872 | tf_op jit(solution)/shard_map/ppermute | solution.py:529
  96.2 20.2 %collective-permute-start.14 = (bf16[128,2048]{1,0:T(8,128)(2,1)S(1)}, bf16[128,2048]{1,0:T(8,128)(2,1)}, u32[]{:S(2)}, u32[]{:S(2)}) collective-permute-start(bf16[128,2048]{1,0:T(8,128)(2,1)S(1)} %collective-permute-done.12.rest_5_), channel_id=1, source_target_pairs={{0,4},{4,0},{24,28},{28,24},{1,5},{5,1},{25,29},{29,25},{2,6},{6,2... | collective-permute-start | bytes 1572872 | tf_op jit(solution)/shard_map/ppermute | solution.py:530
  99.8 16.7 %collective-permute-start.17 = (bf16[128,2048]{1,0:T(8,128)(2,1)}, bf16[128,2048]{1,0:T(8,128)(2,1)}, u32[]{:S(2)}, u32[]{:S(2)}) collective-permute-start(bf16[128,2048]{1,0:T(8,128)(2,1)} %collective-permute-done.15.rest_8_), channel_id=1, source_target_pairs={{8,12},{12,8},{16,20},{20,16},{9,13},{13,9},{17,21},{21,17},{10,14... | collective-permute-start | bytes 1572872 | tf_op jit(solution)/shard_map/ppermute | solution.py:531
  101.3 24.8 %collective-permute-start.18 = (bf16[128,2048]{1,0:T(8,128)(2,1)}, bf16[128,2048]{1,0:T(8,128)(2,1)}, u32[]{:S(2)}, u32[]{:S(2)}) collective-permute-start(bf16[128,2048]{1,0:T(8,128)(2,1)} %collective-permute-done.16.rest_9_), channel_id=1, source_target_pairs={{0,4},{4,0},{24,28},{28,24},{1,5},{5,1},{25,29},{29,25},{2,6},{6,2... | collective-permute-start | bytes 1572872 | tf_op jit(solution)/shard_map/ppermute | solution.py:532
  105.9 20.1 %collective-permute-start.7 = (f32[2,2048]{1,0:T(2,128)S(1)}, f32[2,2048]{1,0:T(2,128)S(1)}, u32[]{:S(2)}, u32[]{:S(2)}) collective-permute-start(f32[2,2048]{1,0:T(2,128)S(1)} %add.15.sum_ref), channel_id=1, source_target_pairs={{0,4},{4,0},{8,12},{12,8},{16,20},{20,16},{24,28},{28,24},{1,5},{5... | collective-permute-start | bytes 49160 | tf_op jit(solution)/shard_map/ppermute | solution.py:560
  107.4 18.7 %copy-start.3 = (bf16[128,2048]{1,0:T(8,128)(2,1)S(1)}, bf16[128,2048]{1,0:T(8,128)(2,1)}, u32[]{:S(2)}) copy-start(bf16[128,2048]{1,0:T(8,128)(2,1)} %copy-done.2) | copy-start | bytes 1572868
  (7 other events, 55.5 us)

commit v2 on v1

--- a/solution.py
+++ b/solution.py
@@ -67,10 +67,18 @@
     return pl.BlockSpec(memory_space=pltpu.HBM)
 
 
-def forward_kernel(core_ref, resid_ref, gain_ref, weight_hbm, keep_ref, send_ref, weight_ref, scaled_ref, sems):
+def forward_kernel(
+    core_ref, resid_hbm, gain_hbm, weight_hbm, keep_ref, send_ref, weight_ref, resid_ref, gain_ref, scaled_ref, sems, own_sems
+):
     halves, rows, total = keep_ref.shape
     columns = total - LANES
     core = core_ref[0]
+    own = [
+        pltpu.make_async_copy(resid_hbm, resid_ref, own_sems.at[0]),
+        pltpu.make_async_copy(gain_hbm, gain_ref, own_sems.at[1]),
+    ]
+    for one in own:
+        one.start()
     copy, width = fetch_columns(weight_hbm, weight_ref, sems)
 
     def put(value, cols):
@@ -86,6 +94,8 @@
             def _():
                 send_ref[half, :, cols] = piece
 
+    for one in own:
+        one.wait()
     floated = resid_ref[...].astype(F32)
     scaled_ref[...] = (floated * gain_ref[...]).astype(BF)
     sums = jnp.sum(floated * floated, axis=1, keepdims=True)
@@ -105,12 +115,15 @@
     return pl.pallas_call(
         forward_kernel,
         out_shape=(out, out),
-        in_specs=[smem(), vmem(), vmem(), hbm()],
+        in_specs=[smem(), hbm(), hbm(), hbm()],
         out_specs=(vmem(), vmem()),
         scratch_shapes=[
             pltpu.VMEM(weight.shape, BF),
             pltpu.VMEM((tokens, features), BF),
+            pltpu.VMEM((1, features), F32),
+            pltpu.VMEM((tokens, features), BF),
             pltpu.SemaphoreType.DMA((4,)),
+            pltpu.SemaphoreType.DMA((2,)),
         ],
         compiler_params=params(BIG),
         cost_estimate=cost(2 * tokens * features * columns, 2 * features * columns),
@@ -332,10 +345,10 @@
     )(resid, weight, grad)
 
 
-def balance_kernel(entries, squares_ref, level_ref, along_ref, cols_ref, sums_ref, share_ref, wide_ref):
+def balance_kernel(entries, squares_ref, got_ref, level_ref, along_ref, cols_ref, sums_ref, share_ref, wide_ref):
     objectives = along_ref.shape[0]
     hidden = wide_ref.shape[1] // objectives
-    rms = jnp.sqrt(squares_ref[...] / entries + grad_eps)
+    rms = jnp.sqrt((squares_ref[...] + got_ref[...]) / entries + grad_eps)
     share = level_ref[...].astype(F32) / denominator / rms
     share_ref[...] = share
     row = lax.broadcasted_iota(jnp.int32, (objectives, objectives), 0)
@@ -347,7 +360,7 @@
         wide_ref[:, which * hidden : (which + 1) * hidden] = jnp.broadcast_to(share[:, which : which + 1], (1, hidden))
 
 
-def balance_of(entries, squares, level, along, col_sums):
+def balance_of(entries, squares, got, level, along, col_sums):
     objectives, features = along.shape
     columns = col_sums.shape[1]
     return pl.pallas_call(
@@ -357,12 +370,12 @@
             jax.ShapeDtypeStruct((1, objectives), F32),
             jax.ShapeDtypeStruct((1, columns), F32),
         ),
-        in_specs=[vmem()] * 4,
+        in_specs=[vmem()] * 5,
         out_specs=(vmem(), vmem(), vmem()),
         compiler_params=params(4),
         cost_estimate=cost(4 * along.size, 8 * along.size),
         name="balance",
-    )(squares, level, along, col_sums)
+    )(squares, got, level, along, col_sums)
 
 
 def backward_kernel(total, share_ref, row_ref, resid_ref, gain_ref, prod_hbm, extra_ref, out_ref, prod_ref, scal_ref, sems):
@@ -424,10 +437,10 @@
     )(share, share, resid, gain, prods, grad)
 
 
-def weight_kernel(plan, order_of, depth, place_ref, gain_ref, wide_ref, sum_ref, got_ref, grad_ref, *rest):
+def weight_kernel(plan, order_of, depth, place_ref, gain_ref, wide_ref, grad_ref, *rest):
     count = len(plan)
-    block_refs = rest[:-8]
-    out_hbm, gain_out_ref, bias_out_ref, turned_ref, blocks_ref, result_ref, sems, out_sems = rest[-8:]
+    block_refs = rest[:-6]
+    out_hbm, turned_ref, blocks_ref, result_ref, sems, out_sems = rest[-6:]
     tokens, features = block_refs[0].shape
     columns = grad_ref.shape[2]
     total_tokens = tokens * count
@@ -455,9 +468,6 @@
 
     for k in range(count):
         turned_ref[:, k * tokens : (k + 1) * tokens] = grad_ref[order[k], :tokens, :].T
-    sums = (sum_ref[...] + got_ref[...]) / total_tokens
-    gain_out_ref[...] = sums[0:1]
-    bias_out_ref[...] = sums[1:2] * wide_ref[...]
     start = pl.multiple_of(place_ref[0] * columns, columns)
     scale = wide_ref[:, pl.ds(start, columns)] / total_tokens
 
@@ -481,20 +491,16 @@
         store(step).wait()
 
 
-def weight_grad(place, gain, wide, sums, got, grads, blocks, plan, order_of):
+def weight_grad(place, gain, wide, grads, blocks, plan, order_of):
     tokens, features = blocks[0].shape
     columns = grads.shape[2]
     depth = 512
     count = len(plan)
     return pl.pallas_call(
         functools.partial(weight_kernel, plan, order_of, depth),
-        out_shape=(
-            jax.ShapeDtypeStruct((features, columns), F32),
-            jax.ShapeDtypeStruct((1, features), F32),
-            jax.ShapeDtypeStruct(wide.shape, F32),
-        ),
-        in_specs=[smem()] + [vmem()] * 5 + [hbm()] * len(blocks),
-        out_specs=(hbm(), vmem(), vmem()),
+        out_shape=jax.ShapeDtypeStruct((features, columns), F32),
+        in_specs=[smem()] + [vmem()] * 3 + [hbm()] * len(blocks),
+        out_specs=hbm(),
         scratch_shapes=[
             pltpu.VMEM((columns, tokens * count), BF),
             pltpu.VMEM((tokens * count, features), BF),
@@ -505,7 +511,25 @@
         compiler_params=params(BIG),
         cost_estimate=cost(2 * tokens * count * features * columns, 8 * features * columns),
         name="weights",
-    )(place, gain, wide, sums, got, grads, *blocks)
+    )(place, gain, wide, grads, *blocks)
+
+
+def finish_kernel(total_tokens, sum_ref, got_ref, wide_ref, gain_ref, bias_ref):
+    sums = (sum_ref[...] + got_ref[...]) / total_tokens
+    gain_ref[...] = sums[0:1]
+    bias_ref[...] = sums[1:2] * wide_ref[...]
+
+
+def finish(total_tokens, sums, got, wide):
+    return pl.pallas_call(
+        functools.partial(finish_kernel, total_tokens),
+        out_shape=(jax.ShapeDtypeStruct((1, sums.shape[1]), F32), jax.ShapeDtypeStruct(wide.shape, F32)),
+        in_specs=[vmem()] * 3,
+        out_specs=(vmem(), vmem()),
+        compiler_params=params(4),
+        cost_estimate=cost(4 * sums.size, 16 * sums.size),
+        name="finish",
+    )(sums, got, wide)
 
 
 def gather_blocks(resid):
@@ -575,7 +599,8 @@
     across = [(i, i ^ 2) for i in range(4)]
 
     blocks, plan, order_of = gather_blocks(resid)
-    keep, send = forward((me % 2)[None], resid, gain, head_in)
+    held = [pltpu.with_memory_space_constraint(one, pltpu.HBM) for one in (resid, gain, head_in)]
+    keep, send = forward((me % 2)[None], *held)
     recv = lax.ppermute(send, "tp", partner)
     mine, send = merge((me // 2)[None], keep, recv)
     recv = lax.ppermute(send, "tp", across)
@@ -597,14 +622,16 @@
     grads = lax.all_to_all(message, "tok", 0, 0)
     prods, along = products(resid, head_in, grad, objectives)
     squares = jnp.sum(grads[:, tokens : tokens + 3, :objectives].astype(F32), axis=(0, 1))
-    squares = lax.psum(squares, "tp")[None, :]
+    squares = squares[None, :]
+    got = lax.ppermute(squares, "tp", partner)
+    squares = squares + got
+    got = lax.ppermute(squares, "tp", across)
     entries = total_tokens * total_features
-    sums, share, wide = balance_of(entries, squares, obj_weight[None, :], along, col_sums)
+    sums, share, wide = balance_of(entries, squares, got, obj_weight[None, :], along, col_sums)
     sums, got = total_over_tok(sums)
     resid_grad = backward(total_features, resid, gain, prods, grad, share)
-    head_in_grad, gain_grad, head_bias_grad = weight_grad(
-        place[None], gain, wide, sums, got, grads, blocks, plan, order_of
-    )
+    head_in_grad = weight_grad(place[None], gain, wide, grads, blocks, plan, order_of)
+    gain_grad, head_bias_grad = finish(total_tokens, sums, got, wide)
     return (resid_grad, gain_grad[0], head_in_grad, head_bias_grad[0])
 
 

time: 133 us -> 135 us (1.015)
  waiting for transfers between devices: 26.4 us -> 44.3 us
  starting transfers between devices: 65.2 us -> 56.6 us
  blocking collectives: 5.66 us -> 0 us
  local copies, waits for them, and re-layouts: 2.56 us -> 0.03 us
  Pallas kernels: 30.7 us -> 32.1 us
    ppermute x1, waiting for transfers between devices: 0.01 us -> 8.14 us  [gather_blocks(): x3e = lax.ppermute(f2, 'tok', cross((0, 3)))]
    ppermute x3, starting transfers between devices: 35.5 us -> 27.6 us  [total_over_tok(): got = lax.ppermute(value, 'tok', [(i, i ^ flip) for i in range(count)])]
    ppermute x1, waiting for transfers between devices: 3.38 us -> 10.5 us  [gather_blocks(): x2e = lax.ppermute(f1, 'tok', cross((0, 3)))]
    all_to_all x1, waiting for transfers between devices: 4.24 us -> 10.1 us  [fast_device(): grads = lax.all_to_all(message, 'tok', 0, 0)]
    psum x1 -> x0, blocking collectives: 5.66 us -> none  [fast_device(): squares = lax.psum(squares, 'tp')[None, :]]
    ppermute x3, waiting for transfers between devices: 9.85 us -> 4.47 us  [total_over_tok(): got = lax.ppermute(value, 'tok', [(i, i ^ flip) for i in range(count)])]
    unnamed x22 -> x14, local copies, waits for them, and re-layouts: 2.56 us -> 0.03 us
    pallas_call x1 -> x2, Pallas kernels: 4.2 us -> 6.18 us  [the longest x1 5.57 us: forward(): pl.pallas_call(forward_kernel, out_shape=(out, out), in_specs=[smem(), hb...]
  transfers between devices with their start and end apart: 20 -> 22, of which waited for: 8 -> 10; matrix products, arithmetic and copies ran while one was open for 1% -> 1% of each run, Pallas kernels for 15% -> 14%
where the time goes in v2:
time: 135 us
  starting transfers between devices  56.6 us (42%)
  waiting for transfers between devices  44.3 us (33%)
  Pallas kernels  32.1 us (24%)
    ppermute x3, starting transfers between devices, total_over_tok(): got = lax.ppermute(value, 'tok', [(i, i ^ flip) for i in range(count)])  27.6 us
    ppermute x1, waiting for transfers between devices, gather_blocks(): x2e = lax.ppermute(f1, 'tok', cross((0, 3)))  10.5 us
    all_to_all x1, waiting for transfers between devices, fast_device(): grads = lax.all_to_all(message, 'tok', 0, 0)  10.1 us
    ppermute x1, waiting for transfers between devices, gather_blocks(): x3e = lax.ppermute(f2, 'tok', cross((0, 3)))  8.14 us
    pallas_call x1, Pallas kernels, products(): pl.pallas_call(products_kernel, out_shape=(jax.ShapeDtypeStruct(shape, BF...  6.31 us
    pallas_call x1, Pallas kernels, backward(): pl.pallas_call(functools.partial(backward_kernel, total), out_shape=jax.S...  5.69 us
    pallas_call x1, Pallas kernels, weight_grad(): pl.pallas_call(functools.partial(weight_kernel, plan, order_of, depth), o...  5.62 us
    pallas_call x1, Pallas kernels, forward(): pl.pallas_call(forward_kernel, out_shape=(out, out), in_specs=[smem(), hb...  5.57 us
  transfers between devices with their start and end apart: 22, of which 10 were waited for; matrix products, arithmetic and copies ran while one was open for 1% of the time, Pallas kernels for 14%

profile of v2, /device:TPU:0, one launch (start us, length us, event | category | flops | bytes accessed | tf_op | source)
XLA Modules:
  0.0 134.7 jit_solution(9429379783149175531)
XLA Ops:
  0.7 5.6 %forward.1 = (f32[2,32,2176]{2,1,0:T(8,128)S(1)}, f32[2,32,2176]{2,1,0:T(8,128)S(1)}) custom-call(s32[1]{0:T(128)} %bitcast.2.core_ref, bf16[128,2048]{1,0:T(8,128)(2,1)} %rest_0_.1, f32[1,2048]{1,0:T(1,128)} %bitcast.14, bf16[2048,2048]{1,0:T(8,128)(2,1)} %weight_hbm.5), custom_call_target="tpu_custom_call" | custom-call | flops 1073741824 | bytes 8388608 | tf_op jit(solution)/shard_map/forward/pallas_call | solution.py:115
  6.8 1.6 %collective-permute-done.recv_ref = f32[2,32,2176]{2,1,0:T(8,128)S(1)} collective-permute-done((f32[2,32,2176]{2,1,0:T(8,128)S(1)}, f32[2,32,2176]{2,1,0:T(8,128)S(1)}, u32[]{:S(2)}, u32[]{:S(2)}) %collective-permute-start) | collective-permute-done | bytes 557088 | tf_op jit(solution)/shard_map/ppermute | solution.py:604
  8.5 2.9 %collective-permute-start.1 = (bf16[32,2176]{1,0:T(8,128)(2,1)S(1)}, bf16[32,2176]{1,0:T(8,128)(2,1)S(1)}, u32[]{:S(2)}, u32[]{:S(2)}) collective-permute-start(bf16[32,2176]{1,0:T(8,128)(2,1)S(1)} %get-tuple-element.21), channel_id=1, source_target_pairs={{0,2},{1,3},{2,0},{3,1},{4,6},{5,7},{6,4},{7,5},{8,10},{9,11},{10,... | collective-permute-start | bytes 417800 | tf_op jit(solution)/shard_map/ppermute | solution.py:606
  11.4 4.0 %collective-permute-done.1.recv_ref = bf16[32,2176]{1,0:T(8,128)(2,1)S(1)} collective-permute-done((bf16[32,2176]{1,0:T(8,128)(2,1)S(1)}, bf16[32,2176]{1,0:T(8,128)(2,1)S(1)}, u32[]{:S(2)}, u32[]{:S(2)}) %collective-permute-start.1) | collective-permute-done | bytes 139296 | tf_op jit(solution)/shard_map/ppermute | solution.py:606
  15.4 2.0 %heads.1.part0_ref = bf16[32,2176]{1,0:T(8,128)(2,1)S(1)} custom-call(s32[1]{0:T(128)} %bitcast.me_ref.spot_ref, f32[32,2176]{1,0:T(8,128)S(1)} %get-tuple-element.20.mine_ref, bf16[32,2176]{1,0:T(8,128)(2,1)S(1)} %collective-permute-done.1.recv_ref, f32[1,2048]{1,0:T(1,128)S(1)} %bitcast.17, f32[1,2048]{1,0:T(1,128)S(1)} %bitcast.18, ...), custom_call_target="tpu_custom_call" | custom-call | flops 2088960 | bytes 557056 | tf_op jit(solution)/shard_map/heads/pallas_call | solution.py:203
  17.4 1.8 %collective-permute-start.3 = (bf16[32,2176]{1,0:T(8,128)(2,1)S(1)}, bf16[32,2176]{1,0:T(8,128)(2,1)S(1)}, u32[]{:S(2)}, u32[]{:S(2)}) collective-permute-start(bf16[32,2176]{1,0:T(8,128)(2,1)S(1)} %heads.1.part0_ref), channel_id=1, source_target_pairs={{0,2},{1,3},{2,0},{3,1},{4,6},{5,7},{6,4},{7,5},{8,10},{9,11},{10,... | collective-permute-start | bytes 417800 | tf_op jit(solution)/shard_map/ppermute | solution.py:619
  19.2 3.4 %collective-permute-done.3.part2_ref = bf16[32,2176]{1,0:T(8,128)(2,1)S(1)} collective-permute-done((bf16[32,2176]{1,0:T(8,128)(2,1)S(1)}, bf16[32,2176]{1,0:T(8,128)(2,1)S(1)}, u32[]{:S(2)}, u32[]{:S(2)}) %collective-permute-start.3) | collective-permute-done | bytes 139296 | tf_op jit(solution)/shard_map/ppermute | solution.py:619
  22.6 1.7 %collective-permute-start.11 = (bf16[128,2048]{1,0:T(8,128)(2,1)S(1)}, bf16[128,2048]{1,0:T(8,128)(2,1)S(1)}, u32[]{:S(2)}, u32[]{:S(2)}) collective-permute-start(bf16[128,2048]{1,0:T(8,128)(2,1)S(1)} %copy-done), channel_id=1, source_target_pairs={{0,8},{4,12},{8,0},{12,4},{16,24},{20,28},{24,16},{28,20},{1,9},{5... | collective-permute-start | bytes 1572872 | tf_op jit(solution)/shard_map/ppermute | solution.py:547
  24.3 4.8 %gram.1.gram_ref = f32[16,128,128]{2,1,0:T(8,128)S(1)} custom-call(bf16[2048,2048]{1,0:T(8,128)(2,1)} %weight_hbm.5), custom_call_target="tpu_custom_call" | custom-call | flops 1073741824 | bytes 8388608 | tf_op jit(solution)/shard_map/gram/pallas_call | solution.py:235
  30.6 4.8 %all-to-all-start = ((bf16[8,144,256]{2,1,0:T(8,128)(2,1)}), bf16[8,144,256]{2,1,0:T(8,128)(2,1)}, u32[]{:S(2)}, u32[]{:S(2)}) async-start(bf16[8,144,256]{2,1,0:T(8,128)(2,1)} %get-tuple-element.22), calls=%async_computation | async-start | bytes 1179648 | tf_op jit(solution)/shard_map/all_to_all | solution.py:622
  38.4 1.6 %collective-permute-start.10 = (bf16[128,2048]{1,0:T(8,128)(2,1)S(1)}, bf16[128,2048]{1,0:T(8,128)(2,1)S(1)}, u32[]{:S(2)}, u32[]{:S(2)}) collective-permute-start(bf16[128,2048]{1,0:T(8,128)(2,1)S(1)} %copy-done), channel_id=1, source_target_pairs={{0,4},{4,0},{8,12},{12,8},{16,20},{20,16},{24,28},{28,24},{1,5},{5... | collective-permute-start | bytes 1572872 | tf_op jit(solution)/shard_map/ppermute | solution.py:546
  42.6 10.1 %all-to-all-done.grad_ref = bf16[8,144,256]{2,1,0:T(8,128)(2,1)} async-done(((bf16[8,144,256]{2,1,0:T(8,128)(2,1)}), bf16[8,144,256]{2,1,0:T(8,128)(2,1)}, u32[]{:S(2)}, u32[]{:S(2)}) %all-to-all-start) | async-done | bytes 589856 | tf_op jit(solution)/shard_map/all_to_all | solution.py:622
  56.2 6.3 %products.1 = (bf16[16,128,2048]{2,1,0:T(8,128)(2,1)}, f32[16,2048]{1,0:T(8,128)S(1)}) custom-call(bf16[128,2048]{1,0:T(8,128)(2,1)S(1)} %copy-done, bf16[2048,2048]{1,0:T(8,128)(2,1)} %weight_hbm.5, bf16[128,2176]{1,0:T(8,128)(2,1)S(1)} %get-tuple-element.23.grad_ref.extra_ref), custom_call_target="tpu_custom_call" | custom-call | flops 1073741824 | bytes 16777216 | tf_op jit(solution)/shard_map/products/pallas_call | solution.py:330
  62.7 24.2 %collective-permute-start.7 = (f32[2,2048]{1,0:T(2,128)S(1)}, f32[2,2048]{1,0:T(2,128)S(1)}, u32[]{:S(2)}, u32[]{:S(2)}) collective-permute-start(f32[2,2048]{1,0:T(2,128)S(1)} %get-tuple-element.28), channel_id=1, source_target_pairs={{0,8},{4,12},{8,0},{12,4},{16,24},{20,28},{24,16},{28,20},{1,9},{5... | collective-permute-start | bytes 49160 | tf_op jit(solution)/shard_map/ppermute | solution.py:584
  86.8 1.7 %collective-permute-done.7 = f32[2,2048]{1,0:T(2,128)S(1)} collective-permute-done((f32[2,2048]{1,0:T(2,128)S(1)}, f32[2,2048]{1,0:T(2,128)S(1)}, u32[]{:S(2)}, u32[]{:S(2)}) %collective-permute-start.7) | collective-permute-done | bytes 16416 | tf_op jit(solution)/shard_map/ppermute | solution.py:584
  88.5 2.0 %collective-permute-start.8 = (f32[2,2048]{1,0:T(2,128)S(1)}, f32[2,2048]{1,0:T(2,128)S(1)}, u32[]{:S(2)}, u32[]{:S(2)}) collective-permute-start(f32[2,2048]{1,0:T(2,128)S(1)} %add.16), channel_id=1, source_target_pairs={{0,16},{4,20},{8,24},{12,28},{16,0},{20,4},{24,8},{28,12},{1,17},{... | collective-permute-start | bytes 49160 | tf_op jit(solution)/shard_map/ppermute | solution.py:584
  90.5 2.7 %collective-permute-done.8 = f32[2,2048]{1,0:T(2,128)S(1)} collective-permute-done((f32[2,2048]{1,0:T(2,128)S(1)}, f32[2,2048]{1,0:T(2,128)S(1)}, u32[]{:S(2)}, u32[]{:S(2)}) %collective-permute-start.8) | collective-permute-done | bytes 16416 | tf_op jit(solution)/shard_map/ppermute | solution.py:584
  93.3 1.5 %collective-permute-start.9 = (f32[2,2048]{1,0:T(2,128)S(1)}, f32[2,2048]{1,0:T(2,128)S(1)}, u32[]{:S(2)}, u32[]{:S(2)}) collective-permute-start(f32[2,2048]{1,0:T(2,128)S(1)} %add.17.sum_ref), channel_id=1, source_target_pairs={{0,4},{4,0},{8,12},{12,8},{16,20},{20,16},{24,28},{28,24},{1,5},{5... | collective-permute-start | bytes 49160 | tf_op jit(solution)/shard_map/ppermute | solution.py:584
  98.3 3.4 %collective-permute-start.16 = (bf16[128,2048]{1,0:T(8,128)(2,1)S(1)}, bf16[128,2048]{1,0:T(8,128)(2,1)}, u32[]{:S(2)}, u32[]{:S(2)}) collective-permute-start(bf16[128,2048]{1,0:T(8,128)(2,1)S(1)} %collective-permute-done.14.rest_5_), channel_id=1, source_target_pairs={{0,4},{4,0},{24,28},{28,24},{1,5},{5,1},{25,29},{29,25},{2,6},{6,2... | collective-permute-start | bytes 1572872 | tf_op jit(solution)/shard_map/ppermute | solution.py:554
  101.7 2.5 %collective-permute-start.20 = (bf16[128,2048]{1,0:T(8,128)(2,1)}, bf16[128,2048]{1,0:T(8,128)(2,1)}, u32[]{:S(2)}, u32[]{:S(2)}) collective-permute-start(bf16[128,2048]{1,0:T(8,128)(2,1)} %collective-permute-done.18.rest_9_), channel_id=1, source_target_pairs={{0,4},{4,0},{24,28},{28,24},{1,5},{5,1},{25,29},{29,25},{2,6},{6,2... | collective-permute-start | bytes 1572872 | tf_op jit(solution)/shard_map/ppermute | solution.py:556
  104.2 5.7 %backward.1 = bf16[128,2048]{1,0:T(8,128)(2,1)} custom-call(f32[1,16]{1,0:T(1,128)S(1)} %get-tuple-element.26.share_ref.row_ref, f32[1,16]{1,0:T(1,128)S(1)} %get-tuple-element.26.share_ref.row_ref, bf16[128,2048]{1,0:T(8,128)(2,1)S(1)} %copy-done, f32[1,2048]{1,0:T(1,128)S(1)} %bitcast.15, bf16[16,128,2048]{2,1,0:T(8,128)(2,1)} %get-tuple-element.27.prod_hbm, ...), custom_call_target="tpu_custom_call" | custom-call | flops 8388608 | bytes 8388608 | tf_op jit(solution)/shard_map/backward/pallas_call | solution.py:416
  110.5 10.5 %collective-permute-done.16.rest_7_ = bf16[128,2048]{1,0:T(8,128)(2,1)} collective-permute-done((bf16[128,2048]{1,0:T(8,128)(2,1)S(1)}, bf16[128,2048]{1,0:T(8,128)(2,1)}, u32[]{:S(2)}, u32[]{:S(2)}) %collective-permute-start.16) | collective-permute-done | bytes 524320 | tf_op jit(solution)/shard_map/ppermute | solution.py:554
  120.9 8.1 %collective-permute-done.20.rest_11_ = bf16[128,2048]{1,0:T(8,128)(2,1)} collective-permute-done((bf16[128,2048]{1,0:T(8,128)(2,1)}, bf16[128,2048]{1,0:T(8,128)(2,1)}, u32[]{:S(2)}, u32[]{:S(2)}) %collective-permute-start.20) | collective-permute-done | bytes 524320 | tf_op jit(solution)/shard_map/ppermute | solution.py:556
  129.1 5.6 %weights.1 = f32[2048,256]{1,0:T(8,128)} custom-call(s32[1]{0:T(128)} %bitcast.11.place_ref, f32[1,2048]{1,0:T(1,128)S(1)} %bitcast.16, f32[1,2048]{1,0:T(1,128)S(1)} %get-tuple-element.29.wide_ref, bf16[8,144,256]{2,1,0:T(8,128)(2,1)} %all-to-all-done.grad_ref, bf16[128,2048]{1,0:T(8,128)(2,1)S(1)} %copy-done, ...), custom_call_target="tpu_custom_call" | custom-call | flops 1073741824 | bytes 4194304 | tf_op jit(solution)/shard_map/weights/pallas_call | solution.py:499
  (48 shorter events, 15.3 us)
Async XLA Ops:
  6.3 2.2 %collective-permute-start = (f32[2,32,2176]{2,1,0:T(8,128)S(1)}, f32[2,32,2176]{2,1,0:T(8,128)S(1)}, u32[]{:S(2)}, u32[]{:S(2)}) collective-permute-start(f32[2,32,2176]{2,1,0:T(8,128)S(1)} %get-tuple-element.19), channel_id=1, source_target_pairs={{0,1},{1,0},{2,3},{3,2},{4,5},{5,4},{6,7},{7,6},{8,9},{9,8},{10,11... | collective-permute-start | bytes 1671176 | tf_op jit(solution)/shard_map/ppermute | solution.py:604
  8.5 6.9 %collective-permute-start.1 = (bf16[32,2176]{1,0:T(8,128)(2,1)S(1)}, bf16[32,2176]{1,0:T(8,128)(2,1)S(1)}, u32[]{:S(2)}, u32[]{:S(2)}) collective-permute-start(bf16[32,2176]{1,0:T(8,128)(2,1)S(1)} %get-tuple-element.21), channel_id=1, source_target_pairs={{0,2},{1,3},{2,0},{3,1},{4,6},{5,7},{6,4},{7,5},{8,10},{9,11},{10,... | collective-permute-start | bytes 417800 | tf_op jit(solution)/shard_map/ppermute | solution.py:606
  17.4 5.2 %collective-permute-start.3 = (bf16[32,2176]{1,0:T(8,128)(2,1)S(1)}, bf16[32,2176]{1,0:T(8,128)(2,1)S(1)}, u32[]{:S(2)}, u32[]{:S(2)}) collective-permute-start(bf16[32,2176]{1,0:T(8,128)(2,1)S(1)} %heads.1.part0_ref), channel_id=1, source_target_pairs={{0,2},{1,3},{2,0},{3,1},{4,6},{5,7},{6,4},{7,5},{8,10},{9,11},{10,... | collective-permute-start | bytes 417800 | tf_op jit(solution)/shard_map/ppermute | solution.py:619
  19.2 10.0 %collective-permute-start.2 = (bf16[32,2176]{1,0:T(8,128)(2,1)S(1)}, bf16[32,2176]{1,0:T(8,128)(2,1)S(1)}, u32[]{:S(2)}, u32[]{:S(2)}) collective-permute-start(bf16[32,2176]{1,0:T(8,128)(2,1)S(1)} %heads.1.part0_ref), channel_id=1, source_target_pairs={{0,1},{1,0},{2,3},{3,2},{4,5},{5,4},{6,7},{7,6},{8,9},{9,8},{10,11... | collective-permute-start | bytes 417800 | tf_op jit(solution)/shard_map/ppermute | solution.py:618
  22.6 6.6 %collective-permute-start.4 = (bf16[32,2176]{1,0:T(8,128)(2,1)S(1)}, bf16[32,2176]{1,0:T(8,128)(2,1)S(1)}, u32[]{:S(2)}, u32[]{:S(2)}) collective-permute-start(bf16[32,2176]{1,0:T(8,128)(2,1)S(1)} %collective-permute-done.3.part2_ref), channel_id=1, source_target_pairs={{0,1},{1,0},{2,3},{3,2},{4,5},{5,4},{6,7},{7,6},{8,9},{9,8},{10,11... | collective-permute-start | bytes 417800 | tf_op jit(solution)/shard_map/ppermute | solution.py:620
  22.6 14.3 %collective-permute-start.11 = (bf16[128,2048]{1,0:T(8,128)(2,1)S(1)}, bf16[128,2048]{1,0:T(8,128)(2,1)S(1)}, u32[]{:S(2)}, u32[]{:S(2)}) collective-permute-start(bf16[128,2048]{1,0:T(8,128)(2,1)S(1)} %copy-done), channel_id=1, source_target_pairs={{0,8},{4,12},{8,0},{12,4},{16,24},{20,28},{24,16},{28,20},{1,9},{5... | collective-permute-start | bytes 1572872 | tf_op jit(solution)/shard_map/ppermute | solution.py:547
  29.1 33.4 %copy-start.6 = (s32[16]{0:T(128)S(1)}, s32[16]{0:T(128)}, u32[]{:S(2)}) copy-start(s32[16]{0:T(128)} %param.15) | copy-start | bytes 196
  29.1 75.0 %copy-start.1 = (f32[2048]{0:T(1024)S(1)}, f32[2048]{0:T(1024)}, u32[]{:S(2)}) copy-start(f32[2048]{0:T(1024)} %param.9) | copy-start | bytes 24580
  30.6 22.2 %all-to-all-start = ((bf16[8,144,256]{2,1,0:T(8,128)(2,1)}), bf16[8,144,256]{2,1,0:T(8,128)(2,1)}, u32[]{:S(2)}, u32[]{:S(2)}) async-start(bf16[8,144,256]{2,1,0:T(8,128)(2,1)} %get-tuple-element.22), calls=%async_computation | async-start | bytes 1179648 | tf_op jit(solution)/shard_map/all_to_all | solution.py:622
  35.3 4.7 %collective-permute-start.13 = (bf16[128,2048]{1,0:T(8,128)(2,1)S(1)}, bf16[128,2048]{1,0:T(8,128)(2,1)S(1)}, u32[]{:S(2)}, u32[]{:S(2)}) collective-permute-start(bf16[128,2048]{1,0:T(8,128)(2,1)S(1)} %copy-done), channel_id=1, source_target_pairs={{8,16},{12,20},{16,8},{20,12},{9,17},{13,21},{17,9},{21,13},{10,18... | collective-permute-start | bytes 1572872 | tf_op jit(solution)/shard_map/ppermute | solution.py:548
  36.9 4.4 %collective-permute-start.17 = (bf16[128,2048]{1,0:T(8,128)(2,1)S(1)}, bf16[128,2048]{1,0:T(8,128)(2,1)}, u32[]{:S(2)}, u32[]{:S(2)}) collective-permute-start(bf16[128,2048]{1,0:T(8,128)(2,1)S(1)} %collective-permute-done.11.rest_2_), channel_id=1, source_target_pairs={{8,16},{12,20},{16,8},{20,12},{9,17},{13,21},{17,9},{21,13},{10,18... | collective-permute-start | bytes 1572872 | tf_op jit(solution)/shard_map/ppermute | solution.py:549
  38.4 57.0 %collective-permute-start.10 = (bf16[128,2048]{1,0:T(8,128)(2,1)S(1)}, bf16[128,2048]{1,0:T(8,128)(2,1)S(1)}, u32[]{:S(2)}, u32[]{:S(2)}) collective-permute-start(bf16[128,2048]{1,0:T(8,128)(2,1)S(1)} %copy-done), channel_id=1, source_target_pairs={{0,4},{4,0},{8,12},{12,8},{16,20},{20,16},{24,28},{28,24},{1,5},{5... | collective-permute-start | bytes 1572872 | tf_op jit(solution)/shard_map/ppermute | solution.py:546
  40.0 56.8 %collective-permute-start.14 = (bf16[128,2048]{1,0:T(8,128)(2,1)S(1)}, bf16[128,2048]{1,0:T(8,128)(2,1)S(1)}, u32[]{:S(2)}, u32[]{:S(2)}) collective-permute-start(bf16[128,2048]{1,0:T(8,128)(2,1)S(1)} %collective-permute-done.13.rest_4_), channel_id=1, source_target_pairs={{8,0},{12,4},{16,24},{20,28},{9,1},{13,5},{17,25},{21,29},{10,2},{... | collective-permute-start | bytes 1572872 | tf_op jit(solution)/shard_map/ppermute | solution.py:551
  41.3 57.0 %collective-permute-start.18 = (bf16[128,2048]{1,0:T(8,128)(2,1)}, bf16[128,2048]{1,0:T(8,128)(2,1)}, u32[]{:S(2)}, u32[]{:S(2)}) collective-permute-start(bf16[128,2048]{1,0:T(8,128)(2,1)} %collective-permute-done.17.rest_8_), channel_id=1, source_target_pairs={{8,0},{12,4},{16,24},{20,28},{9,1},{13,5},{17,25},{21,29},{10,2},{... | collective-permute-start | bytes 1572872 | tf_op jit(solution)/shard_map/ppermute | solution.py:552
  53.5 1.2 collective-permute-start.5
  54.7 7.8 %collective-permute-start.6 = (f32[1,16]{1,0:T(1,128)S(1)}, f32[1,16]{1,0:T(1,128)S(1)}, u32[]{:S(2)}, u32[]{:S(2)}) collective-permute-start(f32[1,16]{1,0:T(1,128)S(1)} %bitcast_add_fusion.squares_ref), channel_id=1, source_target_pairs={{0,2},{1,3},{2,0},{3,1},{4,6},{5,7},{6,4},{7,5},{8,10},{9,11},{10,... | collective-permute-start | bytes 200 | tf_op jit(solution)/shard_map/ppermute | solution.py:628
  62.7 25.9 %collective-permute-start.7 = (f32[2,2048]{1,0:T(2,128)S(1)}, f32[2,2048]{1,0:T(2,128)S(1)}, u32[]{:S(2)}, u32[]{:S(2)}) collective-permute-start(f32[2,2048]{1,0:T(2,128)S(1)} %get-tuple-element.28), channel_id=1, source_target_pairs={{0,8},{4,12},{8,0},{12,4},{16,24},{20,28},{24,16},{28,20},{1,9},{5... | collective-permute-start | bytes 49160 | tf_op jit(solution)/shard_map/ppermute | solution.py:584
  88.5 4.7 %collective-permute-start.8 = (f32[2,2048]{1,0:T(2,128)S(1)}, f32[2,2048]{1,0:T(2,128)S(1)}, u32[]{:S(2)}, u32[]{:S(2)}) collective-permute-start(f32[2,2048]{1,0:T(2,128)S(1)} %add.16), channel_id=1, source_target_pairs={{0,16},{4,20},{8,24},{12,28},{16,0},{20,4},{24,8},{28,12},{1,17},{... | collective-permute-start | bytes 49160 | tf_op jit(solution)/shard_map/ppermute | solution.py:584
  93.3 8.4 %collective-permute-start.9 = (f32[2,2048]{1,0:T(2,128)S(1)}, f32[2,2048]{1,0:T(2,128)S(1)}, u32[]{:S(2)}, u32[]{:S(2)}) collective-permute-start(f32[2,2048]{1,0:T(2,128)S(1)} %add.17.sum_ref), channel_id=1, source_target_pairs={{0,4},{4,0},{8,12},{12,8},{16,20},{20,16},{24,28},{28,24},{1,5},{5... | collective-permute-start | bytes 49160 | tf_op jit(solution)/shard_map/ppermute | solution.py:584
  94.8 15.7 %collective-permute-start.12 = (bf16[128,2048]{1,0:T(8,128)(2,1)S(1)}, bf16[128,2048]{1,0:T(8,128)(2,1)}, u32[]{:S(2)}, u32[]{:S(2)}) collective-permute-start(bf16[128,2048]{1,0:T(8,128)(2,1)S(1)} %collective-permute-done.11.rest_2_), channel_id=1, source_target_pairs={{0,4},{4,0},{8,12},{12,8},{16,20},{20,16},{24,28},{28,24},{1,5},{5... | collective-permute-start | bytes 1572872 | tf_op jit(solution)/shard_map/ppermute | solution.py:550
  95.4 15.1 %collective-permute-start.15 = (bf16[128,2048]{1,0:T(8,128)(2,1)S(1)}, bf16[128,2048]{1,0:T(8,128)(2,1)}, u32[]{:S(2)}, u32[]{:S(2)}) collective-permute-start(bf16[128,2048]{1,0:T(8,128)(2,1)S(1)} %collective-permute-done.13.rest_4_), channel_id=1, source_target_pairs={{8,12},{12,8},{16,20},{20,16},{9,13},{13,9},{17,21},{21,17},{10,14... | collective-permute-start | bytes 1572872 | tf_op jit(solution)/shard_map/ppermute | solution.py:553
  96.8 24.1 %collective-permute-start.19 = (bf16[128,2048]{1,0:T(8,128)(2,1)}, bf16[128,2048]{1,0:T(8,128)(2,1)}, u32[]{:S(2)}, u32[]{:S(2)}) collective-permute-start(bf16[128,2048]{1,0:T(8,128)(2,1)} %collective-permute-done.17.rest_8_), channel_id=1, source_target_pairs={{8,12},{12,8},{16,20},{20,16},{9,13},{13,9},{17,21},{21,17},{10,14... | collective-permute-start | bytes 1572872 | tf_op jit(solution)/shard_map/ppermute | solution.py:555
  98.3 22.7 %collective-permute-start.16 = (bf16[128,2048]{1,0:T(8,128)(2,1)S(1)}, bf16[128,2048]{1,0:T(8,128)(2,1)}, u32[]{:S(2)}, u32[]{:S(2)}) collective-permute-start(bf16[128,2048]{1,0:T(8,128)(2,1)S(1)} %collective-permute-done.14.rest_5_), channel_id=1, source_target_pairs={{0,4},{4,0},{24,28},{28,24},{1,5},{5,1},{25,29},{29,25},{2,6},{6,2... | collective-permute-start | bytes 1572872 | tf_op jit(solution)/shard_map/ppermute | solution.py:554
  101.7 27.4 %collective-permute-start.20 = (bf16[128,2048]{1,0:T(8,128)(2,1)}, bf16[128,2048]{1,0:T(8,128)(2,1)}, u32[]{:S(2)}, u32[]{:S(2)}) collective-permute-start(bf16[128,2048]{1,0:T(8,128)(2,1)} %collective-permute-done.18.rest_9_), channel_id=1, source_target_pairs={{0,4},{4,0},{24,28},{28,24},{1,5},{5,1},{25,29},{29,25},{2,6},{6,2... | collective-permute-start | bytes 1572872 | tf_op jit(solution)/shard_map/ppermute | solution.py:556
  (5 other events, 80.9 us)

commit v3 on v2

--- a/solution.py
+++ b/solution.py
@@ -250,10 +250,10 @@
     tokens = grad_ref.shape[0]
     columns = objectives * hidden
     share = tokens // 4
+    half = tokens // 2
     for flip, part_ref in enumerate((part0_ref, part1_ref, part2_ref, part3_ref)):
         start = pl.multiple_of((spot_ref[0] ^ flip) * share, share)
         grad_ref[pl.ds(start, share), :] = part_ref[...]
-    inverse, _ = scales(grad_ref[:, columns:], objectives)
     lane = lax.broadcasted_iota(jnp.int32, (1, width), 1)
     squares = jnp.zeros((1, width), F32)
     for which in range(objectives):
@@ -264,14 +264,18 @@
     for peer in range(peers):
         piece = grad_ref[:, peer * width : (peer + 1) * width].astype(F32)
         sums_ref[:, peer * width : (peer + 1) * width] = jnp.sum(piece, axis=0, keepdims=True)
-        msg_ref[peer, :tokens, :] = (piece * inverse).astype(BF)
+    mine = pl.ds(pl.multiple_of(lax.rem(spot_ref[0], 2) * half, half), half)
+    inverse, _ = scales(grad_ref[mine, columns:], objectives)
+    for peer in range(peers):
+        piece = grad_ref[mine, peer * width : (peer + 1) * width].astype(F32)
+        msg_ref[peer, :half, :] = (piece * inverse).astype(BF)
     high = squares.astype(BF).astype(F32)
     rest = squares - high
     middle = rest.astype(BF).astype(F32)
-    row = lax.broadcasted_iota(jnp.int32, (rows - tokens, width), 0)
+    row = lax.broadcasted_iota(jnp.int32, (rows - half, width), 0)
     tail = jnp.where(row == 0, high, jnp.where(row == 1, middle, jnp.where(row == 2, rest - middle, 0.0)))
     for peer in range(peers):
-        msg_ref[peer, tokens:, :] = tail.astype(BF)
+        msg_ref[peer, half:, :] = tail.astype(BF)
 
 
 def spread(me, parts, gram, peers):
@@ -282,7 +286,7 @@
         spread_kernel,
         out_shape=(
             jax.ShapeDtypeStruct((tokens, total), BF),
-            jax.ShapeDtypeStruct((peers, tokens + 16, columns // peers), BF),
+            jax.ShapeDtypeStruct((peers, tokens // 2 + 16, columns // peers), BF),
             jax.ShapeDtypeStruct((1, columns), F32),
         ),
         in_specs=[pl.BlockSpec(memory_space=pltpu.SMEM)] + [vmem()] * 5,
@@ -437,10 +441,10 @@
     )(share, share, resid, gain, prods, grad)
 
 
-def weight_kernel(plan, order_of, depth, place_ref, gain_ref, wide_ref, grad_ref, *rest):
+def weight_kernel(plan, order_of, depth, place_ref, core_ref, gain_ref, wide_ref, grad_ref, other_ref, *rest):
     count = len(plan)
-    block_refs = rest[:-6]
-    out_hbm, turned_ref, blocks_ref, result_ref, sems, out_sems = rest[-6:]
+    block_refs = rest[:-7]
+    out_hbm, rows_ref, turned_ref, blocks_ref, result_ref, sems, out_sems = rest[-7:]
     tokens, features = block_refs[0].shape
     columns = grad_ref.shape[2]
     total_tokens = tokens * count
@@ -466,8 +470,13 @@
                 def _():
                     load(k, choice[1], i).start()
 
+    half = tokens // 2
+    mine = pl.ds(pl.multiple_of(core_ref[0] * half, half), half)
+    theirs = pl.ds(pl.multiple_of((1 - core_ref[0]) * half, half), half)
     for k in range(count):
-        turned_ref[:, k * tokens : (k + 1) * tokens] = grad_ref[order[k], :tokens, :].T
+        rows_ref[k, mine, :] = grad_ref[order[k], :half, :]
+        rows_ref[k, theirs, :] = other_ref[order[k], :half, :]
+        turned_ref[:, k * tokens : (k + 1) * tokens] = rows_ref[k].T
     start = pl.multiple_of(place_ref[0] * columns, columns)
     scale = wide_ref[:, pl.ds(start, columns)] / total_tokens
 
@@ -491,7 +500,7 @@
         store(step).wait()
 
 
-def weight_grad(place, gain, wide, grads, blocks, plan, order_of):
+def weight_grad(place, core, gain, wide, grads, others, blocks, plan, order_of):
     tokens, features = blocks[0].shape
     columns = grads.shape[2]
     depth = 512
@@ -499,9 +508,10 @@
     return pl.pallas_call(
         functools.partial(weight_kernel, plan, order_of, depth),
         out_shape=jax.ShapeDtypeStruct((features, columns), F32),
-        in_specs=[smem()] + [vmem()] * 3 + [hbm()] * len(blocks),
+        in_specs=[smem(), smem()] + [vmem()] * 4 + [hbm()] * len(blocks),
         out_specs=hbm(),
         scratch_shapes=[
+            pltpu.VMEM((count, tokens, columns), BF),
             pltpu.VMEM((columns, tokens * count), BF),
             pltpu.VMEM((tokens * count, features), BF),
             pltpu.VMEM((features, columns), F32),
@@ -511,7 +521,7 @@
         compiler_params=params(BIG),
         cost_estimate=cost(2 * tokens * count * features * columns, 8 * features * columns),
         name="weights",
-    )(place, gain, wide, grads, *blocks)
+    )(place, core, gain, wide, grads, others, *blocks)
 
 
 def finish_kernel(total_tokens, sum_ref, got_ref, wide_ref, gain_ref, bias_ref):
@@ -621,16 +631,18 @@
     grad, message, col_sums = spread(me[None], (part, part1, part2, part3), gram, peers)
     grads = lax.all_to_all(message, "tok", 0, 0)
     prods, along = products(resid, head_in, grad, objectives)
-    squares = jnp.sum(grads[:, tokens : tokens + 3, :objectives].astype(F32), axis=(0, 1))
+    half = tokens // 2
+    squares = jnp.sum(grads[:, half : half + 3, :objectives].astype(F32), axis=(0, 1))
     squares = squares[None, :]
     got = lax.ppermute(squares, "tp", partner)
     squares = squares + got
     got = lax.ppermute(squares, "tp", across)
+    others = lax.ppermute(grads, "tp", partner)
     entries = total_tokens * total_features
     sums, share, wide = balance_of(entries, squares, got, obj_weight[None, :], along, col_sums)
     sums, got = total_over_tok(sums)
     resid_grad = backward(total_features, resid, gain, prods, grad, share)
-    head_in_grad = weight_grad(place[None], gain, wide, grads, blocks, plan, order_of)
+    head_in_grad = weight_grad(place[None], (me % 2)[None], gain, wide, grads, others, blocks, plan, order_of)
     gain_grad, head_bias_grad = finish(total_tokens, sums, got, wide)
     return (resid_grad, gain_grad[0], head_in_grad, head_bias_grad[0])
 

time: 135 us -> 113 us (0.84)
  starting transfers between devices: 56.6 us -> 37.4 us
  waiting for transfers between devices: 44.3 us -> 42 us
    ppermute x3, starting transfers between devices: 27.6 us -> 3.19 us  [total_over_tok(): got = lax.ppermute(value, 'tok', [(i, i ^ flip) for i in range(count)])]
    ppermute x3, waiting for transfers between devices: 4.47 us -> 20.4 us  [total_over_tok(): got = lax.ppermute(value, 'tok', [(i, i ^ flip) for i in range(count)])]
    ppermute x1, waiting for transfers between devices: 10.5 us -> 0.01 us  [gather_blocks(): x2e = lax.ppermute(f1, 'tok', cross((0, 3)))]
    ppermute x1, waiting for transfers between devices: 8.14 us -> 0.01 us  [gather_blocks(): x3e = lax.ppermute(f2, 'tok', cross((0, 3)))]
    all_to_all x1, waiting for transfers between devices: 10.1 us -> 14.2 us  [fast_device(): grads = lax.all_to_all(message, 'tok', 0, 0)]
    all_to_all x1, starting transfers between devices: 4.79 us -> 8.73 us  [fast_device(): grads = lax.all_to_all(message, 'tok', 0, 0)]
    ppermute x1, waiting for transfers between devices: 1.58 us -> 0.01 us  [fast_device(): recv = lax.ppermute(send, 'tp', partner)]
  transfers between devices with their start and end apart: 22 -> 23, of which waited for: 10 -> 5; matrix products, arithmetic and copies ran while one was open for 1% -> 0% of each run, Pallas kernels for 14% -> 19%
where the time goes in v3:
time: 113 us; the launch traced here: 112 us
  waiting for transfers between devices  42 us (37%)
  starting transfers between devices  37.4 us (33%)
  Pallas kernels  31 us (27%)
    ppermute x3, waiting for transfers between devices, total_over_tok(): got = lax.ppermute(value, 'tok', [(i, i ^ flip) for i in range(count)])  20.4 us
    all_to_all x1, waiting for transfers between devices, fast_device(): grads = lax.all_to_all(message, 'tok', 0, 0)  14.2 us
    all_to_all x1, starting transfers between devices, fast_device(): grads = lax.all_to_all(message, 'tok', 0, 0)  8.73 us
    pallas_call x1, Pallas kernels, products(): pl.pallas_call(products_kernel, out_shape=(jax.ShapeDtypeStruct(shape, BF...  6.39 us
    pallas_call x1, Pallas kernels, backward(): pl.pallas_call(functools.partial(backward_kernel, total), out_shape=jax.S...  5.69 us
    pallas_call x1, Pallas kernels, forward(): pl.pallas_call(forward_kernel, out_shape=(out, out), in_specs=[smem(), hb...  5.55 us
    pallas_call x1, Pallas kernels, gram_of(): pl.pallas_call(gram_kernel, out_shape=jax.ShapeDtypeStruct((objectives, h...  4.75 us
    pallas_call x1, Pallas kernels, weight_grad(): pl.pallas_call(functools.partial(weight_kernel, plan, order_of, depth), o...  4.6 us
  transfers between devices with their start and end apart: 23, of which 5 were waited for; matrix products, arithmetic and copies ran while one was open for 0% of the time, Pallas kernels for 19%

profile of v3, /device:TPU:0, one launch (start us, length us, event | category | flops | bytes accessed | tf_op | source)
XLA Modules:
  0.0 112.2 jit_solution(2077331563141140763)
XLA Ops:
  0.7 5.5 %forward.1 = (f32[2,32,2176]{2,1,0:T(8,128)S(1)}, f32[2,32,2176]{2,1,0:T(8,128)S(1)}) custom-call(s32[1]{0:T(128)} %bitcast.2.core_ref, bf16[128,2048]{1,0:T(8,128)(2,1)} %rest_0_.1, f32[1,2048]{1,0:T(1,128)} %bitcast.14, bf16[2048,2048]{1,0:T(8,128)(2,1)} %weight_hbm.5), custom_call_target="tpu_custom_call" | custom-call | flops 1073741824 | bytes 8388608 | tf_op jit(solution)/shard_map/forward/pallas_call | solution.py:115
  6.9 2.6 %collective-permute-start.12 = (bf16[128,2048]{1,0:T(8,128)(2,1)S(1)}, bf16[128,2048]{1,0:T(8,128)(2,1)S(1)}, u32[]{:S(2)}, u32[]{:S(2)}) collective-permute-start(bf16[128,2048]{1,0:T(8,128)(2,1)S(1)} %copy-done), channel_id=1, source_target_pairs={{0,8},{4,12},{8,0},{12,4},{16,24},{20,28},{24,16},{28,20},{1,9},{5... | collective-permute-start | bytes 1572872 | tf_op jit(solution)/shard_map/ppermute | solution.py:557
  9.5 1.9 %collective-permute-start.1 = (bf16[32,2176]{1,0:T(8,128)(2,1)S(1)}, bf16[32,2176]{1,0:T(8,128)(2,1)S(1)}, u32[]{:S(2)}, u32[]{:S(2)}) collective-permute-start(bf16[32,2176]{1,0:T(8,128)(2,1)S(1)} %get-tuple-element.21), channel_id=1, source_target_pairs={{0,2},{1,3},{2,0},{3,1},{4,6},{5,7},{6,4},{7,5},{8,10},{9,11},{10,... | collective-permute-start | bytes 417800 | tf_op jit(solution)/shard_map/ppermute | solution.py:616
  11.4 4.0 %collective-permute-done.1.recv_ref = bf16[32,2176]{1,0:T(8,128)(2,1)S(1)} collective-permute-done((bf16[32,2176]{1,0:T(8,128)(2,1)S(1)}, bf16[32,2176]{1,0:T(8,128)(2,1)S(1)}, u32[]{:S(2)}, u32[]{:S(2)}) %collective-permute-start.1) | collective-permute-done | bytes 139296 | tf_op jit(solution)/shard_map/ppermute | solution.py:616
  15.4 2.0 %heads.1.part0_ref = bf16[32,2176]{1,0:T(8,128)(2,1)S(1)} custom-call(s32[1]{0:T(128)} %bitcast.me_ref.spot_ref, f32[32,2176]{1,0:T(8,128)S(1)} %get-tuple-element.20.mine_ref, bf16[32,2176]{1,0:T(8,128)(2,1)S(1)} %collective-permute-done.1.recv_ref, f32[1,2048]{1,0:T(1,128)S(1)} %bitcast.17, f32[1,2048]{1,0:T(1,128)S(1)} %bitcast.18, ...), custom_call_target="tpu_custom_call" | custom-call | flops 2088960 | bytes 557056 | tf_op jit(solution)/shard_map/heads/pallas_call | solution.py:203
  17.4 1.8 %collective-permute-start.3 = (bf16[32,2176]{1,0:T(8,128)(2,1)S(1)}, bf16[32,2176]{1,0:T(8,128)(2,1)S(1)}, u32[]{:S(2)}, u32[]{:S(2)}) collective-permute-start(bf16[32,2176]{1,0:T(8,128)(2,1)S(1)} %heads.1.part0_ref), channel_id=1, source_target_pairs={{0,2},{1,3},{2,0},{3,1},{4,6},{5,7},{6,4},{7,5},{8,10},{9,11},{10,... | collective-permute-start | bytes 417800 | tf_op jit(solution)/shard_map/ppermute | solution.py:629
  19.2 3.3 %collective-permute-done.3.part2_ref = bf16[32,2176]{1,0:T(8,128)(2,1)S(1)} collective-permute-done((bf16[32,2176]{1,0:T(8,128)(2,1)S(1)}, bf16[32,2176]{1,0:T(8,128)(2,1)S(1)}, u32[]{:S(2)}, u32[]{:S(2)}) %collective-permute-start.3) | collective-permute-done | bytes 139296 | tf_op jit(solution)/shard_map/ppermute | solution.py:629
  23.2 4.8 %gram.1.gram_ref = f32[16,128,128]{2,1,0:T(8,128)S(1)} custom-call(bf16[2048,2048]{1,0:T(8,128)(2,1)} %weight_hbm.5), custom_call_target="tpu_custom_call" | custom-call | flops 1073741824 | bytes 8388608 | tf_op jit(solution)/shard_map/gram/pallas_call | solution.py:235
  28.0 1.5 %collective-permute-start.18 = (bf16[128,2048]{1,0:T(8,128)(2,1)S(1)}, bf16[128,2048]{1,0:T(8,128)(2,1)}, u32[]{:S(2)}, u32[]{:S(2)}) collective-permute-start(bf16[128,2048]{1,0:T(8,128)(2,1)S(1)} %collective-permute-done.12.rest_2_), channel_id=1, source_target_pairs={{8,16},{12,20},{16,8},{20,12},{9,17},{13,21},{17,9},{21,13},{10,18... | collective-permute-start | bytes 1572872 | tf_op jit(solution)/shard_map/ppermute | solution.py:559
  30.8 8.7 %all-to-all-start = ((bf16[8,80,256]{2,1,0:T(8,128)(2,1)}), bf16[8,80,256]{2,1,0:T(8,128)(2,1)S(1)}, u32[]{:S(2)}, u32[]{:S(2)}) async-start(bf16[8,80,256]{2,1,0:T(8,128)(2,1)} %get-tuple-element.22), calls=%async_computation | async-start | bytes 655360 | tf_op jit(solution)/shard_map/all_to_all | solution.py:632
  39.5 2.0 %collective-permute-start.11 = (bf16[128,2048]{1,0:T(8,128)(2,1)S(1)}, bf16[128,2048]{1,0:T(8,128)(2,1)S(1)}, u32[]{:S(2)}, u32[]{:S(2)}) collective-permute-start(bf16[128,2048]{1,0:T(8,128)(2,1)S(1)} %copy-done), channel_id=1, source_target_pairs={{0,4},{4,0},{8,12},{12,8},{16,20},{20,16},{24,28},{28,24},{1,5},{5... | collective-permute-start | bytes 1572872 | tf_op jit(solution)/shard_map/ppermute | solution.py:556
  44.1 14.2 %all-to-all-done.grad_ref = bf16[8,80,256]{2,1,0:T(8,128)(2,1)S(1)} async-done(((bf16[8,80,256]{2,1,0:T(8,128)(2,1)}), bf16[8,80,256]{2,1,0:T(8,128)(2,1)S(1)}, u32[]{:S(2)}, u32[]{:S(2)}) %all-to-all-start) | async-done | bytes 327712 | tf_op jit(solution)/shard_map/all_to_all | solution.py:632
  58.4 1.6 %collective-permute-start.13 = (bf16[128,2048]{1,0:T(8,128)(2,1)S(1)}, bf16[128,2048]{1,0:T(8,128)(2,1)S(1)}, u32[]{:S(2)}, u32[]{:S(2)}) collective-permute-start(bf16[128,2048]{1,0:T(8,128)(2,1)S(1)} %collective-permute-done.12.rest_2_), channel_id=1, source_target_pairs={{0,4},{4,0},{8,12},{12,8},{16,20},{20,16},{24,28},{28,24},{1,5},{5... | collective-permute-start | bytes 1572872 | tf_op jit(solution)/shard_map/ppermute | solution.py:560
  60.0 1.5 %collective-permute-start.6 = (f32[1,16]{1,0:T(1,128)S(1)}, f32[1,16]{1,0:T(1,128)S(1)}, u32[]{:S(2)}, u32[]{:S(2)}) collective-permute-start(f32[1,16]{1,0:T(1,128)S(1)} %bitcast_add_fusion.squares_ref), channel_id=1, source_target_pairs={{0,2},{1,3},{2,0},{3,1},{4,6},{5,7},{6,4},{7,5},{8,10},{9,11},{10,... | collective-permute-start | bytes 200 | tf_op jit(solution)/shard_map/ppermute | solution.py:639
  61.5 6.4 %products.1 = (bf16[16,128,2048]{2,1,0:T(8,128)(2,1)}, f32[16,2048]{1,0:T(8,128)S(1)}) custom-call(bf16[128,2048]{1,0:T(8,128)(2,1)S(1)} %copy-done, bf16[2048,2048]{1,0:T(8,128)(2,1)} %weight_hbm.5, bf16[128,2176]{1,0:T(8,128)(2,1)S(1)} %get-tuple-element.23.grad_ref.extra_ref), custom_call_target="tpu_custom_call" | custom-call | flops 1073741824 | bytes 16777216 | tf_op jit(solution)/shard_map/products/pallas_call | solution.py:334
  68.7 3.2 %collective-permute-done.7 = f32[2,2048]{1,0:T(2,128)S(1)} collective-permute-done((f32[2,2048]{1,0:T(2,128)S(1)}, f32[2,2048]{1,0:T(2,128)S(1)}, u32[]{:S(2)}, u32[]{:S(2)}) %collective-permute-start.7) | collective-permute-done | bytes 16416 | tf_op jit(solution)/shard_map/ppermute | solution.py:594
  71.9 1.6 %collective-permute-start.8 = (f32[2,2048]{1,0:T(2,128)S(1)}, f32[2,2048]{1,0:T(2,128)S(1)}, u32[]{:S(2)}, u32[]{:S(2)}) collective-permute-start(f32[2,2048]{1,0:T(2,128)S(1)} %add.17), channel_id=1, source_target_pairs={{0,16},{4,20},{8,24},{12,28},{16,0},{20,4},{24,8},{28,12},{1,17},{... | collective-permute-start | bytes 49160 | tf_op jit(solution)/shard_map/ppermute | solution.py:594
  73.5 1.5 %collective-permute-start.16 = (bf16[128,2048]{1,0:T(8,128)(2,1)S(1)}, bf16[128,2048]{1,0:T(8,128)(2,1)}, u32[]{:S(2)}, u32[]{:S(2)}) collective-permute-start(bf16[128,2048]{1,0:T(8,128)(2,1)S(1)} %collective-permute-done.14.rest_4_), channel_id=1, source_target_pairs={{8,12},{12,8},{16,20},{20,16},{9,13},{13,9},{17,21},{21,17},{10,14... | collective-permute-start | bytes 1572872 | tf_op jit(solution)/shard_map/ppermute | solution.py:563
  75.0 2.8 %collective-permute-start.17 = (bf16[128,2048]{1,0:T(8,128)(2,1)}, bf16[128,2048]{1,0:T(8,128)(2,1)}, u32[]{:S(2)}, u32[]{:S(2)}) collective-permute-start(bf16[128,2048]{1,0:T(8,128)(2,1)} %collective-permute-done.15.rest_5_), channel_id=1, source_target_pairs={{0,4},{4,0},{24,28},{28,24},{1,5},{5,1},{25,29},{29,25},{2,6},{6,2... | collective-permute-start | bytes 1572872 | tf_op jit(solution)/shard_map/ppermute | solution.py:564
  77.8 1.5 %collective-permute-start.20 = (bf16[128,2048]{1,0:T(8,128)(2,1)}, bf16[128,2048]{1,0:T(8,128)(2,1)}, u32[]{:S(2)}, u32[]{:S(2)}) collective-permute-start(bf16[128,2048]{1,0:T(8,128)(2,1)} %collective-permute-done.18.rest_8_), channel_id=1, source_target_pairs={{8,12},{12,8},{16,20},{20,16},{9,13},{13,9},{17,21},{21,17},{10,14... | collective-permute-start | bytes 1572872 | tf_op jit(solution)/shard_map/ppermute | solution.py:565
  79.3 3.0 %collective-permute-start.21 = (bf16[128,2048]{1,0:T(8,128)(2,1)}, bf16[128,2048]{1,0:T(8,128)(2,1)}, u32[]{:S(2)}, u32[]{:S(2)}) collective-permute-start(bf16[128,2048]{1,0:T(8,128)(2,1)} %collective-permute-done.19.rest_9_), channel_id=1, source_target_pairs={{0,4},{4,0},{24,28},{28,24},{1,5},{5,1},{25,29},{29,25},{2,6},{6,2... | collective-permute-start | bytes 1572872 | tf_op jit(solution)/shard_map/ppermute | solution.py:566
  84.1 17.2 %collective-permute-done.9.got_ref = f32[2,2048]{1,0:T(2,128)S(1)} collective-permute-done((f32[2,2048]{1,0:T(2,128)S(1)}, f32[2,2048]{1,0:T(2,128)S(1)}, u32[]{:S(2)}, u32[]{:S(2)}) %collective-permute-start.9) | collective-permute-done | bytes 16416 | tf_op jit(solution)/shard_map/ppermute | solution.py:594
  101.3 5.7 %backward.1 = bf16[128,2048]{1,0:T(8,128)(2,1)} custom-call(f32[1,16]{1,0:T(1,128)S(1)} %get-tuple-element.26.share_ref.row_ref, f32[1,16]{1,0:T(1,128)S(1)} %get-tuple-element.26.share_ref.row_ref, bf16[128,2048]{1,0:T(8,128)(2,1)S(1)} %copy-done, f32[1,2048]{1,0:T(1,128)S(1)} %bitcast.15, bf16[16,128,2048]{2,1,0:T(8,128)(2,1)} %get-tuple-element.27.prod_hbm, ...), custom_call_target="tpu_custom_call" | custom-call | flops 8388608 | bytes 8388608 | tf_op jit(solution)/shard_map/backward/pallas_call | solution.py:420
  107.6 4.6 %weights.1 = f32[2048,256]{1,0:T(8,128)} custom-call(s32[1]{0:T(128)} %bitcast.11.place_ref, s32[1]{0:T(128)} %bitcast.2.core_ref, f32[1,2048]{1,0:T(1,128)S(1)} %bitcast.16, f32[1,2048]{1,0:T(1,128)S(1)} %get-tuple-element.29.wide_ref, bf16[8,80,256]{2,1,0:T(8,128)(2,1)S(1)} %all-to-all-done.grad_ref, ...), custom_call_target="tpu_custom_call" | custom-call | flops 1073741824 | bytes 4194304 | tf_op jit(solution)/shard_map/weights/pallas_call | solution.py:508
  (54 shorter events, 8.5 us)
Async XLA Ops:
  6.3 3.2 %collective-permute-start = (f32[2,32,2176]{2,1,0:T(8,128)S(1)}, f32[2,32,2176]{2,1,0:T(8,128)S(1)}, u32[]{:S(2)}, u32[]{:S(2)}) collective-permute-start(f32[2,32,2176]{2,1,0:T(8,128)S(1)} %get-tuple-element.19), channel_id=1, source_target_pairs={{0,1},{1,0},{2,3},{3,2},{4,5},{5,4},{6,7},{7,6},{8,9},{9,8},{10,11... | collective-permute-start | bytes 1671176 | tf_op jit(solution)/shard_map/ppermute | solution.py:614
  6.9 21.1 %collective-permute-start.12 = (bf16[128,2048]{1,0:T(8,128)(2,1)S(1)}, bf16[128,2048]{1,0:T(8,128)(2,1)S(1)}, u32[]{:S(2)}, u32[]{:S(2)}) collective-permute-start(bf16[128,2048]{1,0:T(8,128)(2,1)S(1)} %copy-done), channel_id=1, source_target_pairs={{0,8},{4,12},{8,0},{12,4},{16,24},{20,28},{24,16},{28,20},{1,9},{5... | collective-permute-start | bytes 1572872 | tf_op jit(solution)/shard_map/ppermute | solution.py:557
  9.5 5.9 %collective-permute-start.1 = (bf16[32,2176]{1,0:T(8,128)(2,1)S(1)}, bf16[32,2176]{1,0:T(8,128)(2,1)S(1)}, u32[]{:S(2)}, u32[]{:S(2)}) collective-permute-start(bf16[32,2176]{1,0:T(8,128)(2,1)S(1)} %get-tuple-element.21), channel_id=1, source_target_pairs={{0,2},{1,3},{2,0},{3,1},{4,6},{5,7},{6,4},{7,5},{8,10},{9,11},{10,... | collective-permute-start | bytes 417800 | tf_op jit(solution)/shard_map/ppermute | solution.py:616
  17.4 83.9 %copy-start.3 = (f32[2048]{0:T(1024)S(1)}, f32[2048]{0:T(1024)}, u32[]{:S(2)}) copy-start(f32[2048]{0:T(1024)} %param.9) | copy-start | bytes 24580
  17.4 5.1 %collective-permute-start.3 = (bf16[32,2176]{1,0:T(8,128)(2,1)S(1)}, bf16[32,2176]{1,0:T(8,128)(2,1)S(1)}, u32[]{:S(2)}, u32[]{:S(2)}) collective-permute-start(bf16[32,2176]{1,0:T(8,128)(2,1)S(1)} %heads.1.part0_ref), channel_id=1, source_target_pairs={{0,2},{1,3},{2,0},{3,1},{4,6},{5,7},{6,4},{7,5},{8,10},{9,11},{10,... | collective-permute-start | bytes 417800 | tf_op jit(solution)/shard_map/ppermute | solution.py:629
  19.2 10.2 %collective-permute-start.2 = (bf16[32,2176]{1,0:T(8,128)(2,1)S(1)}, bf16[32,2176]{1,0:T(8,128)(2,1)S(1)}, u32[]{:S(2)}, u32[]{:S(2)}) collective-permute-start(bf16[32,2176]{1,0:T(8,128)(2,1)S(1)} %heads.1.part0_ref), channel_id=1, source_target_pairs={{0,1},{1,0},{2,3},{3,2},{4,5},{5,4},{6,7},{7,6},{8,9},{9,8},{10,11... | collective-permute-start | bytes 417800 | tf_op jit(solution)/shard_map/ppermute | solution.py:628
  22.5 6.9 %collective-permute-start.4 = (bf16[32,2176]{1,0:T(8,128)(2,1)S(1)}, bf16[32,2176]{1,0:T(8,128)(2,1)S(1)}, u32[]{:S(2)}, u32[]{:S(2)}) collective-permute-start(bf16[32,2176]{1,0:T(8,128)(2,1)S(1)} %collective-permute-done.3.part2_ref), channel_id=1, source_target_pairs={{0,1},{1,0},{2,3},{3,2},{4,5},{5,4},{6,7},{7,6},{8,9},{9,8},{10,11... | collective-permute-start | bytes 417800 | tf_op jit(solution)/shard_map/ppermute | solution.py:630
  22.5 19.0 %collective-permute-start.14 = (bf16[128,2048]{1,0:T(8,128)(2,1)S(1)}, bf16[128,2048]{1,0:T(8,128)(2,1)S(1)}, u32[]{:S(2)}, u32[]{:S(2)}) collective-permute-start(bf16[128,2048]{1,0:T(8,128)(2,1)S(1)} %copy-done), channel_id=1, source_target_pairs={{8,16},{12,20},{16,8},{20,12},{9,17},{13,21},{17,9},{21,13},{10,18... | collective-permute-start | bytes 1572872 | tf_op jit(solution)/shard_map/ppermute | solution.py:558
  28.0 14.8 %collective-permute-start.18 = (bf16[128,2048]{1,0:T(8,128)(2,1)S(1)}, bf16[128,2048]{1,0:T(8,128)(2,1)}, u32[]{:S(2)}, u32[]{:S(2)}) collective-permute-start(bf16[128,2048]{1,0:T(8,128)(2,1)S(1)} %collective-permute-done.12.rest_2_), channel_id=1, source_target_pairs={{8,16},{12,20},{16,8},{20,12},{9,17},{13,21},{17,9},{21,13},{10,18... | collective-permute-start | bytes 1572872 | tf_op jit(solution)/shard_map/ppermute | solution.py:559
  30.8 27.6 %all-to-all-start = ((bf16[8,80,256]{2,1,0:T(8,128)(2,1)}), bf16[8,80,256]{2,1,0:T(8,128)(2,1)S(1)}, u32[]{:S(2)}, u32[]{:S(2)}) async-start(bf16[8,80,256]{2,1,0:T(8,128)(2,1)} %get-tuple-element.22), calls=%async_computation | async-start | bytes 655360 | tf_op jit(solution)/shard_map/all_to_all | solution.py:632
  39.5 34.1 %collective-permute-start.11 = (bf16[128,2048]{1,0:T(8,128)(2,1)S(1)}, bf16[128,2048]{1,0:T(8,128)(2,1)S(1)}, u32[]{:S(2)}, u32[]{:S(2)}) collective-permute-start(bf16[128,2048]{1,0:T(8,128)(2,1)S(1)} %copy-done), channel_id=1, source_target_pairs={{0,4},{4,0},{8,12},{12,8},{16,20},{20,16},{24,28},{28,24},{1,5},{5... | collective-permute-start | bytes 1572872 | tf_op jit(solution)/shard_map/ppermute | solution.py:556
  41.5 33.5 %collective-permute-start.15 = (bf16[128,2048]{1,0:T(8,128)(2,1)S(1)}, bf16[128,2048]{1,0:T(8,128)(2,1)}, u32[]{:S(2)}, u32[]{:S(2)}) collective-permute-start(bf16[128,2048]{1,0:T(8,128)(2,1)S(1)} %collective-permute-done.14.rest_4_), channel_id=1, source_target_pairs={{8,0},{12,4},{16,24},{20,28},{9,1},{13,5},{17,25},{21,29},{10,2},{... | collective-permute-start | bytes 1572872 | tf_op jit(solution)/shard_map/ppermute | solution.py:561
  42.8 35.0 %collective-permute-start.19 = (bf16[128,2048]{1,0:T(8,128)(2,1)}, bf16[128,2048]{1,0:T(8,128)(2,1)}, u32[]{:S(2)}, u32[]{:S(2)}) collective-permute-start(bf16[128,2048]{1,0:T(8,128)(2,1)} %collective-permute-done.18.rest_8_), channel_id=1, source_target_pairs={{8,0},{12,4},{16,24},{20,28},{9,1},{13,5},{17,25},{21,29},{10,2},{... | collective-permute-start | bytes 1572872 | tf_op jit(solution)/shard_map/ppermute | solution.py:562
  58.4 1.6 %collective-permute-start.5 = (f32[1,16]{1,0:T(1,128)S(1)}, f32[1,16]{1,0:T(1,128)S(1)}, u32[]{:S(2)}, u32[]{:S(2)}) collective-permute-start(f32[1,16]{1,0:T(1,128)S(1)} %bitcast.22), channel_id=1, source_target_pairs={{0,1},{1,0},{2,3},{3,2},{4,5},{5,4},{6,7},{7,6},{8,9},{9,8},{10,11... | collective-permute-start | bytes 200 | tf_op jit(solution)/shard_map/ppermute | solution.py:637
  58.4 23.9 %collective-permute-start.13 = (bf16[128,2048]{1,0:T(8,128)(2,1)S(1)}, bf16[128,2048]{1,0:T(8,128)(2,1)S(1)}, u32[]{:S(2)}, u32[]{:S(2)}) collective-permute-start(bf16[128,2048]{1,0:T(8,128)(2,1)S(1)} %collective-permute-done.12.rest_2_), channel_id=1, source_target_pairs={{0,4},{4,0},{8,12},{12,8},{16,20},{20,16},{24,28},{28,24},{1,5},{5... | collective-permute-start | bytes 1572872 | tf_op jit(solution)/shard_map/ppermute | solution.py:560
  60.0 7.9 %collective-permute-start.6 = (f32[1,16]{1,0:T(1,128)S(1)}, f32[1,16]{1,0:T(1,128)S(1)}, u32[]{:S(2)}, u32[]{:S(2)}) collective-permute-start(f32[1,16]{1,0:T(1,128)S(1)} %bitcast_add_fusion.squares_ref), channel_id=1, source_target_pairs={{0,2},{1,3},{2,0},{3,1},{4,6},{5,7},{6,4},{7,5},{8,10},{9,11},{10,... | collective-permute-start | bytes 200 | tf_op jit(solution)/shard_map/ppermute | solution.py:639
  68.1 3.8 %collective-permute-start.7 = (f32[2,2048]{1,0:T(2,128)S(1)}, f32[2,2048]{1,0:T(2,128)S(1)}, u32[]{:S(2)}, u32[]{:S(2)}) collective-permute-start(f32[2,2048]{1,0:T(2,128)S(1)} %get-tuple-element.28), channel_id=1, source_target_pairs={{0,8},{4,12},{8,0},{12,4},{16,24},{20,28},{24,16},{28,20},{1,9},{5... | collective-permute-start | bytes 49160 | tf_op jit(solution)/shard_map/ppermute | solution.py:594
  71.9 7.4 %collective-permute-start.8 = (f32[2,2048]{1,0:T(2,128)S(1)}, f32[2,2048]{1,0:T(2,128)S(1)}, u32[]{:S(2)}, u32[]{:S(2)}) collective-permute-start(f32[2,2048]{1,0:T(2,128)S(1)} %add.17), channel_id=1, source_target_pairs={{0,16},{4,20},{8,24},{12,28},{16,0},{20,4},{24,8},{28,12},{1,17},{... | collective-permute-start | bytes 49160 | tf_op jit(solution)/shard_map/ppermute | solution.py:594
  73.5 34.0 %collective-permute-start.16 = (bf16[128,2048]{1,0:T(8,128)(2,1)S(1)}, bf16[128,2048]{1,0:T(8,128)(2,1)}, u32[]{:S(2)}, u32[]{:S(2)}) collective-permute-start(bf16[128,2048]{1,0:T(8,128)(2,1)S(1)} %collective-permute-done.14.rest_4_), channel_id=1, source_target_pairs={{8,12},{12,8},{16,20},{20,16},{9,13},{13,9},{17,21},{21,17},{10,14... | collective-permute-start | bytes 1572872 | tf_op jit(solution)/shard_map/ppermute | solution.py:563
  75.0 32.6 %collective-permute-start.17 = (bf16[128,2048]{1,0:T(8,128)(2,1)}, bf16[128,2048]{1,0:T(8,128)(2,1)}, u32[]{:S(2)}, u32[]{:S(2)}) collective-permute-start(bf16[128,2048]{1,0:T(8,128)(2,1)} %collective-permute-done.15.rest_5_), channel_id=1, source_target_pairs={{0,4},{4,0},{24,28},{28,24},{1,5},{5,1},{25,29},{29,25},{2,6},{6,2... | collective-permute-start | bytes 1572872 | tf_op jit(solution)/shard_map/ppermute | solution.py:564
  77.8 29.7 %collective-permute-start.20 = (bf16[128,2048]{1,0:T(8,128)(2,1)}, bf16[128,2048]{1,0:T(8,128)(2,1)}, u32[]{:S(2)}, u32[]{:S(2)}) collective-permute-start(bf16[128,2048]{1,0:T(8,128)(2,1)} %collective-permute-done.18.rest_8_), channel_id=1, source_target_pairs={{8,12},{12,8},{16,20},{20,16},{9,13},{13,9},{17,21},{21,17},{10,14... | collective-permute-start | bytes 1572872 | tf_op jit(solution)/shard_map/ppermute | solution.py:565
  79.3 28.3 %collective-permute-start.21 = (bf16[128,2048]{1,0:T(8,128)(2,1)}, bf16[128,2048]{1,0:T(8,128)(2,1)}, u32[]{:S(2)}, u32[]{:S(2)}) collective-permute-start(bf16[128,2048]{1,0:T(8,128)(2,1)} %collective-permute-done.19.rest_9_), channel_id=1, source_target_pairs={{0,4},{4,0},{24,28},{28,24},{1,5},{5,1},{25,29},{29,25},{2,6},{6,2... | collective-permute-start | bytes 1572872 | tf_op jit(solution)/shard_map/ppermute | solution.py:566
  83.1 18.1 %collective-permute-start.9 = (f32[2,2048]{1,0:T(2,128)S(1)}, f32[2,2048]{1,0:T(2,128)S(1)}, u32[]{:S(2)}, u32[]{:S(2)}) collective-permute-start(f32[2,2048]{1,0:T(2,128)S(1)} %add.18.sum_ref), channel_id=1, source_target_pairs={{0,4},{4,0},{8,12},{12,8},{16,20},{20,16},{24,28},{28,24},{1,5},{5... | collective-permute-start | bytes 49160 | tf_op jit(solution)/shard_map/ppermute | solution.py:594
  101.3 6.3 %collective-permute-start.10 = (bf16[8,80,256]{2,1,0:T(8,128)(2,1)S(1)}, bf16[8,80,256]{2,1,0:T(8,128)(2,1)S(1)}, u32[]{:S(2)}, u32[]{:S(2)}) collective-permute-start(bf16[8,80,256]{2,1,0:T(8,128)(2,1)S(1)} %all-to-all-done.grad_ref), channel_id=1, source_target_pairs={{0,1},{1,0},{2,3},{3,2},{4,5},{5,4},{6,7},{7,6},{8,9},{9,8},{10,11... | collective-permute-start | bytes 983048 | tf_op jit(solution)/shard_map/ppermute | solution.py:640
  (8 other events, 122.9 us)

commit v4 on v3

--- a/solution.py
+++ b/solution.py
@@ -159,7 +159,7 @@
 
 
 def heads_kernel(
-    features, me_ref, mine_ref, recv_ref, bias_ref, out_ref, targets_ref, mask_ref, msg_ref, turned_ref
+    features, me_ref, mine_ref, recv_ref, bias_ref, out_ref, targets_ref, mask_ref, msg_ref, turned_ref, hold_ref
 ):
     rows = mine_ref.shape[0]
     columns = mine_ref.shape[1] - LANES
@@ -173,22 +173,28 @@
     tail = recv_ref[:, columns:].astype(F32)
     sums = mine_ref[:, columns : columns + 1] + ((tail[:, 0:1] + tail[:, 1:2]) + tail[:, 2:3])
     inverse = lax.rsqrt(sums / features + norm_eps)
-    lane = lax.broadcasted_iota(jnp.int32, (rows, LANES), 1)
-    extra = jnp.zeros((rows, LANES), F32)
+    spot = lax.broadcasted_iota(jnp.int32, (rows, objectives), 1)
+    scores = jnp.zeros((rows, objectives), F32)
     for which in range(objectives):
         cols = slice(which * hidden, (which + 1) * hidden)
         product = (mine_ref[:, cols] + recv_ref[:, cols].astype(F32)) * inverse
         value = product + bias_ref[:, cols]
         squash = jax.nn.sigmoid(value)
-        weight = out_ref[:, cols]
-        score = jnp.sum(value * squash * weight, axis=1, keepdims=True)
-        error = mask[:, which : which + 1] * (score - target[:, which : which + 1])
-        grad = (error * weight * (squash * (1.0 + value * (1.0 - squash)))).astype(BF)
+        hold_ref[0, :, cols] = product
+        hold_ref[1, :, cols] = squash * (1.0 + value * (1.0 - squash))
+        score = jnp.sum(value * squash * out_ref[:, cols], axis=1, keepdims=True)
+        scores = jnp.where(spot == which, score, scores)
+    errors = mask * (scores - target)
+    lane = lax.broadcasted_iota(jnp.int32, (rows, LANES), 1)
+    alongs = jnp.zeros((rows, LANES), F32)
+    for which in range(objectives):
+        cols = slice(which * hidden, (which + 1) * hidden)
+        grad = (errors[:, which : which + 1] * out_ref[:, cols] * hold_ref[1, :, cols]).astype(BF)
         msg_ref[:, cols] = grad
-        along = jnp.sum(grad.astype(F32) * product, axis=1, keepdims=True)
-        high = along.astype(BF).astype(F32)
-        extra = jnp.where(lane == which, high, extra)
-        extra = jnp.where(lane == objectives + which, along - high, extra)
+        along = jnp.sum(grad.astype(F32) * hold_ref[0, :, cols], axis=1, keepdims=True)
+        alongs = jnp.where((lane == which) | (lane == objectives + which), along, alongs)
+    high = alongs.astype(BF).astype(F32)
+    extra = jnp.where(lane < objectives, high, alongs - high)
     high = inverse.astype(BF).astype(F32)
     rest = inverse - high
     middle = rest.astype(BF).astype(F32)
@@ -205,7 +211,10 @@
         out_shape=jax.ShapeDtypeStruct(mine.shape, BF),
         in_specs=[pl.BlockSpec(memory_space=pltpu.SMEM)] + [vmem()] * 6,
         out_specs=vmem(),
-        scratch_shapes=[pltpu.VMEM((2, tokens, targets.shape[0]), F32)],
+        scratch_shapes=[
+            pltpu.VMEM((2, tokens, targets.shape[0]), F32),
+            pltpu.VMEM((2, mine.shape[0], bias.shape[1]), F32),
+        ],
         compiler_params=params(8),
         cost_estimate=cost(30 * mine.size, 8 * mine.size),
         name="heads",
@@ -433,7 +442,7 @@
         scratch_shapes=[
             pltpu.VMEM(prods.shape, BF),
             pltpu.VMEM((2, tokens, LANES), F32),
-            pltpu.SemaphoreType.DMA((4,)),
+            pltpu.SemaphoreType.DMA((8,)),
         ],
         compiler_params=params(BIG),
         cost_estimate=cost(2 * prods.size, 2 * prods.size),
@@ -586,7 +595,7 @@
 
 def total_over_tok(value):
     count = lax.axis_size("tok")
-    flips = [1 << bit for bit in range(1, count.bit_length() - 1)] + [1]
+    flips = [1 << bit for bit in reversed(range(1, count.bit_length() - 1))] + [1]
     got = None
     for step, flip in enumerate(flips):
         if step:

time: 113 us -> 111 us (0.982)
  transfers between devices with their start and end apart: 23 -> 23, of which waited for: 5 -> 5; matrix products, arithmetic and copies ran while one was open for 0% -> 0% of each run, Pallas kernels for 19% -> 18%
where the time goes in v4:
time: 111 us
  waiting for transfers between devices  41.7 us (38%)
  starting transfers between devices  37.3 us (34%)
  Pallas kernels  30.2 us (27%)
    ppermute x3, waiting for transfers between devices, total_over_tok(): got = lax.ppermute(value, 'tok', [(i, i ^ flip) for i in range(count)])  20.1 us
    all_to_all x1, waiting for transfers between devices, fast_device(): grads = lax.all_to_all(message, 'tok', 0, 0)  14.2 us
    all_to_all x1, starting transfers between devices, fast_device(): grads = lax.all_to_all(message, 'tok', 0, 0)  8.73 us
    pallas_call x1, Pallas kernels, products(): pl.pallas_call(products_kernel, out_shape=(jax.ShapeDtypeStruct(shape, BF...  6.4 us
    pallas_call x1, Pallas kernels, forward(): pl.pallas_call(forward_kernel, out_shape=(out, out), in_specs=[smem(), hb...  5.55 us
    pallas_call x1, Pallas kernels, backward(): pl.pallas_call(functools.partial(backward_kernel, total), out_shape=jax.S...  5.35 us
    pallas_call x1, Pallas kernels, gram_of(): pl.pallas_call(gram_kernel, out_shape=jax.ShapeDtypeStruct((objectives, h...  4.76 us
    pallas_call x1, Pallas kernels, weight_grad(): pl.pallas_call(functools.partial(weight_kernel, plan, order_of, depth), o...  4.6 us
  transfers between devices with their start and end apart: 23, of which 5 were waited for; matrix products, arithmetic and copies ran while one was open for 0% of the time, Pallas kernels for 18%

profile of v4, /device:TPU:0, one launch (start us, length us, event | category | flops | bytes accessed | tf_op | source)
XLA Modules:
  0.0 111.0 jit_solution(791132425324963286)
XLA Ops:
  0.7 5.5 %forward.1 = (f32[2,32,2176]{2,1,0:T(8,128)S(1)}, f32[2,32,2176]{2,1,0:T(8,128)S(1)}) custom-call(s32[1]{0:T(128)} %bitcast.2.core_ref, bf16[128,2048]{1,0:T(8,128)(2,1)} %rest_0_.1, f32[1,2048]{1,0:T(1,128)} %bitcast.14, bf16[2048,2048]{1,0:T(8,128)(2,1)} %weight_hbm.5), custom_call_target="tpu_custom_call" | custom-call | flops 1073741824 | bytes 8388608 | tf_op jit(solution)/shard_map/forward/pallas_call | solution.py:115
  6.9 2.6 %collective-permute-start.12 = (bf16[128,2048]{1,0:T(8,128)(2,1)S(1)}, bf16[128,2048]{1,0:T(8,128)(2,1)S(1)}, u32[]{:S(2)}, u32[]{:S(2)}) collective-permute-start(bf16[128,2048]{1,0:T(8,128)(2,1)S(1)} %copy-done), channel_id=1, source_target_pairs={{0,8},{4,12},{8,0},{12,4},{16,24},{20,28},{24,16},{28,20},{1,9},{5... | collective-permute-start | bytes 1572872 | tf_op jit(solution)/shard_map/ppermute | solution.py:566
  9.5 1.9 %collective-permute-start.1 = (bf16[32,2176]{1,0:T(8,128)(2,1)S(1)}, bf16[32,2176]{1,0:T(8,128)(2,1)S(1)}, u32[]{:S(2)}, u32[]{:S(2)}) collective-permute-start(bf16[32,2176]{1,0:T(8,128)(2,1)S(1)} %get-tuple-element.21), channel_id=1, source_target_pairs={{0,2},{1,3},{2,0},{3,1},{4,6},{5,7},{6,4},{7,5},{8,10},{9,11},{10,... | collective-permute-start | bytes 417800 | tf_op jit(solution)/shard_map/ppermute | solution.py:625
  11.4 4.0 %collective-permute-done.1.recv_ref = bf16[32,2176]{1,0:T(8,128)(2,1)S(1)} collective-permute-done((bf16[32,2176]{1,0:T(8,128)(2,1)S(1)}, bf16[32,2176]{1,0:T(8,128)(2,1)S(1)}, u32[]{:S(2)}, u32[]{:S(2)}) %collective-permute-start.1) | collective-permute-done | bytes 139296 | tf_op jit(solution)/shard_map/ppermute | solution.py:625
  15.4 1.5 %heads.1.part0_ref = bf16[32,2176]{1,0:T(8,128)(2,1)S(1)} custom-call(s32[1]{0:T(128)} %bitcast.me_ref.spot_ref, f32[32,2176]{1,0:T(8,128)S(1)} %get-tuple-element.20.mine_ref, bf16[32,2176]{1,0:T(8,128)(2,1)S(1)} %collective-permute-done.1.recv_ref, f32[1,2048]{1,0:T(1,128)S(1)} %bitcast.17, f32[1,2048]{1,0:T(1,128)S(1)} %bitcast.18, ...), custom_call_target="tpu_custom_call" | custom-call | flops 2088960 | bytes 557056 | tf_op jit(solution)/shard_map/heads/pallas_call | solution.py:209
  16.9 1.8 %collective-permute-start.3 = (bf16[32,2176]{1,0:T(8,128)(2,1)S(1)}, bf16[32,2176]{1,0:T(8,128)(2,1)S(1)}, u32[]{:S(2)}, u32[]{:S(2)}) collective-permute-start(bf16[32,2176]{1,0:T(8,128)(2,1)S(1)} %heads.1.part0_ref), channel_id=1, source_target_pairs={{0,2},{1,3},{2,0},{3,1},{4,6},{5,7},{6,4},{7,5},{8,10},{9,11},{10,... | collective-permute-start | bytes 417800 | tf_op jit(solution)/shard_map/ppermute | solution.py:638
  18.7 3.3 %collective-permute-done.3.part2_ref = bf16[32,2176]{1,0:T(8,128)(2,1)S(1)} collective-permute-done((bf16[32,2176]{1,0:T(8,128)(2,1)S(1)}, bf16[32,2176]{1,0:T(8,128)(2,1)S(1)}, u32[]{:S(2)}, u32[]{:S(2)}) %collective-permute-start.3) | collective-permute-done | bytes 139296 | tf_op jit(solution)/shard_map/ppermute | solution.py:638
  22.7 4.8 %gram.1.gram_ref = f32[16,128,128]{2,1,0:T(8,128)S(1)} custom-call(bf16[2048,2048]{1,0:T(8,128)(2,1)} %weight_hbm.5), custom_call_target="tpu_custom_call" | custom-call | flops 1073741824 | bytes 8388608 | tf_op jit(solution)/shard_map/gram/pallas_call | solution.py:244
  27.5 1.5 %collective-permute-start.18 = (bf16[128,2048]{1,0:T(8,128)(2,1)S(1)}, bf16[128,2048]{1,0:T(8,128)(2,1)}, u32[]{:S(2)}, u32[]{:S(2)}) collective-permute-start(bf16[128,2048]{1,0:T(8,128)(2,1)S(1)} %collective-permute-done.12.rest_2_), channel_id=1, source_target_pairs={{8,16},{12,20},{16,8},{20,12},{9,17},{13,21},{17,9},{21,13},{10,18... | collective-permute-start | bytes 1572872 | tf_op jit(solution)/shard_map/ppermute | solution.py:568
  30.2 8.7 %all-to-all-start = ((bf16[8,80,256]{2,1,0:T(8,128)(2,1)}), bf16[8,80,256]{2,1,0:T(8,128)(2,1)S(1)}, u32[]{:S(2)}, u32[]{:S(2)}) async-start(bf16[8,80,256]{2,1,0:T(8,128)(2,1)} %get-tuple-element.22), calls=%async_computation | async-start | bytes 655360 | tf_op jit(solution)/shard_map/all_to_all | solution.py:641
  39.0 2.0 %collective-permute-start.11 = (bf16[128,2048]{1,0:T(8,128)(2,1)S(1)}, bf16[128,2048]{1,0:T(8,128)(2,1)S(1)}, u32[]{:S(2)}, u32[]{:S(2)}) collective-permute-start(bf16[128,2048]{1,0:T(8,128)(2,1)S(1)} %copy-done), channel_id=1, source_target_pairs={{0,4},{4,0},{8,12},{12,8},{16,20},{20,16},{24,28},{28,24},{1,5},{5... | collective-permute-start | bytes 1572872 | tf_op jit(solution)/shard_map/ppermute | solution.py:565
  43.6 14.2 %all-to-all-done.grad_ref = bf16[8,80,256]{2,1,0:T(8,128)(2,1)S(1)} async-done(((bf16[8,80,256]{2,1,0:T(8,128)(2,1)}), bf16[8,80,256]{2,1,0:T(8,128)(2,1)S(1)}, u32[]{:S(2)}, u32[]{:S(2)}) %all-to-all-start) | async-done | bytes 327712 | tf_op jit(solution)/shard_map/all_to_all | solution.py:641
  57.9 1.6 %collective-permute-start.13 = (bf16[128,2048]{1,0:T(8,128)(2,1)S(1)}, bf16[128,2048]{1,0:T(8,128)(2,1)S(1)}, u32[]{:S(2)}, u32[]{:S(2)}) collective-permute-start(bf16[128,2048]{1,0:T(8,128)(2,1)S(1)} %collective-permute-done.12.rest_2_), channel_id=1, source_target_pairs={{0,4},{4,0},{8,12},{12,8},{16,20},{20,16},{24,28},{28,24},{1,5},{5... | collective-permute-start | bytes 1572872 | tf_op jit(solution)/shard_map/ppermute | solution.py:569
  59.5 1.5 %collective-permute-start.6 = (f32[1,16]{1,0:T(1,128)S(1)}, f32[1,16]{1,0:T(1,128)S(1)}, u32[]{:S(2)}, u32[]{:S(2)}) collective-permute-start(f32[1,16]{1,0:T(1,128)S(1)} %bitcast_add_fusion.squares_ref), channel_id=1, source_target_pairs={{0,2},{1,3},{2,0},{3,1},{4,6},{5,7},{6,4},{7,5},{8,10},{9,11},{10,... | collective-permute-start | bytes 200 | tf_op jit(solution)/shard_map/ppermute | solution.py:648
  61.0 6.4 %products.1 = (bf16[16,128,2048]{2,1,0:T(8,128)(2,1)}, f32[16,2048]{1,0:T(8,128)S(1)}) custom-call(bf16[128,2048]{1,0:T(8,128)(2,1)S(1)} %copy-done, bf16[2048,2048]{1,0:T(8,128)(2,1)} %weight_hbm.5, bf16[128,2176]{1,0:T(8,128)(2,1)S(1)} %get-tuple-element.23.grad_ref.extra_ref), custom_call_target="tpu_custom_call" | custom-call | flops 1073741824 | bytes 16777216 | tf_op jit(solution)/shard_map/products/pallas_call | solution.py:343
  67.6 1.6 %collective-permute-start.7 = (f32[2,2048]{1,0:T(2,128)S(1)}, f32[2,2048]{1,0:T(2,128)S(1)}, u32[]{:S(2)}, u32[]{:S(2)}) collective-permute-start(f32[2,2048]{1,0:T(2,128)S(1)} %get-tuple-element.28), channel_id=1, source_target_pairs={{0,16},{4,20},{8,24},{12,28},{16,0},{20,4},{24,8},{28,12},{1,17},{... | collective-permute-start | bytes 49160 | tf_op jit(solution)/shard_map/ppermute | solution.py:603
  69.2 3.2 %collective-permute-done.7 = f32[2,2048]{1,0:T(2,128)S(1)} collective-permute-done((f32[2,2048]{1,0:T(2,128)S(1)}, f32[2,2048]{1,0:T(2,128)S(1)}, u32[]{:S(2)}, u32[]{:S(2)}) %collective-permute-start.7) | collective-permute-done | bytes 16416 | tf_op jit(solution)/shard_map/ppermute | solution.py:603
  72.9 1.5 %collective-permute-start.16 = (bf16[128,2048]{1,0:T(8,128)(2,1)S(1)}, bf16[128,2048]{1,0:T(8,128)(2,1)}, u32[]{:S(2)}, u32[]{:S(2)}) collective-permute-start(bf16[128,2048]{1,0:T(8,128)(2,1)S(1)} %collective-permute-done.14.rest_4_), channel_id=1, source_target_pairs={{8,12},{12,8},{16,20},{20,16},{9,13},{13,9},{17,21},{21,17},{10,14... | collective-permute-start | bytes 1572872 | tf_op jit(solution)/shard_map/ppermute | solution.py:572
  74.4 2.8 %collective-permute-start.17 = (bf16[128,2048]{1,0:T(8,128)(2,1)}, bf16[128,2048]{1,0:T(8,128)(2,1)}, u32[]{:S(2)}, u32[]{:S(2)}) collective-permute-start(bf16[128,2048]{1,0:T(8,128)(2,1)} %collective-permute-done.15.rest_5_), channel_id=1, source_target_pairs={{0,4},{4,0},{24,28},{28,24},{1,5},{5,1},{25,29},{29,25},{2,6},{6,2... | collective-permute-start | bytes 1572872 | tf_op jit(solution)/shard_map/ppermute | solution.py:573
  77.2 1.5 %collective-permute-start.20 = (bf16[128,2048]{1,0:T(8,128)(2,1)}, bf16[128,2048]{1,0:T(8,128)(2,1)}, u32[]{:S(2)}, u32[]{:S(2)}) collective-permute-start(bf16[128,2048]{1,0:T(8,128)(2,1)} %collective-permute-done.18.rest_8_), channel_id=1, source_target_pairs={{8,12},{12,8},{16,20},{20,16},{9,13},{13,9},{17,21},{21,17},{10,14... | collective-permute-start | bytes 1572872 | tf_op jit(solution)/shard_map/ppermute | solution.py:574
  78.7 3.0 %collective-permute-start.21 = (bf16[128,2048]{1,0:T(8,128)(2,1)}, bf16[128,2048]{1,0:T(8,128)(2,1)}, u32[]{:S(2)}, u32[]{:S(2)}) collective-permute-start(bf16[128,2048]{1,0:T(8,128)(2,1)} %collective-permute-done.19.rest_9_), channel_id=1, source_target_pairs={{0,4},{4,0},{24,28},{28,24},{1,5},{5,1},{25,29},{29,25},{2,6},{6,2... | collective-permute-start | bytes 1572872 | tf_op jit(solution)/shard_map/ppermute | solution.py:575
  83.4 16.9 %collective-permute-done.9.got_ref = f32[2,2048]{1,0:T(2,128)S(1)} collective-permute-done((f32[2,2048]{1,0:T(2,128)S(1)}, f32[2,2048]{1,0:T(2,128)S(1)}, u32[]{:S(2)}, u32[]{:S(2)}) %collective-permute-start.9) | collective-permute-done | bytes 16416 | tf_op jit(solution)/shard_map/ppermute | solution.py:603
  100.4 5.3 %backward.1 = bf16[128,2048]{1,0:T(8,128)(2,1)} custom-call(f32[1,16]{1,0:T(1,128)S(1)} %get-tuple-element.26.share_ref.row_ref, f32[1,16]{1,0:T(1,128)S(1)} %get-tuple-element.26.share_ref.row_ref, bf16[128,2048]{1,0:T(8,128)(2,1)S(1)} %copy-done, f32[1,2048]{1,0:T(1,128)S(1)} %bitcast.15, bf16[16,128,2048]{2,1,0:T(8,128)(2,1)} %get-tuple-element.27.prod_hbm, ...), custom_call_target="tpu_custom_call" | custom-call | flops 8388608 | bytes 8388608 | tf_op jit(solution)/shard_map/backward/pallas_call | solution.py:429
  106.4 4.6 %weights.1 = f32[2048,256]{1,0:T(8,128)} custom-call(s32[1]{0:T(128)} %bitcast.11.place_ref, s32[1]{0:T(128)} %bitcast.2.core_ref, f32[1,2048]{1,0:T(1,128)S(1)} %bitcast.16, f32[1,2048]{1,0:T(1,128)S(1)} %get-tuple-element.29.wide_ref, bf16[8,80,256]{2,1,0:T(8,128)(2,1)S(1)} %all-to-all-done.grad_ref, ...), custom_call_target="tpu_custom_call" | custom-call | flops 1073741824 | bytes 4194304 | tf_op jit(solution)/shard_map/weights/pallas_call | solution.py:517
  (54 shorter events, 8.3 us)
Async XLA Ops:
  6.3 3.2 %collective-permute-start = (f32[2,32,2176]{2,1,0:T(8,128)S(1)}, f32[2,32,2176]{2,1,0:T(8,128)S(1)}, u32[]{:S(2)}, u32[]{:S(2)}) collective-permute-start(f32[2,32,2176]{2,1,0:T(8,128)S(1)} %get-tuple-element.19), channel_id=1, source_target_pairs={{0,1},{1,0},{2,3},{3,2},{4,5},{5,4},{6,7},{7,6},{8,9},{9,8},{10,11... | collective-permute-start | bytes 1671176 | tf_op jit(solution)/shard_map/ppermute | solution.py:623
  6.9 20.6 %collective-permute-start.12 = (bf16[128,2048]{1,0:T(8,128)(2,1)S(1)}, bf16[128,2048]{1,0:T(8,128)(2,1)S(1)}, u32[]{:S(2)}, u32[]{:S(2)}) collective-permute-start(bf16[128,2048]{1,0:T(8,128)(2,1)S(1)} %copy-done), channel_id=1, source_target_pairs={{0,8},{4,12},{8,0},{12,4},{16,24},{20,28},{24,16},{28,20},{1,9},{5... | collective-permute-start | bytes 1572872 | tf_op jit(solution)/shard_map/ppermute | solution.py:566
  9.5 5.9 %collective-permute-start.1 = (bf16[32,2176]{1,0:T(8,128)(2,1)S(1)}, bf16[32,2176]{1,0:T(8,128)(2,1)S(1)}, u32[]{:S(2)}, u32[]{:S(2)}) collective-permute-start(bf16[32,2176]{1,0:T(8,128)(2,1)S(1)} %get-tuple-element.21), channel_id=1, source_target_pairs={{0,2},{1,3},{2,0},{3,1},{4,6},{5,7},{6,4},{7,5},{8,10},{9,11},{10,... | collective-permute-start | bytes 417800 | tf_op jit(solution)/shard_map/ppermute | solution.py:625
  16.9 83.5 %copy-start.3 = (f32[2048]{0:T(1024)S(1)}, f32[2048]{0:T(1024)}, u32[]{:S(2)}) copy-start(f32[2048]{0:T(1024)} %param.9) | copy-start | bytes 24580
  16.9 5.1 %collective-permute-start.3 = (bf16[32,2176]{1,0:T(8,128)(2,1)S(1)}, bf16[32,2176]{1,0:T(8,128)(2,1)S(1)}, u32[]{:S(2)}, u32[]{:S(2)}) collective-permute-start(bf16[32,2176]{1,0:T(8,128)(2,1)S(1)} %heads.1.part0_ref), channel_id=1, source_target_pairs={{0,2},{1,3},{2,0},{3,1},{4,6},{5,7},{6,4},{7,5},{8,10},{9,11},{10,... | collective-permute-start | bytes 417800 | tf_op jit(solution)/shard_map/ppermute | solution.py:638
  18.7 10.2 %collective-permute-start.2 = (bf16[32,2176]{1,0:T(8,128)(2,1)S(1)}, bf16[32,2176]{1,0:T(8,128)(2,1)S(1)}, u32[]{:S(2)}, u32[]{:S(2)}) collective-permute-start(bf16[32,2176]{1,0:T(8,128)(2,1)S(1)} %heads.1.part0_ref), channel_id=1, source_target_pairs={{0,1},{1,0},{2,3},{3,2},{4,5},{5,4},{6,7},{7,6},{8,9},{9,8},{10,11... | collective-permute-start | bytes 417800 | tf_op jit(solution)/shard_map/ppermute | solution.py:637
  22.0 6.9 %collective-permute-start.4 = (bf16[32,2176]{1,0:T(8,128)(2,1)S(1)}, bf16[32,2176]{1,0:T(8,128)(2,1)S(1)}, u32[]{:S(2)}, u32[]{:S(2)}) collective-permute-start(bf16[32,2176]{1,0:T(8,128)(2,1)S(1)} %collective-permute-done.3.part2_ref), channel_id=1, source_target_pairs={{0,1},{1,0},{2,3},{3,2},{4,5},{5,4},{6,7},{7,6},{8,9},{9,8},{10,11... | collective-permute-start | bytes 417800 | tf_op jit(solution)/shard_map/ppermute | solution.py:639
  22.0 19.0 %collective-permute-start.14 = (bf16[128,2048]{1,0:T(8,128)(2,1)S(1)}, bf16[128,2048]{1,0:T(8,128)(2,1)S(1)}, u32[]{:S(2)}, u32[]{:S(2)}) collective-permute-start(bf16[128,2048]{1,0:T(8,128)(2,1)S(1)} %copy-done), channel_id=1, source_target_pairs={{8,16},{12,20},{16,8},{20,12},{9,17},{13,21},{17,9},{21,13},{10,18... | collective-permute-start | bytes 1572872 | tf_op jit(solution)/shard_map/ppermute | solution.py:567
  27.5 14.8 %collective-permute-start.18 = (bf16[128,2048]{1,0:T(8,128)(2,1)S(1)}, bf16[128,2048]{1,0:T(8,128)(2,1)}, u32[]{:S(2)}, u32[]{:S(2)}) collective-permute-start(bf16[128,2048]{1,0:T(8,128)(2,1)S(1)} %collective-permute-done.12.rest_2_), channel_id=1, source_target_pairs={{8,16},{12,20},{16,8},{20,12},{9,17},{13,21},{17,9},{21,13},{10,18... | collective-permute-start | bytes 1572872 | tf_op jit(solution)/shard_map/ppermute | solution.py:568
  30.2 27.6 %all-to-all-start = ((bf16[8,80,256]{2,1,0:T(8,128)(2,1)}), bf16[8,80,256]{2,1,0:T(8,128)(2,1)S(1)}, u32[]{:S(2)}, u32[]{:S(2)}) async-start(bf16[8,80,256]{2,1,0:T(8,128)(2,1)} %get-tuple-element.22), calls=%async_computation | async-start | bytes 655360 | tf_op jit(solution)/shard_map/all_to_all | solution.py:641
  39.0 33.9 %collective-permute-start.11 = (bf16[128,2048]{1,0:T(8,128)(2,1)S(1)}, bf16[128,2048]{1,0:T(8,128)(2,1)S(1)}, u32[]{:S(2)}, u32[]{:S(2)}) collective-permute-start(bf16[128,2048]{1,0:T(8,128)(2,1)S(1)} %copy-done), channel_id=1, source_target_pairs={{0,4},{4,0},{8,12},{12,8},{16,20},{20,16},{24,28},{28,24},{1,5},{5... | collective-permute-start | bytes 1572872 | tf_op jit(solution)/shard_map/ppermute | solution.py:565
  41.0 33.4 %collective-permute-start.15 = (bf16[128,2048]{1,0:T(8,128)(2,1)S(1)}, bf16[128,2048]{1,0:T(8,128)(2,1)}, u32[]{:S(2)}, u32[]{:S(2)}) collective-permute-start(bf16[128,2048]{1,0:T(8,128)(2,1)S(1)} %collective-permute-done.14.rest_4_), channel_id=1, source_target_pairs={{8,0},{12,4},{16,24},{20,28},{9,1},{13,5},{17,25},{21,29},{10,2},{... | collective-permute-start | bytes 1572872 | tf_op jit(solution)/shard_map/ppermute | solution.py:570
  42.3 34.9 %collective-permute-start.19 = (bf16[128,2048]{1,0:T(8,128)(2,1)}, bf16[128,2048]{1,0:T(8,128)(2,1)}, u32[]{:S(2)}, u32[]{:S(2)}) collective-permute-start(bf16[128,2048]{1,0:T(8,128)(2,1)} %collective-permute-done.18.rest_8_), channel_id=1, source_target_pairs={{8,0},{12,4},{16,24},{20,28},{9,1},{13,5},{17,25},{21,29},{10,2},{... | collective-permute-start | bytes 1572872 | tf_op jit(solution)/shard_map/ppermute | solution.py:571
  57.9 1.6 %collective-permute-start.5 = (f32[1,16]{1,0:T(1,128)S(1)}, f32[1,16]{1,0:T(1,128)S(1)}, u32[]{:S(2)}, u32[]{:S(2)}) collective-permute-start(f32[1,16]{1,0:T(1,128)S(1)} %bitcast.22), channel_id=1, source_target_pairs={{0,1},{1,0},{2,3},{3,2},{4,5},{5,4},{6,7},{7,6},{8,9},{9,8},{10,11... | collective-permute-start | bytes 200 | tf_op jit(solution)/shard_map/ppermute | solution.py:646
  57.9 23.8 %collective-permute-start.13 = (bf16[128,2048]{1,0:T(8,128)(2,1)S(1)}, bf16[128,2048]{1,0:T(8,128)(2,1)S(1)}, u32[]{:S(2)}, u32[]{:S(2)}) collective-permute-start(bf16[128,2048]{1,0:T(8,128)(2,1)S(1)} %collective-permute-done.12.rest_2_), channel_id=1, source_target_pairs={{0,4},{4,0},{8,12},{12,8},{16,20},{20,16},{24,28},{28,24},{1,5},{5... | collective-permute-start | bytes 1572872 | tf_op jit(solution)/shard_map/ppermute | solution.py:569
  59.5 7.9 %collective-permute-start.6 = (f32[1,16]{1,0:T(1,128)S(1)}, f32[1,16]{1,0:T(1,128)S(1)}, u32[]{:S(2)}, u32[]{:S(2)}) collective-permute-start(f32[1,16]{1,0:T(1,128)S(1)} %bitcast_add_fusion.squares_ref), channel_id=1, source_target_pairs={{0,2},{1,3},{2,0},{3,1},{4,6},{5,7},{6,4},{7,5},{8,10},{9,11},{10,... | collective-permute-start | bytes 200 | tf_op jit(solution)/shard_map/ppermute | solution.py:648
  67.6 4.8 %collective-permute-start.7 = (f32[2,2048]{1,0:T(2,128)S(1)}, f32[2,2048]{1,0:T(2,128)S(1)}, u32[]{:S(2)}, u32[]{:S(2)}) collective-permute-start(f32[2,2048]{1,0:T(2,128)S(1)} %get-tuple-element.28), channel_id=1, source_target_pairs={{0,16},{4,20},{8,24},{12,28},{16,0},{20,4},{24,8},{28,12},{1,17},{... | collective-permute-start | bytes 49160 | tf_op jit(solution)/shard_map/ppermute | solution.py:603
  72.4 6.2 %collective-permute-start.8 = (f32[2,2048]{1,0:T(2,128)S(1)}, f32[2,2048]{1,0:T(2,128)S(1)}, u32[]{:S(2)}, u32[]{:S(2)}) collective-permute-start(f32[2,2048]{1,0:T(2,128)S(1)} %add.17), channel_id=1, source_target_pairs={{0,8},{4,12},{8,0},{12,4},{16,24},{20,28},{24,16},{28,20},{1,9},{5... | collective-permute-start | bytes 49160 | tf_op jit(solution)/shard_map/ppermute | solution.py:603
  72.9 33.4 %collective-permute-start.16 = (bf16[128,2048]{1,0:T(8,128)(2,1)S(1)}, bf16[128,2048]{1,0:T(8,128)(2,1)}, u32[]{:S(2)}, u32[]{:S(2)}) collective-permute-start(bf16[128,2048]{1,0:T(8,128)(2,1)S(1)} %collective-permute-done.14.rest_4_), channel_id=1, source_target_pairs={{8,12},{12,8},{16,20},{20,16},{9,13},{13,9},{17,21},{21,17},{10,14... | collective-permute-start | bytes 1572872 | tf_op jit(solution)/shard_map/ppermute | solution.py:572
  74.4 32.0 %collective-permute-start.17 = (bf16[128,2048]{1,0:T(8,128)(2,1)}, bf16[128,2048]{1,0:T(8,128)(2,1)}, u32[]{:S(2)}, u32[]{:S(2)}) collective-permute-start(bf16[128,2048]{1,0:T(8,128)(2,1)} %collective-permute-done.15.rest_5_), channel_id=1, source_target_pairs={{0,4},{4,0},{24,28},{28,24},{1,5},{5,1},{25,29},{29,25},{2,6},{6,2... | collective-permute-start | bytes 1572872 | tf_op jit(solution)/shard_map/ppermute | solution.py:573
  77.2 29.1 %collective-permute-start.20 = (bf16[128,2048]{1,0:T(8,128)(2,1)}, bf16[128,2048]{1,0:T(8,128)(2,1)}, u32[]{:S(2)}, u32[]{:S(2)}) collective-permute-start(bf16[128,2048]{1,0:T(8,128)(2,1)} %collective-permute-done.18.rest_8_), channel_id=1, source_target_pairs={{8,12},{12,8},{16,20},{20,16},{9,13},{13,9},{17,21},{21,17},{10,14... | collective-permute-start | bytes 1572872 | tf_op jit(solution)/shard_map/ppermute | solution.py:574
  78.7 27.7 %collective-permute-start.21 = (bf16[128,2048]{1,0:T(8,128)(2,1)}, bf16[128,2048]{1,0:T(8,128)(2,1)}, u32[]{:S(2)}, u32[]{:S(2)}) collective-permute-start(bf16[128,2048]{1,0:T(8,128)(2,1)} %collective-permute-done.19.rest_9_), channel_id=1, source_target_pairs={{0,4},{4,0},{24,28},{28,24},{1,5},{5,1},{25,29},{29,25},{2,6},{6,2... | collective-permute-start | bytes 1572872 | tf_op jit(solution)/shard_map/ppermute | solution.py:575
  82.5 17.9 %collective-permute-start.9 = (f32[2,2048]{1,0:T(2,128)S(1)}, f32[2,2048]{1,0:T(2,128)S(1)}, u32[]{:S(2)}, u32[]{:S(2)}) collective-permute-start(f32[2,2048]{1,0:T(2,128)S(1)} %add.18.sum_ref), channel_id=1, source_target_pairs={{0,4},{4,0},{8,12},{12,8},{16,20},{20,16},{24,28},{28,24},{1,5},{5... | collective-permute-start | bytes 49160 | tf_op jit(solution)/shard_map/ppermute | solution.py:603
  100.3 6.0 %collective-permute-start.10 = (bf16[8,80,256]{2,1,0:T(8,128)(2,1)S(1)}, bf16[8,80,256]{2,1,0:T(8,128)(2,1)S(1)}, u32[]{:S(2)}, u32[]{:S(2)}) collective-permute-start(bf16[8,80,256]{2,1,0:T(8,128)(2,1)S(1)} %all-to-all-done.grad_ref), channel_id=1, source_target_pairs={{0,1},{1,0},{2,3},{3,2},{4,5},{5,4},{6,7},{7,6},{8,9},{9,8},{10,11... | collective-permute-start | bytes 983048 | tf_op jit(solution)/shard_map/ppermute | solution.py:649
  (8 other events, 122.5 us)
